TPU v7x, 1024 devices: a whole 4x8x16 slice. The times are simulated.
1024 devices in a mesh: walk: 128 (over z, x, core), chol: 8 (over y).
Axes of the slice: x: 4, y: 8, z: 16, core: 2. Of those that a mesh axis runs over, the one named last changes fastest.
Arguments:
- walkers: bfloat16 [768, 2048, 128], P('walk', 'chol'), may hold values from -6 to 6
- inv_intersection: bfloat16 [768, 128, 128], P('walk'), may hold values from -0.5 to 0.5
- fields: bfloat16 [768, 16], P('walk', 'chol'), may hold values from -5 to 5
- cholesky: bfloat16 [16, 512, 2048], P('chol'), may hold values from -0.125 to 0.125
- trial_rows: bfloat16 [512, 128], replicated, may hold values from -0.234375 to 0.234375
- counts: int32 [128], replicated, may hold values from 1 to 6, as said below
- partner: int32 [128], replicated, may hold values from 0 to 127, as said below
Outputs:
- new_walkers: bfloat16 [512, 512, 128], P('walk', 'chol')
- log_weight: float32 [512], P('walk')
Inputs may be any that keep to these rules, and one draw needn't show every extreme that they name: `counts`: of w and partner[w], exactly one holds more than 4 walkers, and the other holds at most 8 minus that count; some walk index holds exactly 6 walkers. partner[partner[w]] = w, and partner[w] differs from w in exactly one bit.
All inputs are finite; a program needn't handle non-finite values.
Results may differ from a plain program's by a relative error of at most 0.0075.
Values may be sent and summed in bfloat16 or wider, within the bound.
No kernel may reach another device: no remote copies, remote signals or barrier semaphores. Data moves between devices by JAX's collectives and lax.ppermute only.
A program may use at most 32 MiB of HBM per device.

v0:
```python
import jax
import jax.numpy as jnp
from jax import lax
from jax.sharding import PartitionSpec as P

ROWS_DEV = 64
LIVE = 4
MOVE = 2


STEP_ROOT = 0.1


def from_partner(block, axis, distance):
    count = lax.axis_size(axis)
    route = []
    for low in range(count):
        high = low | 1 << distance
        if high != low and high < count:
            route += [(low, high), (high, low)]
    return lax.ppermute(block, axis, route)


def expand_mask(mask_in, target):
    return mask_in.reshape(mask_in.shape + (1,) * (target.ndim - mask_in.ndim))


def select_slots(own_part, arriving, own_mask, incoming):
    arrived = jnp.zeros_like(own_part)
    for slot_num in range(MOVE):
        flag = incoming[:, slot_num]
        arrived = jnp.where(expand_mask(flag, own_part), arriving[slot_num : slot_num + 1], arrived)
    return jnp.where(expand_mask(own_mask, own_part), own_part, arrived)


def propagate(walker_rows, minv, field_part, cholesky, trial_rows):
    products = jnp.einsum(
        "grk,wkn->wgrn",
        cholesky,
        lax.all_gather(walker_rows, "chol", axis=1, tiled=True),
        preferred_element_type=jnp.float32,
    )
    weighted = jnp.einsum("rb,wab->wra", trial_rows, minv, preferred_element_type=jnp.float32)
    force_bias = -STEP_ROOT * jnp.einsum("wgrn,wrn->wg", products, weighted)
    field_wide = field_part.astype(jnp.float32)
    shifted = STEP_ROOT * (field_wide - force_bias)
    row_terms = jnp.einsum("wg,wgrn->wrn", shifted, products)
    weight_terms = jnp.sum(field_wide * force_bias - 0.5 * force_bias * force_bias, axis=1)
    increment = lax.psum_scatter(row_terms, "chol", scatter_dimension=1, tiled=True)
    log_terms = lax.psum(weight_terms, "chol")
    window = walker_rows[:, :ROWS_DEV, :].astype(jnp.float32)
    return (window + increment, log_terms)


def shards(walkers, inv_intersection, fields, cholesky, trial_rows, counts, partner):
    walk_index = lax.axis_index("walk")
    own_count = counts[walk_index]
    mate_id = partner[walk_index]
    arriving_count = jnp.maximum(counts[mate_id] - LIVE, 0)
    bit_count = lax.axis_size("walk").bit_length() - 1
    slot_ids = jnp.arange(LIVE, dtype=jnp.int32)
    move_ids = jnp.arange(MOVE, dtype=jnp.int32)
    own_mask = slot_ids < jnp.minimum(own_count, LIVE)
    incoming = (slot_ids[:, None] - own_count == move_ids[None, :]) & (
        move_ids[None, :] < arriving_count
    )
    live_wide = (own_mask | jnp.any(incoming, axis=1)).astype(jnp.float32)
    outgoing = (walkers[LIVE:], inv_intersection[LIVE:], fields[LIVE:])
    received = tuple((jnp.zeros_like(member) for member in outgoing))
    for bit_num in range(bit_count):
        fetched = from_partner((outgoing[0], outgoing[1], outgoing[2]), "walk", bit_num)
        active = jnp.bitwise_xor(mate_id, walk_index) == 1 << bit_num
        received = tuple(
            (jnp.where(active, new_part, old_part) for new_part, old_part in zip(fetched, received))
        )
    phi = select_slots(walkers[:LIVE], received[0], own_mask, incoming)
    minv = select_slots(inv_intersection[:LIVE], received[1], own_mask, incoming)
    field_part = select_slots(fields[:LIVE], received[2], own_mask, incoming)
    new_rows, log_terms = propagate(phi, minv, field_part, cholesky, trial_rows)
    new_walkers = (live_wide[:, None, None] * new_rows).astype(jnp.bfloat16)
    return (new_walkers, live_wide * log_terms)


def solution(mesh):
    in_specs = (
        P("walk", "chol", None),
        P("walk", None, None),
        P("walk", "chol"),
        P("chol", None, None),
        P(),
        P(),
        P(),
    )
    out_specs = (P("walk", "chol", None), P("walk"))
    return jax.shard_map(shards, mesh=mesh, in_specs=in_specs, out_specs=out_specs, check_vma=False)
```

profile of v0, /device:TPU:2, one launch (start us, length us, event | category | flops | bytes accessed | tf_op | source)
XLA Modules:
  0.0 245.5 jit_solution(5758774938898666809)
XLA Ops:
  7.2 1.0 slice.51
  8.2 19.4 %collective-permute-start = (bf16[2,256,128]{2,1,0:T(8,128)(2,1)S(1)}, bf16[2,256,128]{2,1,0:T(8,128)(2,1)S(1)}, u32[]{:S(2)}, u32[]{:S(2)}) collective-permute-start(bf16[2,256,128]{2,1,0:T(8,128)(2,1)S(1)} %slice.51), channel_id=1, source_target_pairs={{0,512},{512,0},{8,520},{520,8},{16,528},{528,16},{24,536},{536,24... | collective-permute-start | bytes 393224 | tf_op jit(solution)/shard_map/ppermute | solution.py:21
  27.6 6.1 %collective-permute-start.1 = (bf16[2,256,128]{2,1,0:T(8,128)(2,1)S(1)}, bf16[2,256,128]{2,1,0:T(8,128)(2,1)S(1)}, u32[]{:S(2)}, u32[]{:S(2)}) collective-permute-start(bf16[2,256,128]{2,1,0:T(8,128)(2,1)S(1)} %slice.51), channel_id=1, source_target_pairs={{0,256},{256,0},{8,264},{264,8},{16,272},{272,16},{24,280},{280,24... | collective-permute-start | bytes 393224 | tf_op jit(solution)/shard_map/ppermute | solution.py:21
  33.7 4.3 %collective-permute-start.2 = (bf16[2,256,128]{2,1,0:T(8,128)(2,1)S(1)}, bf16[2,256,128]{2,1,0:T(8,128)(2,1)S(1)}, u32[]{:S(2)}, u32[]{:S(2)}) collective-permute-start(bf16[2,256,128]{2,1,0:T(8,128)(2,1)S(1)} %slice.51), channel_id=1, source_target_pairs={{0,128},{128,0},{8,136},{136,8},{16,144},{144,16},{24,152},{152,24... | collective-permute-start | bytes 393224 | tf_op jit(solution)/shard_map/ppermute | solution.py:21
  38.0 3.4 %collective-permute-start.3 = (bf16[2,256,128]{2,1,0:T(8,128)(2,1)S(1)}, bf16[2,256,128]{2,1,0:T(8,128)(2,1)S(1)}, u32[]{:S(2)}, u32[]{:S(2)}) collective-permute-start(bf16[2,256,128]{2,1,0:T(8,128)(2,1)S(1)} %slice.51), channel_id=1, source_target_pairs={{0,64},{64,0},{8,72},{72,8},{16,80},{80,16},{24,88},{88,24},{32,96... | collective-permute-start | bytes 393224 | tf_op jit(solution)/shard_map/ppermute | solution.py:21
  41.4 4.0 %collective-permute-start.4 = (bf16[2,256,128]{2,1,0:T(8,128)(2,1)S(1)}, bf16[2,256,128]{2,1,0:T(8,128)(2,1)S(1)}, u32[]{:S(2)}, u32[]{:S(2)}) collective-permute-start(bf16[2,256,128]{2,1,0:T(8,128)(2,1)S(1)} %slice.51), channel_id=1, source_target_pairs={{0,32},{32,0},{8,40},{40,8},{16,48},{48,16},{24,56},{56,24},{64,96... | collective-permute-start | bytes 393224 | tf_op jit(solution)/shard_map/ppermute | solution.py:21
  45.5 1.2 dynamic_slice.10
  48.6 1.3 fusion.28
  50.0 0.6 iota_subtract_fusion
  51.3 3.3 %collective-permute-start.5 = (bf16[2,256,128]{2,1,0:T(8,128)(2,1)S(1)}, bf16[2,256,128]{2,1,0:T(8,128)(2,1)S(1)}, u32[]{:S(2)}, u32[]{:S(2)}) collective-permute-start(bf16[2,256,128]{2,1,0:T(8,128)(2,1)S(1)} %slice.51), channel_id=1, source_target_pairs={{0,16},{16,0},{8,24},{24,8},{32,48},{48,32},{40,56},{56,40},{64,80... | collective-permute-start | bytes 393224 | tf_op jit(solution)/shard_map/ppermute | solution.py:21
  54.6 1.9 collective-permute-start.6
  57.2 1.0 slice.49
  58.9 0.1 copy.27
  59.4 0.8 select_select_fusion
  60.3 3.2 %collective-permute-start.14 = (bf16[2,128,128]{2,1,0:T(8,128)(2,1)S(1)}, bf16[2,128,128]{2,1,0:T(8,128)(2,1)S(1)}, u32[]{:S(2)}, u32[]{:S(2)}) collective-permute-start(bf16[2,128,128]{2,1,0:T(8,128)(2,1)S(1)} %slice.61), channel_id=1, source_target_pairs={{0,512},{512,0},{8,520},{520,8},{16,528},{528,16},{24,536},{536,24... | collective-permute-start | bytes 196616 | tf_op jit(solution)/shard_map/ppermute | solution.py:21
  63.6 3.9 %collective-permute-start.15 = (bf16[2,128,128]{2,1,0:T(8,128)(2,1)S(1)}, bf16[2,128,128]{2,1,0:T(8,128)(2,1)S(1)}, u32[]{:S(2)}, u32[]{:S(2)}) collective-permute-start(bf16[2,128,128]{2,1,0:T(8,128)(2,1)S(1)} %slice.61), channel_id=1, source_target_pairs={{0,256},{256,0},{8,264},{264,8},{16,272},{272,16},{24,280},{280,24... | collective-permute-start | bytes 196616 | tf_op jit(solution)/shard_map/ppermute | solution.py:21
  67.4 3.3 %collective-permute-start.16 = (bf16[2,128,128]{2,1,0:T(8,128)(2,1)S(1)}, bf16[2,128,128]{2,1,0:T(8,128)(2,1)S(1)}, u32[]{:S(2)}, u32[]{:S(2)}) collective-permute-start(bf16[2,128,128]{2,1,0:T(8,128)(2,1)S(1)} %slice.61), channel_id=1, source_target_pairs={{0,128},{128,0},{8,136},{136,8},{16,144},{144,16},{24,152},{152,24... | collective-permute-start | bytes 196616 | tf_op jit(solution)/shard_map/ppermute | solution.py:21
  70.7 3.0 %collective-permute-start.17 = (bf16[2,128,128]{2,1,0:T(8,128)(2,1)S(1)}, bf16[2,128,128]{2,1,0:T(8,128)(2,1)S(1)}, u32[]{:S(2)}, u32[]{:S(2)}) collective-permute-start(bf16[2,128,128]{2,1,0:T(8,128)(2,1)S(1)} %slice.61), channel_id=1, source_target_pairs={{0,64},{64,0},{8,72},{72,8},{16,80},{80,16},{24,88},{88,24},{32,96... | collective-permute-start | bytes 196616 | tf_op jit(solution)/shard_map/ppermute | solution.py:21
  73.8 2.8 %collective-permute-start.10 = (bf16[2,2]{0,1:T(2,128)(2,1)S(1)}, bf16[2,2]{0,1:T(2,128)(2,1)S(1)}, u32[]{:S(2)}, u32[]{:S(2)}) collective-permute-start(bf16[2,2]{0,1:T(2,128)(2,1)S(1)} %slice.57), channel_id=1, source_target_pairs={{0,64},{64,0},{8,72},{72,8},{16,80},{80,16},{24,88},{88,24},{32,96... | collective-permute-start | bytes 32 | tf_op jit(solution)/shard_map/ppermute | solution.py:21
  76.6 2.6 %collective-permute-done.10 = bf16[2,2]{0,1:T(2,128)(2,1)S(1)} collective-permute-done((bf16[2,2]{0,1:T(2,128)(2,1)S(1)}, bf16[2,2]{0,1:T(2,128)(2,1)S(1)}, u32[]{:S(2)}, u32[]{:S(2)}) %collective-permute-start.10) | collective-permute-done | bytes 40 | tf_op jit(solution)/shard_map/ppermute | solution.py:21
  79.2 4.8 %collective-permute-start.11 = (bf16[2,2]{0,1:T(2,128)(2,1)S(1)}, bf16[2,2]{0,1:T(2,128)(2,1)S(1)}, u32[]{:S(2)}, u32[]{:S(2)}) collective-permute-start(bf16[2,2]{0,1:T(2,128)(2,1)S(1)} %slice.57), channel_id=1, source_target_pairs={{0,32},{32,0},{8,40},{40,8},{16,48},{48,16},{24,56},{56,24},{64,96... | collective-permute-start | bytes 32 | tf_op jit(solution)/shard_map/ppermute | solution.py:21
  84.1 2.1 collective-permute-done.11
  86.2 2.7 %collective-permute-start.12 = (bf16[2,2]{0,1:T(2,128)(2,1)S(1)}, bf16[2,2]{0,1:T(2,128)(2,1)S(1)}, u32[]{:S(2)}, u32[]{:S(2)}) collective-permute-start(bf16[2,2]{0,1:T(2,128)(2,1)S(1)} %slice.57), channel_id=1, source_target_pairs={{0,16},{16,0},{8,24},{24,8},{32,48},{48,32},{40,56},{56,40},{64,80... | collective-permute-start | bytes 32 | tf_op jit(solution)/shard_map/ppermute | solution.py:21
  89.0 2.7 %collective-permute-done.12 = bf16[2,2]{0,1:T(2,128)(2,1)S(1)} collective-permute-done((bf16[2,2]{0,1:T(2,128)(2,1)S(1)}, bf16[2,2]{0,1:T(2,128)(2,1)S(1)}, u32[]{:S(2)}, u32[]{:S(2)}) %collective-permute-start.12) | collective-permute-done | bytes 40 | tf_op jit(solution)/shard_map/ppermute | solution.py:21
  91.7 1.9 collective-permute-start.13
  93.6 1.1 collective-permute-done.13
  94.7 11.3 %collective-permute-start.7 = (bf16[2,2]{0,1:T(2,128)(2,1)S(1)}, bf16[2,2]{0,1:T(2,128)(2,1)S(1)}, u32[]{:S(2)}, u32[]{:S(2)}) collective-permute-start(bf16[2,2]{0,1:T(2,128)(2,1)S(1)} %slice.57), channel_id=1, source_target_pairs={{0,512},{512,0},{8,520},{520,8},{16,528},{528,16},{24,536},{536,24... | collective-permute-start | bytes 32 | tf_op jit(solution)/shard_map/ppermute | solution.py:21
  106.0 2.9 %collective-permute-done.7 = bf16[2,2]{0,1:T(2,128)(2,1)S(1)} collective-permute-done((bf16[2,2]{0,1:T(2,128)(2,1)S(1)}, bf16[2,2]{0,1:T(2,128)(2,1)S(1)}, u32[]{:S(2)}, u32[]{:S(2)}) %collective-permute-start.7) | collective-permute-done | bytes 40 | tf_op jit(solution)/shard_map/ppermute | solution.py:21
  108.9 3.7 %collective-permute-start.8 = (bf16[2,2]{0,1:T(2,128)(2,1)S(1)}, bf16[2,2]{0,1:T(2,128)(2,1)S(1)}, u32[]{:S(2)}, u32[]{:S(2)}) collective-permute-start(bf16[2,2]{0,1:T(2,128)(2,1)S(1)} %slice.57), channel_id=1, source_target_pairs={{0,256},{256,0},{8,264},{264,8},{16,272},{272,16},{24,280},{280,24... | collective-permute-start | bytes 32 | tf_op jit(solution)/shard_map/ppermute | solution.py:21
  112.6 5.6 %collective-permute-done.8 = bf16[2,2]{0,1:T(2,128)(2,1)S(1)} collective-permute-done((bf16[2,2]{0,1:T(2,128)(2,1)S(1)}, bf16[2,2]{0,1:T(2,128)(2,1)S(1)}, u32[]{:S(2)}, u32[]{:S(2)}) %collective-permute-start.8) | collective-permute-done | bytes 40 | tf_op jit(solution)/shard_map/ppermute | solution.py:21
  118.2 4.3 %collective-permute-start.9 = (bf16[2,2]{0,1:T(2,128)(2,1)S(1)}, bf16[2,2]{0,1:T(2,128)(2,1)S(1)}, u32[]{:S(2)}, u32[]{:S(2)}) collective-permute-start(bf16[2,2]{0,1:T(2,128)(2,1)S(1)} %slice.57), channel_id=1, source_target_pairs={{0,128},{128,0},{8,136},{136,8},{16,144},{144,16},{24,152},{152,24... | collective-permute-start | bytes 32 | tf_op jit(solution)/shard_map/ppermute | solution.py:21
  122.5 2.0 collective-permute-done.9
  124.6 4.8 %collective-permute-start.18 = (bf16[2,128,128]{2,1,0:T(8,128)(2,1)S(1)}, bf16[2,128,128]{2,1,0:T(8,128)(2,1)S(1)}, u32[]{:S(2)}, u32[]{:S(2)}) collective-permute-start(bf16[2,128,128]{2,1,0:T(8,128)(2,1)S(1)} %slice.61), channel_id=1, source_target_pairs={{0,32},{32,0},{8,40},{40,8},{16,48},{48,16},{24,56},{56,24},{64,96... | collective-permute-start | bytes 196616 | tf_op jit(solution)/shard_map/ppermute | solution.py:21
  129.4 3.0 %collective-permute-start.19 = (bf16[2,128,128]{2,1,0:T(8,128)(2,1)S(1)}, bf16[2,128,128]{2,1,0:T(8,128)(2,1)S(1)}, u32[]{:S(2)}, u32[]{:S(2)}) collective-permute-start(bf16[2,128,128]{2,1,0:T(8,128)(2,1)S(1)} %slice.61), channel_id=1, source_target_pairs={{0,16},{16,0},{8,24},{24,8},{32,48},{48,32},{40,56},{56,40},{64,80... | collective-permute-start | bytes 196616 | tf_op jit(solution)/shard_map/ppermute | solution.py:21
  132.4 1.9 collective-permute-start.20
  134.4 0.2 slice_reduce_fusion
  134.6 1.0 collective-permute-done.19
  135.6 0.3 convolution_bitcast_fusion
  136.0 5.2 %fusion.5 = f32[4,2,512,128]{2,3,1,0:T(8,128)S(1)} fusion(bf16[2,512,2048]{2,1,0:T(8,128)(2,1)} %param.10, bf16[4,2048,128]{1,2,0:T(8,128)(2,1)} %all-gather.2.cloned.1.call-done), kind=kOutput, calls=%fused_computation.6 | convolution fusion | flops 2147483648 | bytes 8388608 | tf_op jit(solution)/shard_map/grk,wkn->wgrn/dot_general | solution.py:37
  141.2 3.1 %fusion.3 = f32[4,1,2,1]{2,1,3,0:T(1,128)S(1)} fusion(f32[4,2,512,128]{2,3,1,0:T(8,128)S(1)} %fusion.5, bf16[4,512,128,1]{1,2,0,3:T(8,128)(2,1)S(1)} %convolution_bitcast_fusion), kind=kOutput, calls=%fused_computation.4 | convolution fusion | flops 1048576 | bytes 2621472 | tf_op jit(solution)/shard_map/wgrn,wrn->wg/dot_general | solution.py:44
  144.6 0.4 multiply_reduce_fusion
  144.9 1.3 copy.26
  146.3 1.3 dynamic-slice
  148.3 16.4 %psum.7 = f32[4]{0:T(128)S(1)} all-reduce(f32[4]{0:T(128)S(1)} %get-tuple-element.8), channel_id=1, replica_groups=mesh['walk'=128,'chol'=8] {'chol'}, use_global_device_ids=true, to_apply=%region_3.4 | all-reduce | flops 4 | bytes 32 | tf_op jit(solution)/shard_map/psum | solution.py:50
  164.7 0.5 broadcast_select_fusion.10
  165.2 71.6 %all-reduce.3.cloned.1.call-done = f32[4,512,128]{2,0,1:T(4,128)} async-done(((f32[4,512,128]{2,0,1:T(4,128)}), f32[4,512,128]{2,0,1:T(4,128)}) %all-reduce.3.cloned.1.call-update) | async-done | bytes 1048592
  236.8 0.9 constant_dynamic-slice_fusion
  238.0 0.7 copy.17
  (46 shorter events, 1.2 us)
Async XLA Ops:
  7.2 128.5 %copy-start = (bf16[512,128]{1,0:T(8,128)(2,1)S(1)}, bf16[512,128]{1,0:T(8,128)(2,1)}, u32[]{:S(2)}) copy-start(bf16[512,128]{1,0:T(8,128)(2,1)} %param.11) | copy-start | bytes 393220
  7.2 53.1 %copy-start.2 = (bf16[6,128,128]{2,1,0:T(8,128)(2,1)S(1)}, bf16[6,128,128]{2,1,0:T(8,128)(2,1)}, u32[]{:S(2)}) copy-start(bf16[6,128,128]{2,1,0:T(8,128)(2,1)} %param.8) | copy-start | bytes 589828
  7.2 66.5 %copy-start.3 = (bf16[6,2]{0,1:T(2,128)(2,1)S(1)}, bf16[6,2]{0,1:T(2,128)(2,1)}, u32[]{:S(2)}) copy-start(bf16[6,2]{0,1:T(2,128)(2,1)} %param.9) | copy-start | bytes 76
  7.2 128.8 %all-gather.2.cloned.1.call-start = ((), (), s32[]{:S(2)}) async-start(), calls=%async_computation | async-start | bytes 2359296 | tf_op jit(solution)/shard_map/all_gather | solution.py:40
  8.2 43.0 %collective-permute-start = (bf16[2,256,128]{2,1,0:T(8,128)(2,1)S(1)}, bf16[2,256,128]{2,1,0:T(8,128)(2,1)S(1)}, u32[]{:S(2)}, u32[]{:S(2)}) collective-permute-start(bf16[2,256,128]{2,1,0:T(8,128)(2,1)S(1)} %slice.51), channel_id=1, source_target_pairs={{0,512},{512,0},{8,520},{520,8},{16,528},{528,16},{24,536},{536,24... | collective-permute-start | bytes 393224 | tf_op jit(solution)/shard_map/ppermute | solution.py:21
  27.6 27.0 %collective-permute-start.1 = (bf16[2,256,128]{2,1,0:T(8,128)(2,1)S(1)}, bf16[2,256,128]{2,1,0:T(8,128)(2,1)S(1)}, u32[]{:S(2)}, u32[]{:S(2)}) collective-permute-start(bf16[2,256,128]{2,1,0:T(8,128)(2,1)S(1)} %slice.51), channel_id=1, source_target_pairs={{0,256},{256,0},{8,264},{264,8},{16,272},{272,16},{24,280},{280,24... | collective-permute-start | bytes 393224 | tf_op jit(solution)/shard_map/ppermute | solution.py:21
  33.7 25.3 %collective-permute-start.2 = (bf16[2,256,128]{2,1,0:T(8,128)(2,1)S(1)}, bf16[2,256,128]{2,1,0:T(8,128)(2,1)S(1)}, u32[]{:S(2)}, u32[]{:S(2)}) collective-permute-start(bf16[2,256,128]{2,1,0:T(8,128)(2,1)S(1)} %slice.51), channel_id=1, source_target_pairs={{0,128},{128,0},{8,136},{136,8},{16,144},{144,16},{24,152},{152,24... | collective-permute-start | bytes 393224 | tf_op jit(solution)/shard_map/ppermute | solution.py:21
  38.0 21.0 %collective-permute-start.3 = (bf16[2,256,128]{2,1,0:T(8,128)(2,1)S(1)}, bf16[2,256,128]{2,1,0:T(8,128)(2,1)S(1)}, u32[]{:S(2)}, u32[]{:S(2)}) collective-permute-start(bf16[2,256,128]{2,1,0:T(8,128)(2,1)S(1)} %slice.51), channel_id=1, source_target_pairs={{0,64},{64,0},{8,72},{72,8},{16,80},{80,16},{24,88},{88,24},{32,96... | collective-permute-start | bytes 393224 | tf_op jit(solution)/shard_map/ppermute | solution.py:21
  41.4 17.6 %collective-permute-start.4 = (bf16[2,256,128]{2,1,0:T(8,128)(2,1)S(1)}, bf16[2,256,128]{2,1,0:T(8,128)(2,1)S(1)}, u32[]{:S(2)}, u32[]{:S(2)}) collective-permute-start(bf16[2,256,128]{2,1,0:T(8,128)(2,1)S(1)} %slice.51), channel_id=1, source_target_pairs={{0,32},{32,0},{8,40},{40,8},{16,48},{48,16},{24,56},{56,24},{64,96... | collective-permute-start | bytes 393224 | tf_op jit(solution)/shard_map/ppermute | solution.py:21
  51.3 7.8 %collective-permute-start.5 = (bf16[2,256,128]{2,1,0:T(8,128)(2,1)S(1)}, bf16[2,256,128]{2,1,0:T(8,128)(2,1)S(1)}, u32[]{:S(2)}, u32[]{:S(2)}) collective-permute-start(bf16[2,256,128]{2,1,0:T(8,128)(2,1)S(1)} %slice.51), channel_id=1, source_target_pairs={{0,16},{16,0},{8,24},{24,8},{32,48},{48,32},{40,56},{56,40},{64,80... | collective-permute-start | bytes 393224 | tf_op jit(solution)/shard_map/ppermute | solution.py:21
  54.6 4.4 %collective-permute-start.6 = (bf16[2,256,128]{2,1,0:T(8,128)(2,1)S(1)}, bf16[2,256,128]{2,1,0:T(8,128)(2,1)S(1)}, u32[]{:S(2)}, u32[]{:S(2)}) collective-permute-start(bf16[2,256,128]{2,1,0:T(8,128)(2,1)S(1)} %slice.51), channel_id=1, source_target_pairs={{0,8},{8,0},{16,24},{24,16},{32,40},{40,32},{48,56},{56,48},{64,72... | collective-permute-start | bytes 393224 | tf_op jit(solution)/shard_map/ppermute | solution.py:21
  60.2 176.6 %all-reduce.3.cloned.1.call-start = ((), (), s32[]{:S(2)}) async-start(), calls=%async_computation.1 | async-start | bytes 2097152
  60.3 69.1 %collective-permute-start.14 = (bf16[2,128,128]{2,1,0:T(8,128)(2,1)S(1)}, bf16[2,128,128]{2,1,0:T(8,128)(2,1)S(1)}, u32[]{:S(2)}, u32[]{:S(2)}) collective-permute-start(bf16[2,128,128]{2,1,0:T(8,128)(2,1)S(1)} %slice.61), channel_id=1, source_target_pairs={{0,512},{512,0},{8,520},{520,8},{16,528},{528,16},{24,536},{536,24... | collective-permute-start | bytes 196616 | tf_op jit(solution)/shard_map/ppermute | solution.py:21
  63.6 68.9 %collective-permute-start.15 = (bf16[2,128,128]{2,1,0:T(8,128)(2,1)S(1)}, bf16[2,128,128]{2,1,0:T(8,128)(2,1)S(1)}, u32[]{:S(2)}, u32[]{:S(2)}) collective-permute-start(bf16[2,128,128]{2,1,0:T(8,128)(2,1)S(1)} %slice.61), channel_id=1, source_target_pairs={{0,256},{256,0},{8,264},{264,8},{16,272},{272,16},{24,280},{280,24... | collective-permute-start | bytes 196616 | tf_op jit(solution)/shard_map/ppermute | solution.py:21
  67.4 67.1 %collective-permute-start.16 = (bf16[2,128,128]{2,1,0:T(8,128)(2,1)S(1)}, bf16[2,128,128]{2,1,0:T(8,128)(2,1)S(1)}, u32[]{:S(2)}, u32[]{:S(2)}) collective-permute-start(bf16[2,128,128]{2,1,0:T(8,128)(2,1)S(1)} %slice.61), channel_id=1, source_target_pairs={{0,128},{128,0},{8,136},{136,8},{16,144},{144,16},{24,152},{152,24... | collective-permute-start | bytes 196616 | tf_op jit(solution)/shard_map/ppermute | solution.py:21
  70.7 63.9 %collective-permute-start.17 = (bf16[2,128,128]{2,1,0:T(8,128)(2,1)S(1)}, bf16[2,128,128]{2,1,0:T(8,128)(2,1)S(1)}, u32[]{:S(2)}, u32[]{:S(2)}) collective-permute-start(bf16[2,128,128]{2,1,0:T(8,128)(2,1)S(1)} %slice.61), channel_id=1, source_target_pairs={{0,64},{64,0},{8,72},{72,8},{16,80},{80,16},{24,88},{88,24},{32,96... | collective-permute-start | bytes 196616 | tf_op jit(solution)/shard_map/ppermute | solution.py:21
  73.8 5.5 %collective-permute-start.10 = (bf16[2,2]{0,1:T(2,128)(2,1)S(1)}, bf16[2,2]{0,1:T(2,128)(2,1)S(1)}, u32[]{:S(2)}, u32[]{:S(2)}) collective-permute-start(bf16[2,2]{0,1:T(2,128)(2,1)S(1)} %slice.57), channel_id=1, source_target_pairs={{0,64},{64,0},{8,72},{72,8},{16,80},{80,16},{24,88},{88,24},{32,96... | collective-permute-start | bytes 32 | tf_op jit(solution)/shard_map/ppermute | solution.py:21
  79.2 7.0 %collective-permute-start.11 = (bf16[2,2]{0,1:T(2,128)(2,1)S(1)}, bf16[2,2]{0,1:T(2,128)(2,1)S(1)}, u32[]{:S(2)}, u32[]{:S(2)}) collective-permute-start(bf16[2,2]{0,1:T(2,128)(2,1)S(1)} %slice.57), channel_id=1, source_target_pairs={{0,32},{32,0},{8,40},{40,8},{16,48},{48,16},{24,56},{56,24},{64,96... | collective-permute-start | bytes 32 | tf_op jit(solution)/shard_map/ppermute | solution.py:21
  86.2 5.5 %collective-permute-start.12 = (bf16[2,2]{0,1:T(2,128)(2,1)S(1)}, bf16[2,2]{0,1:T(2,128)(2,1)S(1)}, u32[]{:S(2)}, u32[]{:S(2)}) collective-permute-start(bf16[2,2]{0,1:T(2,128)(2,1)S(1)} %slice.57), channel_id=1, source_target_pairs={{0,16},{16,0},{8,24},{24,8},{32,48},{48,32},{40,56},{56,40},{64,80... | collective-permute-start | bytes 32 | tf_op jit(solution)/shard_map/ppermute | solution.py:21
  91.7 3.0 %collective-permute-start.13 = (bf16[2,2]{0,1:T(2,128)(2,1)S(1)}, bf16[2,2]{0,1:T(2,128)(2,1)S(1)}, u32[]{:S(2)}, u32[]{:S(2)}) collective-permute-start(bf16[2,2]{0,1:T(2,128)(2,1)S(1)} %slice.57), channel_id=1, source_target_pairs={{0,8},{8,0},{16,24},{24,16},{32,40},{40,32},{48,56},{56,48},{64,72... | collective-permute-start | bytes 32 | tf_op jit(solution)/shard_map/ppermute | solution.py:21
  94.7 14.2 %collective-permute-start.7 = (bf16[2,2]{0,1:T(2,128)(2,1)S(1)}, bf16[2,2]{0,1:T(2,128)(2,1)S(1)}, u32[]{:S(2)}, u32[]{:S(2)}) collective-permute-start(bf16[2,2]{0,1:T(2,128)(2,1)S(1)} %slice.57), channel_id=1, source_target_pairs={{0,512},{512,0},{8,520},{520,8},{16,528},{528,16},{24,536},{536,24... | collective-permute-start | bytes 32 | tf_op jit(solution)/shard_map/ppermute | solution.py:21
  108.9 9.4 %collective-permute-start.8 = (bf16[2,2]{0,1:T(2,128)(2,1)S(1)}, bf16[2,2]{0,1:T(2,128)(2,1)S(1)}, u32[]{:S(2)}, u32[]{:S(2)}) collective-permute-start(bf16[2,2]{0,1:T(2,128)(2,1)S(1)} %slice.57), channel_id=1, source_target_pairs={{0,256},{256,0},{8,264},{264,8},{16,272},{272,16},{24,280},{280,24... | collective-permute-start | bytes 32 | tf_op jit(solution)/shard_map/ppermute | solution.py:21
  118.2 6.3 %collective-permute-start.9 = (bf16[2,2]{0,1:T(2,128)(2,1)S(1)}, bf16[2,2]{0,1:T(2,128)(2,1)S(1)}, u32[]{:S(2)}, u32[]{:S(2)}) collective-permute-start(bf16[2,2]{0,1:T(2,128)(2,1)S(1)} %slice.57), channel_id=1, source_target_pairs={{0,128},{128,0},{8,136},{136,8},{16,144},{144,16},{24,152},{152,24... | collective-permute-start | bytes 32 | tf_op jit(solution)/shard_map/ppermute | solution.py:21
  124.6 10.0 %collective-permute-start.18 = (bf16[2,128,128]{2,1,0:T(8,128)(2,1)S(1)}, bf16[2,128,128]{2,1,0:T(8,128)(2,1)S(1)}, u32[]{:S(2)}, u32[]{:S(2)}) collective-permute-start(bf16[2,128,128]{2,1,0:T(8,128)(2,1)S(1)} %slice.61), channel_id=1, source_target_pairs={{0,32},{32,0},{8,40},{40,8},{16,48},{48,16},{24,56},{56,24},{64,96... | collective-permute-start | bytes 196616 | tf_op jit(solution)/shard_map/ppermute | solution.py:21
  129.4 6.2 %collective-permute-start.19 = (bf16[2,128,128]{2,1,0:T(8,128)(2,1)S(1)}, bf16[2,128,128]{2,1,0:T(8,128)(2,1)S(1)}, u32[]{:S(2)}, u32[]{:S(2)}) collective-permute-start(bf16[2,128,128]{2,1,0:T(8,128)(2,1)S(1)} %slice.61), channel_id=1, source_target_pairs={{0,16},{16,0},{8,24},{24,8},{32,48},{48,32},{40,56},{56,40},{64,80... | collective-permute-start | bytes 196616 | tf_op jit(solution)/shard_map/ppermute | solution.py:21
  132.4 3.2 %collective-permute-start.20 = (bf16[2,128,128]{2,1,0:T(8,128)(2,1)S(1)}, bf16[2,128,128]{2,1,0:T(8,128)(2,1)S(1)}, u32[]{:S(2)}, u32[]{:S(2)}) collective-permute-start(bf16[2,128,128]{2,1,0:T(8,128)(2,1)S(1)} %slice.61), channel_id=1, source_target_pairs={{0,8},{8,0},{16,24},{24,16},{32,40},{40,32},{48,56},{56,48},{64,72... | collective-permute-start | bytes 196616 | tf_op jit(solution)/shard_map/ppermute | solution.py:21
  144.9 92.9 %copy-start.1 = (bf16[4,256,128]{1,2,0:T(8,128)(2,1)S(1)}, bf16[4,256,128]{1,2,0:T(8,128)(2,1)}, u32[]{:S(2)}) copy-start(bf16[4,256,128]{1,2,0:T(8,128)(2,1)} %select_select_fusion) | copy-start | bytes 786436
Sparse Core Ops, SparseCore 0:
  60.4 49.0 all-gather.1
  146.4 90.3 all-reduce.2
where the time goes:
time: 246 us
  starting transfers between devices  97.2 us (40%)
  waiting for transfers between devices  91.8 us (37%)
  between operations  19 us (8%)
  blocking collectives  16.4 us (7%)
  local copies, waits for them, and re-layouts  9.78 us (4%)
  matrix products  8.57 us (3%)
  other arithmetic  2.77 us (1%)
    ppermute x21, starting transfers between devices, from_partner(): return lax.ppermute(block, axis, route)  97.1 us
    unnamed x3, waiting for transfers between devices  71.6 us
    ppermute x21, waiting for transfers between devices, from_partner(): return lax.ppermute(block, axis, route)  20.2 us
    psum x1, blocking collectives, propagate(): log_terms = lax.psum(weight_terms, 'chol')  16.4 us
    dot_general x1, matrix products, propagate(): jnp.einsum('grk,wkn->wgrn', cholesky, lax.all_gather(walker_rows, 'chol',...  5.18 us
  transfers between devices with their start and end apart: 23, of which 9 were waited for; matrix products, arithmetic and copies ran while one was open for 3% of the time, Pallas kernels for 0%

commit v1 on v0

v1 whole, which is shorter than its diff:
```python
import jax
import jax.numpy as jnp
from jax import lax
from jax.experimental import pallas as pl
from jax.experimental.pallas import tpu as pltpu
from jax.sharding import PartitionSpec as P

ROWS_DEV = 64
LIVE = 4
MOVE = 2
STEP_ROOT = 0.1
N_CHOL = 8
OFFSETS = (0, -1, 1, -2, 2, -3, 3, -4)
TILE = 16


def ring(block):
    up = [(i, (i + 1) % N_CHOL) for i in range(N_CHOL)]
    down = [(i, (i - 1) % N_CHOL) for i in range(N_CHOL)]
    parts, low, high = [block], block, block
    for step in range(N_CHOL // 2):
        low = lax.ppermute(low, "chol", up)
        parts.append(low)
        if step < N_CHOL // 2 - 1:
            high = lax.ppermute(high, "chol", down)
            parts.append(high)
    return parts


def pair_kernel(late, blocks, x, *refs):
    parts, rest = refs[:N_CHOL], refs[N_CHOL:]
    if late:
        chol, trial, before, out, buf, acc, minv, sems = rest
    else:
        chol, trial, minv_in, out, buf, acc, sems = rest
    step = pl.program_id(0)
    stride = buf.shape[1] // 2
    rows = stride - TILE if late else stride

    def copy(d):
        return pltpu.make_async_copy(parts[d], buf.at[d], sems.at[d])

    @pl.when(step == 0)
    def _():
        for d in range(N_CHOL):
            copy(d).start()
        acc[...] = jnp.zeros_like(acc)

    pltpu.make_async_copy(parts[0], buf.at[step], sems.at[step]).wait()
    phi = jnp.concatenate([buf[step, :rows], buf[step, stride : stride + rows]], axis=1)
    for g in range(2):
        acc[g] += jnp.dot(chol[g], phi, preferred_element_type=jnp.float32)

    @pl.when(step == N_CHOL - 1)
    def _():
        base = LIVE // 2 if late else 0
        lanes = out.shape[2]
        row_id = lax.broadcasted_iota(jnp.int32, (TILE, lanes), 0)
        lane_id = lax.broadcasted_iota(jnp.int32, (TILE, lanes), 1)
        logs = jnp.zeros((TILE, lanes), jnp.float32)
        if late:
            logs = before[0, 2 * ROWS_DEV :].astype(jnp.float32)
            for d in range(N_CHOL):
                spot = pl.ds(pl.multiple_of(blocks[d] * TILE, TILE), TILE)
                for q in range(2):
                    minv[q, spot] = buf[d, q * stride + rows : (q + 1) * stride]
        for q in range(2):
            inv = minv[q] if late else minv_in[q]
            weighted = lax.dot_general(
                trial[...], inv, (((1,), (1,)), ((), ())), preferred_element_type=jnp.float32
            )
            total = jnp.zeros_like(weighted)
            log = jnp.zeros((1, 1), jnp.float32)
            for g in range(2):
                product = acc[g, :, q * lanes : (q + 1) * lanes]
                bias = -STEP_ROOT * jnp.sum(product * weighted, keepdims=True)
                field = x[base + q, g]
                total += STEP_ROOT * (field - bias) * product
                log += field * bias - 0.5 * bias * bias
            spread = total.astype(jnp.bfloat16).reshape(N_CHOL, ROWS_DEV, lanes)
            first = (base + q) * ROWS_DEV
            out[:, first : first + ROWS_DEV] = spread
            high = log.astype(jnp.bfloat16).astype(jnp.float32)
            here = row_id == base + q
            logs = jnp.where(here & (lane_id == 0), high, logs)
            logs = jnp.where(here & (lane_id == 1), log - high, logs)
        if late:
            out[:, : 2 * ROWS_DEV] = before[:, : 2 * ROWS_DEV]
        end = (base + 2) * ROWS_DEV
        for k in range(N_CHOL):
            out[k, end : end + TILE] = logs.astype(jnp.bfloat16)


def pair_call(late, blocks, x, parts, cholesky, trial, extra):
    rows, lanes = parts[0].shape
    vectors, window, orbitals = cholesky.shape
    depth = orbitals // N_CHOL
    out_rows = (LIVE if late else LIVE // 2) * ROWS_DEV + TILE
    whole = pl.BlockSpec(memory_space=pltpu.VMEM)
    scratch = [
        pltpu.VMEM((N_CHOL, rows, lanes), jnp.bfloat16),
        pltpu.VMEM((vectors, window, 2 * lanes), jnp.float32),
    ]
    if late:
        scratch.append(pltpu.VMEM((2, lanes, lanes), jnp.bfloat16))
    scratch.append(pltpu.SemaphoreType.DMA((N_CHOL,)))

    def body(*refs):
        pair_kernel(late, *refs)

    grid_spec = pltpu.PrefetchScalarGridSpec(
        num_scalar_prefetch=2,
        grid=(N_CHOL,),
        in_specs=[pl.BlockSpec(memory_space=pl.ANY)] * N_CHOL
        + [pl.BlockSpec((vectors, window, depth), lambda d, blocks, x: (0, 0, blocks[d]))]
        + [whole, whole],
        out_specs=whole,
        scratch_shapes=scratch,
    )
    flops = 4 * vectors * window * orbitals * lanes
    return pl.pallas_call(
        body,
        grid_spec=grid_spec,
        out_shape=jax.ShapeDtypeStruct((N_CHOL, out_rows, lanes), jnp.bfloat16),
        name="late_pair" if late else "early_pair",
        cost_estimate=pl.CostEstimate(flops=flops, bytes_accessed=6 << 20, transcendentals=0),
    )(blocks, x, *parts, cholesky, trial, extra)


def finish_kernel(order, got, window, out, log_out):
    for s in range(LIVE):
        spot = order[s]
        live = order[LIVE + s] > 0
        rows = pl.ds(pl.multiple_of(spot * ROWS_DEV, ROWS_DEV), ROWS_DEV)
        total = window[rows].astype(jnp.float32)
        for k in range(N_CHOL):
            total += got[k, rows].astype(jnp.float32)
        out[s] = jnp.where(live, total, 0.0).astype(jnp.bfloat16)
        tile = jnp.zeros((TILE, got.shape[2]), jnp.float32)
        for k in range(N_CHOL):
            tile += got[k, LIVE * ROWS_DEV :].astype(jnp.float32)
        row_id = lax.broadcasted_iota(jnp.int32, tile.shape, 0)
        log = jnp.sum(jnp.where(row_id == spot, tile, 0.0))
        log_out[s] = jnp.where(live, log, 0.0)


def finish_call(order, got, window):
    lanes = got.shape[2]
    whole = pl.BlockSpec(memory_space=pltpu.VMEM)
    scalars = pl.BlockSpec(memory_space=pltpu.SMEM)
    return pl.pallas_call(
        finish_kernel,
        in_specs=[scalars, whole, whole],
        out_specs=(whole, scalars),
        out_shape=(
            jax.ShapeDtypeStruct((LIVE, ROWS_DEV, lanes), jnp.bfloat16),
            jax.ShapeDtypeStruct((LIVE,), jnp.float32),
        ),
        name="finish",
    )(order, got, window)


def shards(walkers, inv_intersection, fields, cholesky, trial_rows, counts, partner):
    walk_index = lax.axis_index("walk")
    chol_index = lax.axis_index("chol")
    own_count = counts[walk_index]
    mate_id = partner[walk_index]
    arriving_count = jnp.maximum(counts[mate_id] - LIVE, 0)
    distance = jnp.bitwise_xor(mate_id, walk_index)
    walk_size = lax.axis_size("walk")
    rows = walkers.shape[1]
    lanes = walkers.shape[2]

    inv_rows = lax.dynamic_slice_in_dim(inv_intersection, chol_index * TILE, TILE, 1)
    packed = jnp.concatenate([walkers[2:], inv_rows[2:]], axis=1)
    field_rows = jnp.pad(fields[LIVE:], ((0, TILE - MOVE), (0, lanes - fields.shape[1])))
    stride = rows + TILE
    outgoing = jnp.concatenate([packed[2:].reshape(MOVE * stride, lanes), field_rows], axis=0)

    received = jnp.zeros_like(outgoing)
    for bit in reversed(range(walk_size.bit_length() - 1)):
        route = [(i, i ^ 1 << bit) for i in range(walk_size)]
        fetched = lax.ppermute(outgoing, "walk", route)
        received = jnp.where(distance == 1 << bit, fetched, received)

    early = walkers[:2].reshape(2 * rows, lanes)
    early_parts = ring(early)

    keep = own_count > jnp.array([2, 3], jnp.int32)
    moved = received[: MOVE * stride].reshape(MOVE, stride, lanes)[::-1]
    late = jnp.where(keep[:, None, None], packed[:2], moved)
    moved_fields = received[MOVE * stride : MOVE * stride + MOVE, : fields.shape[1]][::-1]
    late_fields = jnp.where(keep[:, None], fields[2:LIVE], moved_fields)
    x = jnp.concatenate([fields[:2], late_fields], axis=0).astype(jnp.float32)
    late_parts = ring(late.reshape(2 * stride, lanes))

    blocks = (chol_index + jnp.array(OFFSETS, jnp.int32)) & (N_CHOL - 1)
    first = pair_call(False, blocks, x, early_parts, cholesky, trial_rows, inv_intersection[:2])
    sums = pair_call(True, blocks, x, late_parts, cholesky, trial_rows, first)
    sums = lax.all_to_all(sums, "chol", 0, 0, tiled=True)

    slots = jnp.arange(LIVE, dtype=jnp.int32)
    own = slots < own_count
    moved_slot = slots - own_count
    live = own | (moved_slot < arriving_count)
    spot = jnp.where(own, slots, jnp.clip(LIVE - 1 - moved_slot, 0, LIVE - 1))
    order = jnp.concatenate([spot, live.astype(jnp.int32)])
    window = jnp.concatenate([walkers[:2, :ROWS_DEV], late[:, :ROWS_DEV]], axis=0)
    return tuple(finish_call(order, sums, window.reshape(LIVE * ROWS_DEV, lanes)))


def solution(mesh):
    in_specs = (
        P("walk", "chol", None),
        P("walk", None, None),
        P("walk", "chol"),
        P("chol", None, None),
        P(),
        P(),
        P(),
    )
    out_specs = (P("walk", "chol", None), P("walk"))
    return jax.shard_map(shards, mesh=mesh, in_specs=in_specs, out_specs=out_specs, check_vma=False)
```

time: 246 us -> 162 us (0.66)
  the two profiles are of different devices: /device:TPU:2 before, /device:TPU:128 now
where the time goes in v1:
time: 162 us; the launch traced here: 160 us
  starting transfers between devices  92.4 us (57%)
  waiting for transfers between devices  25.3 us (16%)
  Pallas kernels  19.7 us (12%)
  local copies, waits for them, and re-layouts  12.8 us (8%)
  other arithmetic  5.91 us (4%)
  between operations  4.43 us (3%)
    ppermute x7, starting transfers between devices, shards(): fetched = lax.ppermute(outgoing, 'walk', route)  39.5 us
    ppermute x6, starting transfers between devices, ring(): high = lax.ppermute(high, 'chol', down)  24.5 us
    ppermute x8, starting transfers between devices, ring(): low = lax.ppermute(low, 'chol', up)  21 us
    pallas_call x2, Pallas kernels, pair_call(): pl.pallas_call(body, grid_spec=grid_spec, out_shape=jax.ShapeDtypeStruct(...  17.9 us
    ppermute x7, waiting for transfers between devices, shards(): fetched = lax.ppermute(outgoing, 'walk', route)  14.8 us
    all_to_all x1, waiting for transfers between devices, shards(): sums = lax.all_to_all(sums, 'chol', 0, 0, tiled=True)  9.47 us
    all_to_all x1, starting transfers between devices, shards(): sums = lax.all_to_all(sums, 'chol', 0, 0, tiled=True)  7.42 us
    unnamed x37, local copies, waits for them, and re-layouts  3.63 us
  transfers between devices with their start and end apart: 22, of which 3 were waited for; matrix products, arithmetic and copies ran while one was open for 8% of the time, Pallas kernels for 5%

profile of v1, /device:TPU:128, one launch (start us, length us, event | category | flops | bytes accessed | tf_op | source)
XLA Modules:
  0.0 160.4 jit_solution(13848268073213530416)
XLA Ops:
  0.6 1.0 slice.41
  1.6 0.8 fusion.4
  2.6 0.7 constant_dynamic-slice_fusion
  3.3 1.9 %collective-permute-start = (bf16[560,128]{1,0:T(8,128)(2,1)S(1)}, bf16[560,128]{1,0:T(8,128)(2,1)S(1)}, u32[]{:S(2)}, u32[]{:S(2)}) collective-permute-start(bf16[560,128]{1,0:T(8,128)(2,1)S(1)} %fusion.1), channel_id=1, source_target_pairs={{0,8},{8,0},{16,24},{24,16},{32,40},{40,32},{48,56},{56,48},{64,72... | collective-permute-start | bytes 430088 | tf_op jit(solution)/shard_map/ppermute | solution.py:183
  5.2 3.4 %collective-permute-start.1 = (bf16[560,128]{1,0:T(8,128)(2,1)S(1)}, bf16[560,128]{1,0:T(8,128)(2,1)S(1)}, u32[]{:S(2)}, u32[]{:S(2)}) collective-permute-start(bf16[560,128]{1,0:T(8,128)(2,1)S(1)} %fusion.1), channel_id=1, source_target_pairs={{0,16},{8,24},{16,0},{24,8},{32,48},{40,56},{48,32},{56,40},{64,80... | collective-permute-start | bytes 430088 | tf_op jit(solution)/shard_map/ppermute | solution.py:183
  8.7 4.6 %collective-permute-start.2 = (bf16[560,128]{1,0:T(8,128)(2,1)S(1)}, bf16[560,128]{1,0:T(8,128)(2,1)S(1)}, u32[]{:S(2)}, u32[]{:S(2)}) collective-permute-start(bf16[560,128]{1,0:T(8,128)(2,1)S(1)} %fusion.1), channel_id=1, source_target_pairs={{0,32},{8,40},{16,48},{24,56},{32,0},{40,8},{48,16},{56,24},{64,96... | collective-permute-start | bytes 430088 | tf_op jit(solution)/shard_map/ppermute | solution.py:183
  13.3 4.3 %collective-permute-start.3 = (bf16[560,128]{1,0:T(8,128)(2,1)S(1)}, bf16[560,128]{1,0:T(8,128)(2,1)S(1)}, u32[]{:S(2)}, u32[]{:S(2)}) collective-permute-start(bf16[560,128]{1,0:T(8,128)(2,1)S(1)} %fusion.1), channel_id=1, source_target_pairs={{0,64},{8,72},{16,80},{24,88},{32,96},{40,104},{48,112},{56,120},{... | collective-permute-start | bytes 430088 | tf_op jit(solution)/shard_map/ppermute | solution.py:183
  17.6 6.7 %collective-permute-start.4 = (bf16[560,128]{1,0:T(8,128)(2,1)S(1)}, bf16[560,128]{1,0:T(8,128)(2,1)S(1)}, u32[]{:S(2)}, u32[]{:S(2)}) collective-permute-start(bf16[560,128]{1,0:T(8,128)(2,1)S(1)} %fusion.1), channel_id=1, source_target_pairs={{0,128},{8,136},{16,144},{24,152},{32,160},{40,168},{48,176},{56,1... | collective-permute-start | bytes 430088 | tf_op jit(solution)/shard_map/ppermute | solution.py:183
  24.3 1.2 dynamic_slice.13
  27.5 0.9 slice.48
  29.1 1.4 fusion.5
  30.5 6.1 %collective-permute-start.5 = (bf16[560,128]{1,0:T(8,128)(2,1)S(1)}, bf16[560,128]{1,0:T(8,128)(2,1)S(1)}, u32[]{:S(2)}, u32[]{:S(2)}) collective-permute-start(bf16[560,128]{1,0:T(8,128)(2,1)S(1)} %fusion.1), channel_id=1, source_target_pairs={{0,256},{8,264},{16,272},{24,280},{32,288},{40,296},{48,304},{56,3... | collective-permute-start | bytes 430088 | tf_op jit(solution)/shard_map/ppermute | solution.py:183
  36.7 12.4 %collective-permute-start.6 = (bf16[560,128]{1,0:T(8,128)(2,1)S(1)}, bf16[560,128]{1,0:T(8,128)(2,1)S(1)}, u32[]{:S(2)}, u32[]{:S(2)}) collective-permute-start(bf16[560,128]{1,0:T(8,128)(2,1)S(1)} %fusion.1), channel_id=1, source_target_pairs={{0,512},{8,520},{16,528},{24,536},{32,544},{40,552},{48,560},{56,5... | collective-permute-start | bytes 430088 | tf_op jit(solution)/shard_map/ppermute | solution.py:183
  49.1 1.3 broadcast_compare_fusion
  50.4 3.5 %collective-permute-start.14 = (bf16[512,128]{1,0:T(8,128)(2,1)S(1)}, bf16[512,128]{1,0:T(8,128)(2,1)S(1)}, u32[]{:S(2)}, u32[]{:S(2)}) collective-permute-start(bf16[512,128]{1,0:T(8,128)(2,1)S(1)} %bitcast.13), channel_id=1, source_target_pairs={{0,1},{1,2},{2,3},{3,4},{4,5},{5,6},{6,7},{7,0},{8,9},{9,10},{10,1... | collective-permute-start | bytes 393224 | tf_op jit(solution)/shard_map/ppermute | solution.py:22
  53.9 14.8 %collective-permute-done.6 = bf16[560,128]{1,0:T(8,128)(2,1)S(1)} collective-permute-done((bf16[560,128]{1,0:T(8,128)(2,1)S(1)}, bf16[560,128]{1,0:T(8,128)(2,1)S(1)}, u32[]{:S(2)}, u32[]{:S(2)}) %collective-permute-start.6) | collective-permute-done | bytes 143392 | tf_op jit(solution)/shard_map/ppermute | solution.py:183
  68.9 3.5 %collective-permute-start.7 = (bf16[544,128]{1,0:T(8,128)(2,1)S(1)}, bf16[544,128]{1,0:T(8,128)(2,1)S(1)}, u32[]{:S(2)}, u32[]{:S(2)}) collective-permute-start(bf16[544,128]{1,0:T(8,128)(2,1)S(1)} %bitcast.8), channel_id=1, source_target_pairs={{0,1},{1,2},{2,3},{3,4},{4,5},{5,6},{6,7},{7,0},{8,9},{9,10},{10,1... | collective-permute-start | bytes 417800 | tf_op jit(solution)/shard_map/ppermute | solution.py:22
  72.4 3.8 %collective-permute-start.15 = (bf16[512,128]{1,0:T(8,128)(2,1)S(1)}, bf16[512,128]{1,0:T(8,128)(2,1)S(1)}, u32[]{:S(2)}, u32[]{:S(2)}) collective-permute-start(bf16[512,128]{1,0:T(8,128)(2,1)S(1)} %bitcast.14), channel_id=1, source_target_pairs={{0,7},{1,0},{2,1},{3,2},{4,3},{5,4},{6,5},{7,6},{8,15},{9,8},{10,9... | collective-permute-start | bytes 393224 | tf_op jit(solution)/shard_map/ppermute | solution.py:25
  76.2 2.0 %collective-permute-start.16 = (bf16[512,128]{1,0:T(8,128)(2,1)S(1)}, bf16[512,128]{1,0:T(8,128)(2,1)S(1)}, u32[]{:S(2)}, u32[]{:S(2)}) collective-permute-start(bf16[512,128]{1,0:T(8,128)(2,1)S(1)} %collective-permute-done.14.refs_3_), channel_id=1, source_target_pairs={{0,1},{1,2},{2,3},{3,4},{4,5},{5,6},{6,7},{7,0},{8,9},{9,10},{10,1... | collective-permute-start | bytes 393224 | tf_op jit(solution)/shard_map/ppermute | solution.py:22
  78.3 1.5 slice.49.refs_12_
  80.0 5.0 %collective-permute-start.17 = (bf16[512,128]{1,0:T(8,128)(2,1)S(1)}, bf16[512,128]{1,0:T(8,128)(2,1)S(1)}, u32[]{:S(2)}, u32[]{:S(2)}) collective-permute-start(bf16[512,128]{1,0:T(8,128)(2,1)S(1)} %collective-permute-done.15.refs_4_), channel_id=1, source_target_pairs={{0,7},{1,0},{2,1},{3,2},{4,3},{5,4},{6,5},{7,6},{8,15},{9,8},{10,9... | collective-permute-start | bytes 393224 | tf_op jit(solution)/shard_map/ppermute | solution.py:25
  85.0 2.7 %collective-permute-start.8 = (bf16[544,128]{1,0:T(8,128)(2,1)S(1)}, bf16[544,128]{1,0:T(8,128)(2,1)S(1)}, u32[]{:S(2)}, u32[]{:S(2)}) collective-permute-start(bf16[544,128]{1,0:T(8,128)(2,1)S(1)} %bitcast.9), channel_id=1, source_target_pairs={{0,7},{1,0},{2,1},{3,2},{4,3},{5,4},{6,5},{7,6},{8,15},{9,8},{10,9... | collective-permute-start | bytes 417800 | tf_op jit(solution)/shard_map/ppermute | solution.py:25
  87.7 3.1 %collective-permute-start.18 = (bf16[512,128]{1,0:T(8,128)(2,1)S(1)}, bf16[512,128]{1,0:T(8,128)(2,1)S(1)}, u32[]{:S(2)}, u32[]{:S(2)}) collective-permute-start(bf16[512,128]{1,0:T(8,128)(2,1)S(1)} %collective-permute-done.16.refs_5_), channel_id=1, source_target_pairs={{0,1},{1,2},{2,3},{3,4},{4,5},{5,6},{6,7},{7,0},{8,9},{9,10},{10,1... | collective-permute-start | bytes 393224 | tf_op jit(solution)/shard_map/ppermute | solution.py:22
  90.9 1.9 %collective-permute-start.9 = (bf16[544,128]{1,0:T(8,128)(2,1)S(1)}, bf16[544,128]{1,0:T(8,128)(2,1)S(1)}, u32[]{:S(2)}, u32[]{:S(2)}) collective-permute-start(bf16[544,128]{1,0:T(8,128)(2,1)S(1)} %collective-permute-done.7.refs_3_), channel_id=1, source_target_pairs={{0,1},{1,2},{2,3},{3,4},{4,5},{5,6},{6,7},{7,0},{8,9},{9,10},{10,1... | collective-permute-start | bytes 417800 | tf_op jit(solution)/shard_map/ppermute | solution.py:22
  92.8 1.1 add_and_fusion.refs_0_
  94.0 5.1 %collective-permute-start.19 = (bf16[512,128]{1,0:T(8,128)(2,1)S(1)}, bf16[512,128]{1,0:T(8,128)(2,1)S(1)}, u32[]{:S(2)}, u32[]{:S(2)}) collective-permute-start(bf16[512,128]{1,0:T(8,128)(2,1)S(1)} %collective-permute-done.17.refs_6_), channel_id=1, source_target_pairs={{0,7},{1,0},{2,1},{3,2},{4,3},{5,4},{6,5},{7,6},{8,15},{9,8},{10,9... | collective-permute-start | bytes 393224 | tf_op jit(solution)/shard_map/ppermute | solution.py:25
  99.2 2.7 %collective-permute-start.10 = (bf16[544,128]{1,0:T(8,128)(2,1)S(1)}, bf16[544,128]{1,0:T(8,128)(2,1)S(1)}, u32[]{:S(2)}, u32[]{:S(2)}) collective-permute-start(bf16[544,128]{1,0:T(8,128)(2,1)S(1)} %collective-permute-done.8.refs_4_), channel_id=1, source_target_pairs={{0,7},{1,0},{2,1},{3,2},{4,3},{5,4},{6,5},{7,6},{8,15},{9,8},{10,9... | collective-permute-start | bytes 417800 | tf_op jit(solution)/shard_map/ppermute | solution.py:25
  101.9 3.1 %collective-permute-start.20 = (bf16[512,128]{1,0:T(8,128)(2,1)S(1)}, bf16[512,128]{1,0:T(8,128)(2,1)S(1)}, u32[]{:S(2)}, u32[]{:S(2)}) collective-permute-start(bf16[512,128]{1,0:T(8,128)(2,1)S(1)} %collective-permute-done.18.refs_7_), channel_id=1, source_target_pairs={{0,1},{1,2},{2,3},{3,4},{4,5},{5,6},{6,7},{7,0},{8,9},{9,10},{10,1... | collective-permute-start | bytes 393224 | tf_op jit(solution)/shard_map/ppermute | solution.py:22
  105.0 1.9 %collective-permute-start.11 = (bf16[544,128]{1,0:T(8,128)(2,1)S(1)}, bf16[544,128]{1,0:T(8,128)(2,1)S(1)}, u32[]{:S(2)}, u32[]{:S(2)}) collective-permute-start(bf16[544,128]{1,0:T(8,128)(2,1)S(1)} %collective-permute-done.9.refs_5_), channel_id=1, source_target_pairs={{0,1},{1,2},{2,3},{3,4},{4,5},{5,6},{6,7},{7,0},{8,9},{9,10},{10,1... | collective-permute-start | bytes 417800 | tf_op jit(solution)/shard_map/ppermute | solution.py:22
  107.1 5.1 %collective-permute-start.12 = (bf16[544,128]{1,0:T(8,128)(2,1)S(1)}, bf16[544,128]{1,0:T(8,128)(2,1)S(1)}, u32[]{:S(2)}, u32[]{:S(2)}) collective-permute-start(bf16[544,128]{1,0:T(8,128)(2,1)S(1)} %collective-permute-done.10.refs_6_), channel_id=1, source_target_pairs={{0,7},{1,0},{2,1},{3,2},{4,3},{5,4},{6,5},{7,6},{8,15},{9,8},{10,9... | collective-permute-start | bytes 417800 | tf_op jit(solution)/shard_map/ppermute | solution.py:25
  112.2 1.0 collective-permute-done.11.refs_7_
  113.2 1.9 %collective-permute-start.13 = (bf16[544,128]{1,0:T(8,128)(2,1)S(1)}, bf16[544,128]{1,0:T(8,128)(2,1)S(1)}, u32[]{:S(2)}, u32[]{:S(2)}) collective-permute-start(bf16[544,128]{1,0:T(8,128)(2,1)S(1)} %collective-permute-done.11.refs_7_), channel_id=1, source_target_pairs={{0,1},{1,2},{2,3},{3,4},{4,5},{5,6},{6,7},{7,0},{8,9},{9,10},{10,1... | collective-permute-start | bytes 417800 | tf_op jit(solution)/shard_map/ppermute | solution.py:22
  115.8 0.6 copy-done.15
  116.4 0.6 copy-done.16
  117.0 8.8 %early_pair.1.refs_12_ = bf16[8,144,128]{2,1,0:T(8,128)(2,1)} custom-call(s32[8]{0:T(128)} %add_and_fusion.refs_0_, f32[4,2]{1,0:T(4,128)} %maximum_convert_fusion.refs_1_, bf16[512,128]{1,0:T(8,128)(2,1)} %bitcast.15, bf16[512,128]{1,0:T(8,128)(2,1)} %copy-done.10, bf16[512,128]{1,0:T(8,128)(2,1)} %copy-done.11, bf16[512,128]{1,0:T(8,128)(2,1)} %copy-done.12, ...), custom_call_target="tpu_custom_call" | custom-call | flops 1073741824 | bytes 6291456 | tf_op jit(solution)/shard_map/early_pair/pallas_call | solution.py:121
  125.9 0.6 copy-done.8
  126.5 0.6 copy-done.9
  127.2 9.0 %late_pair.1 = bf16[8,272,128]{2,1,0:T(8,128)(2,1)} custom-call(s32[8]{0:T(128)} %add_and_fusion.refs_0_, f32[4,2]{1,0:T(4,128)} %maximum_convert_fusion.refs_1_, bf16[544,128]{1,0:T(8,128)(2,1)} %bitcast.10, bf16[544,128]{1,0:T(8,128)(2,1)} %copy-done.3, bf16[544,128]{1,0:T(8,128)(2,1)} %copy-done.4, bf16[544,128]{1,0:T(8,128)(2,1)} %copy-done.5, ...), custom_call_target="tpu_custom_call" | custom-call | flops 1073741824 | bytes 6291456 | tf_op jit(solution)/shard_map/late_pair/pallas_call | solution.py:121
  136.2 7.4 %all-to-all-start = ((bf16[8,272,128]{2,1,0:T(8,128)(2,1)}), bf16[8,272,128]{2,1,0:T(8,128)(2,1)S(1)}, u32[]{:S(2)}, u32[]{:S(2)}) async-start(bf16[8,272,128]{2,1,0:T(8,128)(2,1)} %late_pair.1), calls=%async_computation | async-start | bytes 1114112 | tf_op jit(solution)/shard_map/all_to_all | solution.py:200
  143.6 0.8 slice.50
  145.0 0.7 compare_select_fusion
  145.7 0.7 or_convert_fusion
  146.3 0.6 pad_add_fusion.order
  147.0 0.8 slice.56
  147.7 0.6 pad_maximum_fusion.1
  148.4 9.5 %all-to-all-done.got = bf16[8,272,128]{2,1,0:T(8,128)(2,1)S(1)} async-done(((bf16[8,272,128]{2,1,0:T(8,128)(2,1)}), bf16[8,272,128]{2,1,0:T(8,128)(2,1)S(1)}, u32[]{:S(2)}, u32[]{:S(2)}) %all-to-all-start) | async-done | bytes 557088 | tf_op jit(solution)/shard_map/all_to_all | solution.py:200
  157.9 0.8 copy-done
  158.6 1.8 %finish.1 = (bf16[4,64,128]{2,1,0:T(8,128)(2,1)}, f32[4]{0:T(128)}) custom-call(s32[8]{0:T(128)} %pad_add_fusion.order, bf16[8,272,128]{2,1,0:T(8,128)(2,1)} %copy-done, bf16[256,128]{1,0:T(8,128)(2,1)} %bitcast.16), custom_call_target="tpu_custom_call" | custom-call | tf_op jit(solution)/shard_map/finish/pallas_call | solution.py:151
  (60 shorter events, 1.3 us)
Async XLA Ops:
  3.3 27.2 %collective-permute-start = (bf16[560,128]{1,0:T(8,128)(2,1)S(1)}, bf16[560,128]{1,0:T(8,128)(2,1)S(1)}, u32[]{:S(2)}, u32[]{:S(2)}) collective-permute-start(bf16[560,128]{1,0:T(8,128)(2,1)S(1)} %fusion.1), channel_id=1, source_target_pairs={{0,8},{8,0},{16,24},{24,16},{32,40},{40,32},{48,56},{56,48},{64,72... | collective-permute-start | bytes 430088 | tf_op jit(solution)/shard_map/ppermute | solution.py:183
  5.2 31.4 %collective-permute-start.1 = (bf16[560,128]{1,0:T(8,128)(2,1)S(1)}, bf16[560,128]{1,0:T(8,128)(2,1)S(1)}, u32[]{:S(2)}, u32[]{:S(2)}) collective-permute-start(bf16[560,128]{1,0:T(8,128)(2,1)S(1)} %fusion.1), channel_id=1, source_target_pairs={{0,16},{8,24},{16,0},{24,8},{32,48},{40,56},{48,32},{56,40},{64,80... | collective-permute-start | bytes 430088 | tf_op jit(solution)/shard_map/ppermute | solution.py:183
  8.7 41.7 %collective-permute-start.2 = (bf16[560,128]{1,0:T(8,128)(2,1)S(1)}, bf16[560,128]{1,0:T(8,128)(2,1)S(1)}, u32[]{:S(2)}, u32[]{:S(2)}) collective-permute-start(bf16[560,128]{1,0:T(8,128)(2,1)S(1)} %fusion.1), channel_id=1, source_target_pairs={{0,32},{8,40},{16,48},{24,56},{32,0},{40,8},{48,16},{56,24},{64,96... | collective-permute-start | bytes 430088 | tf_op jit(solution)/shard_map/ppermute | solution.py:183
  13.3 40.6 %collective-permute-start.3 = (bf16[560,128]{1,0:T(8,128)(2,1)S(1)}, bf16[560,128]{1,0:T(8,128)(2,1)S(1)}, u32[]{:S(2)}, u32[]{:S(2)}) collective-permute-start(bf16[560,128]{1,0:T(8,128)(2,1)S(1)} %fusion.1), channel_id=1, source_target_pairs={{0,64},{8,72},{16,80},{24,88},{32,96},{40,104},{48,112},{56,120},{... | collective-permute-start | bytes 430088 | tf_op jit(solution)/shard_map/ppermute | solution.py:183
  17.6 36.3 %collective-permute-start.4 = (bf16[560,128]{1,0:T(8,128)(2,1)S(1)}, bf16[560,128]{1,0:T(8,128)(2,1)S(1)}, u32[]{:S(2)}, u32[]{:S(2)}) collective-permute-start(bf16[560,128]{1,0:T(8,128)(2,1)S(1)} %fusion.1), channel_id=1, source_target_pairs={{0,128},{8,136},{16,144},{24,152},{32,160},{40,168},{48,176},{56,1... | collective-permute-start | bytes 430088 | tf_op jit(solution)/shard_map/ppermute | solution.py:183
  28.4 87.3 %copy-start.2 = (bf16[2,256,128]{2,1,0:T(8,128)(2,1)}, bf16[2,256,128]{2,1,0:T(8,128)(2,1)S(1)}, u32[]{:S(2)}) copy-start(bf16[2,256,128]{2,1,0:T(8,128)(2,1)S(1)} %slice.48) | copy-start | bytes 393220
  30.5 23.3 %collective-permute-start.5 = (bf16[560,128]{1,0:T(8,128)(2,1)S(1)}, bf16[560,128]{1,0:T(8,128)(2,1)S(1)}, u32[]{:S(2)}, u32[]{:S(2)}) collective-permute-start(bf16[560,128]{1,0:T(8,128)(2,1)S(1)} %fusion.1), channel_id=1, source_target_pairs={{0,256},{8,264},{16,272},{24,280},{32,288},{40,296},{48,304},{56,3... | collective-permute-start | bytes 430088 | tf_op jit(solution)/shard_map/ppermute | solution.py:183
  36.7 32.0 %collective-permute-start.6 = (bf16[560,128]{1,0:T(8,128)(2,1)S(1)}, bf16[560,128]{1,0:T(8,128)(2,1)S(1)}, u32[]{:S(2)}, u32[]{:S(2)}) collective-permute-start(bf16[560,128]{1,0:T(8,128)(2,1)S(1)} %fusion.1), channel_id=1, source_target_pairs={{0,512},{8,520},{16,528},{24,536},{32,544},{40,552},{48,560},{56,5... | collective-permute-start | bytes 430088 | tf_op jit(solution)/shard_map/ppermute | solution.py:183
  50.4 25.8 %collective-permute-start.14 = (bf16[512,128]{1,0:T(8,128)(2,1)S(1)}, bf16[512,128]{1,0:T(8,128)(2,1)S(1)}, u32[]{:S(2)}, u32[]{:S(2)}) collective-permute-start(bf16[512,128]{1,0:T(8,128)(2,1)S(1)} %bitcast.13), channel_id=1, source_target_pairs={{0,1},{1,2},{2,3},{3,4},{4,5},{5,6},{6,7},{7,0},{8,9},{9,10},{10,1... | collective-permute-start | bytes 393224 | tf_op jit(solution)/shard_map/ppermute | solution.py:22
  68.9 57.0 %copy-start.1 = (bf16[2,272,128]{2,1,0:T(8,128)(2,1)}, bf16[2,272,128]{2,1,0:T(8,128)(2,1)S(1)}, u32[]{:S(2)}) copy-start(bf16[2,272,128]{2,1,0:T(8,128)(2,1)S(1)} %fusion.3) | copy-start | bytes 417796
  68.9 22.0 %collective-permute-start.7 = (bf16[544,128]{1,0:T(8,128)(2,1)S(1)}, bf16[544,128]{1,0:T(8,128)(2,1)S(1)}, u32[]{:S(2)}, u32[]{:S(2)}) collective-permute-start(bf16[544,128]{1,0:T(8,128)(2,1)S(1)} %bitcast.8), channel_id=1, source_target_pairs={{0,1},{1,2},{2,3},{3,4},{4,5},{5,6},{6,7},{7,0},{8,9},{9,10},{10,1... | collective-permute-start | bytes 417800 | tf_op jit(solution)/shard_map/ppermute | solution.py:22
  72.4 7.6 %collective-permute-start.15 = (bf16[512,128]{1,0:T(8,128)(2,1)S(1)}, bf16[512,128]{1,0:T(8,128)(2,1)S(1)}, u32[]{:S(2)}, u32[]{:S(2)}) collective-permute-start(bf16[512,128]{1,0:T(8,128)(2,1)S(1)} %bitcast.14), channel_id=1, source_target_pairs={{0,7},{1,0},{2,1},{3,2},{4,3},{5,4},{6,5},{7,6},{8,15},{9,8},{10,9... | collective-permute-start | bytes 393224 | tf_op jit(solution)/shard_map/ppermute | solution.py:25
  76.2 39.5 %copy-start.10 = (bf16[512,128]{1,0:T(8,128)(2,1)}, bf16[512,128]{1,0:T(8,128)(2,1)S(1)}, u32[]{:S(2)}) copy-start(bf16[512,128]{1,0:T(8,128)(2,1)S(1)} %collective-permute-done.14.refs_3_) | copy-start | bytes 393220
  76.2 11.5 %collective-permute-start.16 = (bf16[512,128]{1,0:T(8,128)(2,1)S(1)}, bf16[512,128]{1,0:T(8,128)(2,1)S(1)}, u32[]{:S(2)}, u32[]{:S(2)}) collective-permute-start(bf16[512,128]{1,0:T(8,128)(2,1)S(1)} %collective-permute-done.14.refs_3_), channel_id=1, source_target_pairs={{0,1},{1,2},{2,3},{3,4},{4,5},{5,6},{6,7},{7,0},{8,9},{9,10},{10,1... | collective-permute-start | bytes 393224 | tf_op jit(solution)/shard_map/ppermute | solution.py:22
  80.0 35.8 %copy-start.11 = (bf16[512,128]{1,0:T(8,128)(2,1)}, bf16[512,128]{1,0:T(8,128)(2,1)S(1)}, u32[]{:S(2)}) copy-start(bf16[512,128]{1,0:T(8,128)(2,1)S(1)} %collective-permute-done.15.refs_4_) | copy-start | bytes 393220
  80.0 14.0 %collective-permute-start.17 = (bf16[512,128]{1,0:T(8,128)(2,1)S(1)}, bf16[512,128]{1,0:T(8,128)(2,1)S(1)}, u32[]{:S(2)}, u32[]{:S(2)}) collective-permute-start(bf16[512,128]{1,0:T(8,128)(2,1)S(1)} %collective-permute-done.15.refs_4_), channel_id=1, source_target_pairs={{0,7},{1,0},{2,1},{3,2},{4,3},{5,4},{6,5},{7,6},{8,15},{9,8},{10,9... | collective-permute-start | bytes 393224 | tf_op jit(solution)/shard_map/ppermute | solution.py:25
  85.0 14.2 %collective-permute-start.8 = (bf16[544,128]{1,0:T(8,128)(2,1)S(1)}, bf16[544,128]{1,0:T(8,128)(2,1)S(1)}, u32[]{:S(2)}, u32[]{:S(2)}) collective-permute-start(bf16[544,128]{1,0:T(8,128)(2,1)S(1)} %bitcast.9), channel_id=1, source_target_pairs={{0,7},{1,0},{2,1},{3,2},{4,3},{5,4},{6,5},{7,6},{8,15},{9,8},{10,9... | collective-permute-start | bytes 417800 | tf_op jit(solution)/shard_map/ppermute | solution.py:25
  87.7 28.0 %copy-start.12 = (bf16[512,128]{1,0:T(8,128)(2,1)}, bf16[512,128]{1,0:T(8,128)(2,1)S(1)}, u32[]{:S(2)}) copy-start(bf16[512,128]{1,0:T(8,128)(2,1)S(1)} %collective-permute-done.16.refs_5_) | copy-start | bytes 393220
  87.7 14.2 %collective-permute-start.18 = (bf16[512,128]{1,0:T(8,128)(2,1)S(1)}, bf16[512,128]{1,0:T(8,128)(2,1)S(1)}, u32[]{:S(2)}, u32[]{:S(2)}) collective-permute-start(bf16[512,128]{1,0:T(8,128)(2,1)S(1)} %collective-permute-done.16.refs_5_), channel_id=1, source_target_pairs={{0,1},{1,2},{2,3},{3,4},{4,5},{5,6},{6,7},{7,0},{8,9},{9,10},{10,1... | collective-permute-start | bytes 393224 | tf_op jit(solution)/shard_map/ppermute | solution.py:22
  90.9 35.0 %copy-start.3 = (bf16[544,128]{1,0:T(8,128)(2,1)}, bf16[544,128]{1,0:T(8,128)(2,1)S(1)}, u32[]{:S(2)}) copy-start(bf16[544,128]{1,0:T(8,128)(2,1)S(1)} %collective-permute-done.7.refs_3_) | copy-start | bytes 417796
  90.9 14.2 %collective-permute-start.9 = (bf16[544,128]{1,0:T(8,128)(2,1)S(1)}, bf16[544,128]{1,0:T(8,128)(2,1)S(1)}, u32[]{:S(2)}, u32[]{:S(2)}) collective-permute-start(bf16[544,128]{1,0:T(8,128)(2,1)S(1)} %collective-permute-done.7.refs_3_), channel_id=1, source_target_pairs={{0,1},{1,2},{2,3},{3,4},{4,5},{5,6},{6,7},{7,0},{8,9},{9,10},{10,1... | collective-permute-start | bytes 417800 | tf_op jit(solution)/shard_map/ppermute | solution.py:22
  94.0 21.8 %copy-start.13 = (bf16[512,128]{1,0:T(8,128)(2,1)}, bf16[512,128]{1,0:T(8,128)(2,1)S(1)}, u32[]{:S(2)}) copy-start(bf16[512,128]{1,0:T(8,128)(2,1)S(1)} %collective-permute-done.17.refs_6_) | copy-start | bytes 393220
  94.0 21.7 %collective-permute-start.19 = (bf16[512,128]{1,0:T(8,128)(2,1)S(1)}, bf16[512,128]{1,0:T(8,128)(2,1)S(1)}, u32[]{:S(2)}, u32[]{:S(2)}) collective-permute-start(bf16[512,128]{1,0:T(8,128)(2,1)S(1)} %collective-permute-done.17.refs_6_), channel_id=1, source_target_pairs={{0,7},{1,0},{2,1},{3,2},{4,3},{5,4},{6,5},{7,6},{8,15},{9,8},{10,9... | collective-permute-start | bytes 393224 | tf_op jit(solution)/shard_map/ppermute | solution.py:25
  99.1 26.7 %copy-start.4 = (bf16[544,128]{1,0:T(8,128)(2,1)}, bf16[544,128]{1,0:T(8,128)(2,1)S(1)}, u32[]{:S(2)}) copy-start(bf16[544,128]{1,0:T(8,128)(2,1)S(1)} %collective-permute-done.8.refs_4_) | copy-start | bytes 417796
  99.2 7.9 %collective-permute-start.10 = (bf16[544,128]{1,0:T(8,128)(2,1)S(1)}, bf16[544,128]{1,0:T(8,128)(2,1)S(1)}, u32[]{:S(2)}, u32[]{:S(2)}) collective-permute-start(bf16[544,128]{1,0:T(8,128)(2,1)S(1)} %collective-permute-done.8.refs_4_), channel_id=1, source_target_pairs={{0,7},{1,0},{2,1},{3,2},{4,3},{5,4},{6,5},{7,6},{8,15},{9,8},{10,9... | collective-permute-start | bytes 417800 | tf_op jit(solution)/shard_map/ppermute | solution.py:25
  101.9 13.9 %copy-start.14 = (bf16[512,128]{1,0:T(8,128)(2,1)}, bf16[512,128]{1,0:T(8,128)(2,1)S(1)}, u32[]{:S(2)}) copy-start(bf16[512,128]{1,0:T(8,128)(2,1)S(1)} %collective-permute-done.18.refs_7_) | copy-start | bytes 393220
  101.9 13.8 %collective-permute-start.20 = (bf16[512,128]{1,0:T(8,128)(2,1)S(1)}, bf16[512,128]{1,0:T(8,128)(2,1)S(1)}, u32[]{:S(2)}, u32[]{:S(2)}) collective-permute-start(bf16[512,128]{1,0:T(8,128)(2,1)S(1)} %collective-permute-done.18.refs_7_), channel_id=1, source_target_pairs={{0,1},{1,2},{2,3},{3,4},{4,5},{5,6},{6,7},{7,0},{8,9},{9,10},{10,1... | collective-permute-start | bytes 393224 | tf_op jit(solution)/shard_map/ppermute | solution.py:22
  105.0 20.9 %copy-start.5 = (bf16[544,128]{1,0:T(8,128)(2,1)}, bf16[544,128]{1,0:T(8,128)(2,1)S(1)}, u32[]{:S(2)}) copy-start(bf16[544,128]{1,0:T(8,128)(2,1)S(1)} %collective-permute-done.9.refs_5_) | copy-start | bytes 417796
  105.0 8.2 %collective-permute-start.11 = (bf16[544,128]{1,0:T(8,128)(2,1)S(1)}, bf16[544,128]{1,0:T(8,128)(2,1)S(1)}, u32[]{:S(2)}, u32[]{:S(2)}) collective-permute-start(bf16[544,128]{1,0:T(8,128)(2,1)S(1)} %collective-permute-done.9.refs_5_), channel_id=1, source_target_pairs={{0,1},{1,2},{2,3},{3,4},{4,5},{5,6},{6,7},{7,0},{8,9},{9,10},{10,1... | collective-permute-start | bytes 417800 | tf_op jit(solution)/shard_map/ppermute | solution.py:22
  107.1 18.8 %copy-start.6 = (bf16[544,128]{1,0:T(8,128)(2,1)}, bf16[544,128]{1,0:T(8,128)(2,1)S(1)}, u32[]{:S(2)}) copy-start(bf16[544,128]{1,0:T(8,128)(2,1)S(1)} %collective-permute-done.10.refs_6_) | copy-start | bytes 417796
  107.1 18.8 %collective-permute-start.12 = (bf16[544,128]{1,0:T(8,128)(2,1)S(1)}, bf16[544,128]{1,0:T(8,128)(2,1)S(1)}, u32[]{:S(2)}, u32[]{:S(2)}) collective-permute-start(bf16[544,128]{1,0:T(8,128)(2,1)S(1)} %collective-permute-done.10.refs_6_), channel_id=1, source_target_pairs={{0,7},{1,0},{2,1},{3,2},{4,3},{5,4},{6,5},{7,6},{8,15},{9,8},{10,9... | collective-permute-start | bytes 417800 | tf_op jit(solution)/shard_map/ppermute | solution.py:25
  113.2 12.7 %copy-start.7 = (bf16[544,128]{1,0:T(8,128)(2,1)}, bf16[544,128]{1,0:T(8,128)(2,1)S(1)}, u32[]{:S(2)}) copy-start(bf16[544,128]{1,0:T(8,128)(2,1)S(1)} %collective-permute-done.11.refs_7_) | copy-start | bytes 417796
  113.2 12.6 %collective-permute-start.13 = (bf16[544,128]{1,0:T(8,128)(2,1)S(1)}, bf16[544,128]{1,0:T(8,128)(2,1)S(1)}, u32[]{:S(2)}, u32[]{:S(2)}) collective-permute-start(bf16[544,128]{1,0:T(8,128)(2,1)S(1)} %collective-permute-done.11.refs_7_), channel_id=1, source_target_pairs={{0,1},{1,2},{2,3},{3,4},{4,5},{5,6},{6,7},{7,0},{8,9},{9,10},{10,1... | collective-permute-start | bytes 417800 | tf_op jit(solution)/shard_map/ppermute | solution.py:22
  115.7 0.7 copy-start.15
  116.4 0.6 copy-start.16
  125.8 0.7 copy-start.8
  126.5 0.6 copy-start.9
  136.2 21.6 %all-to-all-start = ((bf16[8,272,128]{2,1,0:T(8,128)(2,1)}), bf16[8,272,128]{2,1,0:T(8,128)(2,1)S(1)}, u32[]{:S(2)}, u32[]{:S(2)}) async-start(bf16[8,272,128]{2,1,0:T(8,128)(2,1)} %late_pair.1), calls=%async_computation | async-start | bytes 1114112 | tf_op jit(solution)/shard_map/all_to_all | solution.py:200
  157.8 0.8 copy-start

commit v2 on v0

v2 whole, which is shorter than its diff:
```python
import jax
import jax.numpy as jnp
from jax import lax
from jax.experimental import pallas as pl
from jax.experimental.pallas import tpu as pltpu
from jax.sharding import PartitionSpec as P

ROWS_DEV = 64
LIVE = 4
MOVE = 2
STEP_ROOT = 0.1
N_CHOL = 8
OFFSETS = (0, -1, 1, -2, 2, -3, 3, -4)
TILE = 16
ORBS = 256
STRIDE = ORBS + TILE
STARTS = (0, ORBS, 2 * ORBS, 2 * ORBS + STRIDE)
RING_ROWS = 2 * ORBS + 2 * STRIDE
FIELD_ROW = MOVE * STRIDE

ANY = pl.BlockSpec(memory_space=pl.ANY)
WHOLE = pl.BlockSpec(memory_space=pltpu.VMEM)
SCALARS = pl.BlockSpec(memory_space=pltpu.SMEM)
F32 = jnp.float32
BF16 = jnp.bfloat16


def ring(block):
    up = [(i, (i + 1) % N_CHOL) for i in range(N_CHOL)]
    down = [(i, (i - 1) % N_CHOL) for i in range(N_CHOL)]
    parts, low, high = [block], block, block
    for step in range(N_CHOL // 2):
        low = lax.ppermute(low, "chol", up)
        parts.append(low)
        if step < N_CHOL // 2 - 1:
            high = lax.ppermute(high, "chol", down)
            parts.append(high)
    return parts


def inv_rows(inv, slot):
    share = pl.multiple_of(lax.axis_index("chol") * TILE, TILE)
    return inv.at[slot, pl.ds(share, TILE)]


def pack_kernel(walkers, inv, fields, out, sems):
    copies = []
    for j in range(MOVE):
        rows = out.at[pl.ds(j * STRIDE, ORBS)]
        copies.append(pltpu.make_async_copy(walkers.at[LIVE + j], rows, sems.at[2 * j]))
        rows = out.at[pl.ds(j * STRIDE + ORBS, TILE)]
        copies.append(pltpu.make_async_copy(inv_rows(inv, LIVE + j), rows, sems.at[2 * j + 1]))
    for copy in copies:
        copy.start()
    out[FIELD_ROW:] = jnp.zeros((TILE, out.shape[1]), BF16)
    out[FIELD_ROW : FIELD_ROW + fields.shape[0], : fields.shape[1]] = fields[...]
    for copy in copies:
        copy.wait()


def pack_call(walkers, inv, fields):
    return pl.pallas_call(
        pack_kernel,
        in_specs=[ANY, ANY, WHOLE],
        out_specs=WHOLE,
        out_shape=jax.ShapeDtypeStruct((FIELD_ROW + TILE, walkers.shape[2]), BF16),
        scratch_shapes=[pltpu.SemaphoreType.DMA((2 * MOVE,))],
        name="pack",
    )(walkers, inv, fields)


def merge_kernel(bits, counts, partner, fields, walkers, inv, *refs):
    received, (out, x, moved, sems) = refs[:bits], refs[bits:]
    walk = lax.axis_index("walk")
    own = counts[walk]
    distance = jnp.bitwise_xor(partner[walk], walk)

    def start(slot, source, size, sem, first=0):
        rows = out.at[pl.ds(STARTS[slot] + first, size)]
        pltpu.make_async_copy(source, rows, sems.at[sem]).start()

    start(0, walkers.at[0], ORBS, 0)
    start(1, walkers.at[1], ORBS, 1)
    for slot in (2, 3):

        @pl.when(own > slot)
        def _():
            start(slot, walkers.at[slot], ORBS, slot)
            start(slot, inv_rows(inv, slot), TILE, slot + 2, ORBS)

    for bit in range(bits):

        @pl.when(distance == 1 << bit)
        def _():
            block = received[bit]
            pltpu.make_async_copy(block.at[pl.ds(FIELD_ROW, TILE)], moved, sems.at[6]).start()
            for slot in (2, 3):

                @pl.when(own <= slot)
                def _():
                    first = (3 - slot) * STRIDE
                    start(slot, block.at[pl.ds(first, ORBS)], ORBS, slot)
                    start(slot, block.at[pl.ds(first + ORBS, TILE)], TILE, slot + 2, ORBS)

    def wait(slot, size, sem, first=0):
        rows = out.at[pl.ds(STARTS[slot] + first, size)]
        pltpu.make_async_copy(rows, rows, sems.at[sem]).wait()

    pltpu.make_async_copy(moved, moved, sems.at[6]).wait()
    mine = fields[...].astype(F32)
    theirs = moved[: fields.shape[0], : fields.shape[1]].astype(F32)
    x[...] = jnp.zeros_like(x)
    for slot in range(LIVE):
        row = mine[slot : slot + 1]
        if slot > 1:
            sent = LIVE + 3 - slot
            row = jnp.where(own > slot, row, theirs[sent : sent + 1])
        x[slot : slot + 1, : fields.shape[1]] = row
    for slot in range(LIVE):
        wait(slot, ORBS, slot)
        if slot > 1:
            wait(slot, TILE, slot + 2, ORBS)


def merge_call(counts, partner, fields, walkers, inv, received):
    bits, lanes = len(received), walkers.shape[2]

    def body(*refs):
        merge_kernel(bits, *refs)

    return pl.pallas_call(
        body,
        in_specs=[SCALARS, SCALARS, WHOLE, ANY, ANY] + [ANY] * bits,
        out_specs=(WHOLE, WHOLE),
        out_shape=(
            jax.ShapeDtypeStruct((RING_ROWS, lanes), BF16),
            jax.ShapeDtypeStruct((8, lanes), F32),
        ),
        scratch_shapes=[pltpu.VMEM((TILE, lanes), BF16), pltpu.SemaphoreType.DMA((7,))],
        name="merge",
    )(counts, partner, fields, walkers, inv, *received)


def product_kernel(x, chol, trial, inv, *refs):
    parts, (out, minv) = refs[:N_CHOL], refs[N_CHOL:]
    lanes = out.shape[2]
    me = lax.axis_index("chol")
    owners = [jnp.bitwise_and(me + offset, N_CHOL - 1) for offset in OFFSETS]
    columns = [pl.ds(pl.multiple_of(owner * ORBS, ORBS), ORBS) for owner in owners]
    for owner, part in zip(owners, parts):
        share = pl.ds(pl.multiple_of(owner * TILE, TILE), TILE)
        for q in range(2):
            first = STARTS[2 + q] + ORBS
            minv[q, share] = part[first : first + TILE]
    row_id = lax.broadcasted_iota(jnp.int32, (TILE, lanes), 0)
    lane_id = lax.broadcasted_iota(jnp.int32, (TILE, lanes), 1)
    logs = jnp.zeros((TILE, lanes), F32)
    for pair in range(2):
        slots = (2 * pair, 2 * pair + 1)
        phi = jnp.concatenate(
            [
                jnp.concatenate([part[STARTS[s] : STARTS[s] + ORBS] for s in slots], axis=1)
                for part in parts
            ],
            axis=0,
        )
        products = []
        for g in range(chol.shape[0]):
            rows = jnp.concatenate([chol[g, :, spot] for spot in columns], axis=1)
            products.append(jnp.dot(rows, phi, preferred_element_type=F32))
        for q, slot in enumerate(slots):
            weighted = lax.dot_general(
                trial[...],
                minv[q] if pair else inv[q],
                (((1,), (1,)), ((), ())),
                preferred_element_type=F32,
            )
            total = jnp.zeros_like(weighted)
            log = jnp.zeros((1, 1), F32)
            for g, both in enumerate(products):
                product = both[:, q * lanes : (q + 1) * lanes]
                bias = -STEP_ROOT * jnp.sum(product * weighted, keepdims=True)
                field = x[slot : slot + 1, g : g + 1]
                total += STEP_ROOT * (field - bias) * product
                log += field * bias - 0.5 * bias * bias
            spread = total.astype(BF16).reshape(N_CHOL, ROWS_DEV, lanes)
            out[:, slot * ROWS_DEV : (slot + 1) * ROWS_DEV] = spread
            high = log.astype(BF16).astype(F32)
            here = row_id == slot
            logs = jnp.where(here & (lane_id == 0), high, logs)
            logs = jnp.where(here & (lane_id == 1), log - high, logs)
    for k in range(N_CHOL):
        out[k, LIVE * ROWS_DEV :] = logs.astype(BF16)


def product_call(x, cholesky, trial, inv, parts):
    lanes = trial.shape[1]
    vectors, window, orbitals = cholesky.shape
    flops = 2 * LIVE * vectors * window * orbitals * lanes
    return pl.pallas_call(
        product_kernel,
        in_specs=[WHOLE] * (4 + N_CHOL),
        out_specs=WHOLE,
        out_shape=jax.ShapeDtypeStruct((N_CHOL, LIVE * ROWS_DEV + TILE, lanes), BF16),
        scratch_shapes=[pltpu.VMEM((2, lanes, lanes), BF16)],
        name="products",
        cost_estimate=pl.CostEstimate(flops=flops, bytes_accessed=6 << 20, transcendentals=0),
    )(x, cholesky, trial, inv, *parts)


def finish_kernel(counts, partner, got, block, out, log_out):
    walk = lax.axis_index("walk")
    own = jnp.minimum(counts[walk], LIVE)
    arriving = jnp.maximum(counts[partner[walk]] - LIVE, 0)
    tile = jnp.zeros((TILE, got.shape[2]), F32)
    for k in range(N_CHOL):
        tile += got[k, LIVE * ROWS_DEV :].astype(F32)
    row_id = lax.broadcasted_iota(jnp.int32, tile.shape, 0)
    for slot in range(LIVE):
        mine = slot < own
        live = mine | (slot - own < arriving)
        spot = jnp.where(mine, slot, jnp.clip(LIVE - 1 - slot + own, 0, LIVE - 1))
        first = spot * ORBS + jnp.maximum(spot - 2, 0) * TILE
        total = block[pl.ds(pl.multiple_of(first, TILE), ROWS_DEV)].astype(F32)
        rows = pl.ds(pl.multiple_of(spot * ROWS_DEV, ROWS_DEV), ROWS_DEV)
        for k in range(N_CHOL):
            total += got[k, rows].astype(F32)
        out[slot] = jnp.where(live, total, 0.0).astype(BF16)
        log_out[slot] = jnp.where(live, jnp.sum(jnp.where(row_id == spot, tile, 0.0)), 0.0)


def finish_call(counts, partner, got, block):
    lanes = got.shape[2]
    return pl.pallas_call(
        finish_kernel,
        in_specs=[SCALARS, SCALARS, WHOLE, WHOLE],
        out_specs=(WHOLE, SCALARS),
        out_shape=(
            jax.ShapeDtypeStruct((LIVE, ROWS_DEV, lanes), BF16),
            jax.ShapeDtypeStruct((LIVE,), F32),
        ),
        name="finish",
    )(counts, partner, got, block)


def shards(walkers, inv_intersection, fields, cholesky, trial_rows, counts, partner):
    walk_size = lax.axis_size("walk")
    outgoing = pack_call(walkers, inv_intersection, fields)
    received = []
    for bit in range(walk_size.bit_length() - 1):
        route = [(i, i ^ 1 << bit) for i in range(walk_size)]
        received.append(lax.ppermute(outgoing, "walk", route))
    block, x = merge_call(counts, partner, fields, walkers, inv_intersection, received)
    parts = ring(block)
    sums = product_call(x, cholesky, trial_rows, inv_intersection, parts)
    sums = lax.all_to_all(sums, "chol", 0, 0, tiled=True)
    return tuple(finish_call(counts, partner, sums, block))


def solution(mesh):
    in_specs = (
        P("walk", "chol", None),
        P("walk", None, None),
        P("walk", "chol"),
        P("chol", None, None),
        P(),
        P(),
        P(),
    )
    out_specs = (P("walk", "chol", None), P("walk"))
    return jax.shard_map(shards, mesh=mesh, in_specs=in_specs, out_specs=out_specs, check_vma=False)
```

time: 246 us -> 131 us (0.53)
  waiting for transfers between devices: 91.8 us -> 26.2 us
  starting transfers between devices: 97.2 us -> 65.7 us
  between operations: 19 us -> 0.95 us
  Pallas kernels: 0 us -> 13.5 us
  matrix products: 8.57 us -> 0 us
  local copies, waits for them, and re-layouts: 9.78 us -> 2.71 us
  blocking collectives: 16.4 us -> 20.9 us
  other arithmetic: 2.77 us -> 0 us
    unnamed x3 -> x0, waiting for transfers between devices: 71.6 us -> none
    ppermute x21 -> x14, starting transfers between devices: 97.1 us -> 65.7 us  [the longest x7 42.4 us: shards(): received.append(lax.ppermute(outgoing, 'walk', route))]
    all_to_all x0 -> x1, blocking collectives: none -> 20.9 us  [shards(): sums = lax.all_to_all(sums, 'chol', 0, 0, tiled=True)]
    psum x1 -> x0, blocking collectives: 16.4 us -> none  [propagate(): log_terms = lax.psum(weight_terms, 'chol')]
    pallas_call x0 -> x4, Pallas kernels: none -> 13.5 us  [the longest x1 6.95 us: product_call(): pl.pallas_call(product_kernel, in_specs=[WHOLE] * (4 + N_CHOL), out_specs...]
    dot_general x3 -> x0, matrix products: 8.57 us -> none  [the longest x1 5.18 us: propagate(): jnp.einsum('grk,wkn->wgrn', cholesky, lax.all_gather(walker_rows, 'chol',...]
    ppermute x21 -> x14, waiting for transfers between devices: 20.2 us -> 26.2 us  [the longest x4 19.7 us: ring(): low = lax.ppermute(low, 'chol', up)]
    dynamic_slice x2 -> x0, local copies, waits for them, and re-layouts: 2.57 us -> none  [the longest x1 1.32 us: shards(): own_count = counts[walk_index]]
  transfers between devices with their start and end apart: 23 -> 14, of which waited for: 9 -> 6; matrix products, arithmetic and copies ran while one was open for 3% -> 0% of each run, Pallas kernels for 0% -> 0%
where the time goes in v2:
time: 131 us; the launch traced here: 130 us
  starting transfers between devices  65.7 us (50%)
  waiting for transfers between devices  26.2 us (20%)
  blocking collectives  20.9 us (16%)
  Pallas kernels  13.5 us (10%)
  local copies, waits for them, and re-layouts  2.71 us (2%)
    ppermute x7, starting transfers between devices, shards(): received.append(lax.ppermute(outgoing, 'walk', route))  42.4 us
    all_to_all x1, blocking collectives, shards(): sums = lax.all_to_all(sums, 'chol', 0, 0, tiled=True)  20.9 us
    ppermute x4, waiting for transfers between devices, ring(): low = lax.ppermute(low, 'chol', up)  19.7 us
    ppermute x3, starting transfers between devices, ring(): high = lax.ppermute(high, 'chol', down)  14.1 us
    ppermute x4, starting transfers between devices, ring(): low = lax.ppermute(low, 'chol', up)  9.21 us
    pallas_call x1, Pallas kernels, product_call(): pl.pallas_call(product_kernel, in_specs=[WHOLE] * (4 + N_CHOL), out_specs...  6.95 us
    ppermute x7, waiting for transfers between devices, shards(): received.append(lax.ppermute(outgoing, 'walk', route))  6.47 us
    unnamed x29, local copies, waits for them, and re-layouts  2.71 us
  transfers between devices with their start and end apart: 14, of which 6 were waited for; matrix products, arithmetic and copies ran while one was open for 0% of the time, Pallas kernels for 0%

profile of v2, /device:TPU:2, one launch (start us, length us, event | category | flops | bytes accessed | tf_op | source)
XLA Modules:
  0.0 130.0 jit_solution(18156953096559537564)
XLA Ops:
  0.6 1.3 %copy.10.fields.refs_2_ = bf16[6,2]{1,0:T(8,128)(2,1)} copy(bf16[6,2]{0,1:T(2,128)(2,1)} %param.9) | data formatting | bytes 48 | tf_op args[2]
  1.9 2.3 %pack.1 = bf16[560,128]{1,0:T(8,128)(2,1)} custom-call(bf16[6,256,128]{2,1,0:T(8,128)(2,1)} %refs_3_.1, bf16[6,128,128]{2,1,0:T(8,128)(2,1)} %inv.3, bf16[6,2]{1,0:T(8,128)(2,1)} %copy.10.fields.refs_2_), custom_call_target="tpu_custom_call" | custom-call | tf_op jit(solution)/shard_map/pack/pallas_call | solution.py:62
  4.2 19.4 %collective-permute-start.6 = (bf16[560,128]{1,0:T(8,128)(2,1)}, bf16[560,128]{1,0:T(8,128)(2,1)S(1)}, u32[]{:S(2)}, u32[]{:S(2)}) collective-permute-start(bf16[560,128]{1,0:T(8,128)(2,1)} %pack.1), channel_id=1, source_target_pairs={{0,512},{8,520},{16,528},{24,536},{32,544},{40,552},{48,560},{56,5... | collective-permute-start | bytes 430088 | tf_op jit(solution)/shard_map/ppermute | solution.py:252
  23.6 6.1 %collective-permute-start.5 = (bf16[560,128]{1,0:T(8,128)(2,1)}, bf16[560,128]{1,0:T(8,128)(2,1)S(1)}, u32[]{:S(2)}, u32[]{:S(2)}) collective-permute-start(bf16[560,128]{1,0:T(8,128)(2,1)} %pack.1), channel_id=1, source_target_pairs={{0,256},{8,264},{16,272},{24,280},{32,288},{40,296},{48,304},{56,3... | collective-permute-start | bytes 430088 | tf_op jit(solution)/shard_map/ppermute | solution.py:252
  29.7 4.3 %collective-permute-start.4 = (bf16[560,128]{1,0:T(8,128)(2,1)}, bf16[560,128]{1,0:T(8,128)(2,1)S(1)}, u32[]{:S(2)}, u32[]{:S(2)}) collective-permute-start(bf16[560,128]{1,0:T(8,128)(2,1)} %pack.1), channel_id=1, source_target_pairs={{0,128},{8,136},{16,144},{24,152},{32,160},{40,168},{48,176},{56,1... | collective-permute-start | bytes 430088 | tf_op jit(solution)/shard_map/ppermute | solution.py:252
  34.0 3.4 %collective-permute-start.3 = (bf16[560,128]{1,0:T(8,128)(2,1)}, bf16[560,128]{1,0:T(8,128)(2,1)S(1)}, u32[]{:S(2)}, u32[]{:S(2)}) collective-permute-start(bf16[560,128]{1,0:T(8,128)(2,1)} %pack.1), channel_id=1, source_target_pairs={{0,64},{8,72},{16,80},{24,88},{32,96},{40,104},{48,112},{56,120},{... | collective-permute-start | bytes 430088 | tf_op jit(solution)/shard_map/ppermute | solution.py:252
  37.4 4.0 %collective-permute-start.2 = (bf16[560,128]{1,0:T(8,128)(2,1)}, bf16[560,128]{1,0:T(8,128)(2,1)S(1)}, u32[]{:S(2)}, u32[]{:S(2)}) collective-permute-start(bf16[560,128]{1,0:T(8,128)(2,1)} %pack.1), channel_id=1, source_target_pairs={{0,32},{8,40},{16,48},{24,56},{32,0},{40,8},{48,16},{56,24},{64,96... | collective-permute-start | bytes 430088 | tf_op jit(solution)/shard_map/ppermute | solution.py:252
  41.4 0.0 collective-permute-done.6.refs_11_
  41.4 0.0 copy-start
  41.4 3.3 %collective-permute-start.1 = (bf16[560,128]{1,0:T(8,128)(2,1)}, bf16[560,128]{1,0:T(8,128)(2,1)S(1)}, u32[]{:S(2)}, u32[]{:S(2)}) collective-permute-start(bf16[560,128]{1,0:T(8,128)(2,1)} %pack.1), channel_id=1, source_target_pairs={{0,16},{8,24},{16,0},{24,8},{32,48},{40,56},{48,32},{56,40},{64,80... | collective-permute-start | bytes 430088 | tf_op jit(solution)/shard_map/ppermute | solution.py:252
  44.8 5.0 %collective-permute-done.5.refs_10_ = bf16[560,128]{1,0:T(8,128)(2,1)S(1)} collective-permute-done((bf16[560,128]{1,0:T(8,128)(2,1)}, bf16[560,128]{1,0:T(8,128)(2,1)S(1)}, u32[]{:S(2)}, u32[]{:S(2)}) %collective-permute-start.5) | collective-permute-done | bytes 143392 | tf_op jit(solution)/shard_map/ppermute | solution.py:252
  49.8 1.9 %collective-permute-start = (bf16[560,128]{1,0:T(8,128)(2,1)}, bf16[560,128]{1,0:T(8,128)(2,1)S(1)}, u32[]{:S(2)}, u32[]{:S(2)}) collective-permute-start(bf16[560,128]{1,0:T(8,128)(2,1)} %pack.1), channel_id=1, source_target_pairs={{0,8},{8,0},{16,24},{24,16},{32,40},{40,32},{48,56},{56,48},{64,72... | collective-permute-start | bytes 430088 | tf_op jit(solution)/shard_map/ppermute | solution.py:252
  51.7 0.0 collective-permute-done.4.refs_9_
  51.7 0.0 copy-start.2
  51.7 0.0 collective-permute-done.3.refs_8_
  51.7 0.0 copy-start.3
  51.8 0.0 collective-permute-done.2.refs_7_
  51.8 0.0 copy-start.4
  51.8 0.0 collective-permute-done.1.refs_6_
  51.8 0.0 copy-start.5
  51.8 1.5 %collective-permute-done.refs_5_ = bf16[560,128]{1,0:T(8,128)(2,1)S(1)} collective-permute-done((bf16[560,128]{1,0:T(8,128)(2,1)}, bf16[560,128]{1,0:T(8,128)(2,1)S(1)}, u32[]{:S(2)}, u32[]{:S(2)}) %collective-permute-start) | collective-permute-done | bytes 143392 | tf_op jit(solution)/shard_map/ppermute | solution.py:252
  53.3 0.0 copy-done.2
  53.3 0.0 copy-done.3
  53.3 0.0 copy-done.4
  53.3 0.0 copy-done.5
  53.3 0.0 copy-start.6
  53.3 0.7 copy-done.6
  54.0 2.4 %merge.1 = (bf16[1056,128]{1,0:T(8,128)(2,1)}, f32[8,128]{1,0:T(8,128)}) custom-call(s32[128]{0:T(128)} %counts.1, s32[128]{0:T(128)} %partner.1, bf16[6,2]{1,0:T(8,128)(2,1)} %copy.10.fields.refs_2_, bf16[6,256,128]{2,1,0:T(8,128)(2,1)} %refs_3_.1, bf16[6,128,128]{2,1,0:T(8,128)(2,1)} %inv.3, bf16[560,128]{1,0:T(8,128)(2,1)} %copy-done.6, ...), custom_call_target="tpu_custom_call" | custom-call | tf_op jit(solution)/shard_map/merge/pallas_call | solution.py:131
  56.4 3.5 %collective-permute-start.7 = (bf16[1056,128]{1,0:T(8,128)(2,1)}, bf16[1056,128]{1,0:T(8,128)(2,1)S(1)}, u32[]{:S(2)}, u32[]{:S(2)}) collective-permute-start(bf16[1056,128]{1,0:T(8,128)(2,1)} %get-tuple-element.5.refs_0_.block), channel_id=1, source_target_pairs={{0,1},{1,2},{2,3},{3,4},{4,5},{5,6},{6,7},{7,0},{8,9},{9,10},{10,1... | collective-permute-start | bytes 811016 | tf_op jit(solution)/shard_map/ppermute | solution.py:33
  59.9 3.8 %collective-permute-start.8 = (bf16[1056,128]{1,0:T(8,128)(2,1)}, bf16[1056,128]{1,0:T(8,128)(2,1)S(1)}, u32[]{:S(2)}, u32[]{:S(2)}) collective-permute-start(bf16[1056,128]{1,0:T(8,128)(2,1)} %get-tuple-element.5.refs_0_.block), channel_id=1, source_target_pairs={{0,7},{1,0},{2,1},{3,2},{4,3},{5,4},{6,5},{7,6},{8,15},{9,8},{10,9... | collective-permute-start | bytes 811016 | tf_op jit(solution)/shard_map/ppermute | solution.py:36
  63.7 5.1 %collective-permute-done.7.refs_1_ = bf16[1056,128]{1,0:T(8,128)(2,1)S(1)} collective-permute-done((bf16[1056,128]{1,0:T(8,128)(2,1)}, bf16[1056,128]{1,0:T(8,128)(2,1)S(1)}, u32[]{:S(2)}, u32[]{:S(2)}) %collective-permute-start.7) | collective-permute-done | bytes 270368 | tf_op jit(solution)/shard_map/ppermute | solution.py:33
  68.7 1.9 %collective-permute-start.9 = (bf16[1056,128]{1,0:T(8,128)(2,1)S(1)}, bf16[1056,128]{1,0:T(8,128)(2,1)S(1)}, u32[]{:S(2)}, u32[]{:S(2)}) collective-permute-start(bf16[1056,128]{1,0:T(8,128)(2,1)S(1)} %collective-permute-done.7.refs_1_), channel_id=1, source_target_pairs={{0,1},{1,2},{2,3},{3,4},{4,5},{5,6},{6,7},{7,0},{8,9},{9,10},{10,1... | collective-permute-start | bytes 811016 | tf_op jit(solution)/shard_map/ppermute | solution.py:33
  70.6 0.0 collective-permute-done.8.refs_2_
  70.7 0.0 copy-start.8
  70.7 5.1 %collective-permute-start.10 = (bf16[1056,128]{1,0:T(8,128)(2,1)S(1)}, bf16[1056,128]{1,0:T(8,128)(2,1)S(1)}, u32[]{:S(2)}, u32[]{:S(2)}) collective-permute-start(bf16[1056,128]{1,0:T(8,128)(2,1)S(1)} %collective-permute-done.8.refs_2_), channel_id=1, source_target_pairs={{0,7},{1,0},{2,1},{3,2},{4,3},{5,4},{6,5},{7,6},{8,15},{9,8},{10,9... | collective-permute-start | bytes 811016 | tf_op jit(solution)/shard_map/ppermute | solution.py:36
  75.8 4.0 %collective-permute-done.9.refs_3_ = bf16[1056,128]{1,0:T(8,128)(2,1)S(1)} collective-permute-done((bf16[1056,128]{1,0:T(8,128)(2,1)S(1)}, bf16[1056,128]{1,0:T(8,128)(2,1)S(1)}, u32[]{:S(2)}, u32[]{:S(2)}) %collective-permute-start.9) | collective-permute-done | bytes 270368 | tf_op jit(solution)/shard_map/ppermute | solution.py:33
  79.8 1.9 %collective-permute-start.11 = (bf16[1056,128]{1,0:T(8,128)(2,1)S(1)}, bf16[1056,128]{1,0:T(8,128)(2,1)S(1)}, u32[]{:S(2)}, u32[]{:S(2)}) collective-permute-start(bf16[1056,128]{1,0:T(8,128)(2,1)S(1)} %collective-permute-done.9.refs_3_), channel_id=1, source_target_pairs={{0,1},{1,2},{2,3},{3,4},{4,5},{5,6},{6,7},{7,0},{8,9},{9,10},{10,1... | collective-permute-start | bytes 811016 | tf_op jit(solution)/shard_map/ppermute | solution.py:33
  81.7 0.0 collective-permute-done.10.refs_4_
  81.7 0.0 copy-start.10
  81.7 5.1 %collective-permute-start.12 = (bf16[1056,128]{1,0:T(8,128)(2,1)S(1)}, bf16[1056,128]{1,0:T(8,128)(2,1)S(1)}, u32[]{:S(2)}, u32[]{:S(2)}) collective-permute-start(bf16[1056,128]{1,0:T(8,128)(2,1)S(1)} %collective-permute-done.10.refs_4_), channel_id=1, source_target_pairs={{0,7},{1,0},{2,1},{3,2},{4,3},{5,4},{6,5},{7,6},{8,15},{9,8},{10,9... | collective-permute-start | bytes 811016 | tf_op jit(solution)/shard_map/ppermute | solution.py:36
  86.9 3.1 %collective-permute-done.11.refs_5_ = bf16[1056,128]{1,0:T(8,128)(2,1)S(1)} collective-permute-done((bf16[1056,128]{1,0:T(8,128)(2,1)S(1)}, bf16[1056,128]{1,0:T(8,128)(2,1)S(1)}, u32[]{:S(2)}, u32[]{:S(2)}) %collective-permute-start.11) | collective-permute-done | bytes 270368 | tf_op jit(solution)/shard_map/ppermute | solution.py:33
  90.0 1.9 %collective-permute-start.13 = (bf16[1056,128]{1,0:T(8,128)(2,1)S(1)}, bf16[1056,128]{1,0:T(8,128)(2,1)S(1)}, u32[]{:S(2)}, u32[]{:S(2)}) collective-permute-start(bf16[1056,128]{1,0:T(8,128)(2,1)S(1)} %collective-permute-done.11.refs_5_), channel_id=1, source_target_pairs={{0,1},{1,2},{2,3},{3,4},{4,5},{5,6},{6,7},{7,0},{8,9},{9,10},{10,1... | collective-permute-start | bytes 811016 | tf_op jit(solution)/shard_map/ppermute | solution.py:33
  91.9 0.0 collective-permute-done.12.refs_6_
  91.9 7.6 %collective-permute-done.13.refs_7_ = bf16[1056,128]{1,0:T(8,128)(2,1)S(1)} collective-permute-done((bf16[1056,128]{1,0:T(8,128)(2,1)S(1)}, bf16[1056,128]{1,0:T(8,128)(2,1)S(1)}, u32[]{:S(2)}, u32[]{:S(2)}) %collective-permute-start.13) | collective-permute-done | bytes 270368 | tf_op jit(solution)/shard_map/ppermute | solution.py:33
  99.6 0.7 copy-done.13
  100.2 7.0 %products.1 = bf16[8,272,128]{2,1,0:T(8,128)(2,1)} custom-call(f32[8,128]{1,0:T(8,128)} %get-tuple-element.4.x, bf16[2,512,2048]{2,1,0:T(8,128)(2,1)} %chol.1, bf16[512,128]{1,0:T(8,128)(2,1)} %trial.1, bf16[6,128,128]{2,1,0:T(8,128)(2,1)} %inv.3, bf16[1056,128]{1,0:T(8,128)(2,1)} %get-tuple-element.5.refs_0_.block, bf16[1056,128]{1,0:T(8,128)(2,1)} %copy-done.7, ...), custom_call_target="tpu_custom_call" | custom-call | flops 2147483648 | bytes 6291456 | tf_op jit(solution)/shard_map/products/pallas_call | solution.py:200
  107.2 20.9 %all_to_all.5.got = bf16[8,272,128]{2,1,0:T(8,128)(2,1)} all-to-all(bf16[8,272,128]{2,1,0:T(8,128)(2,1)} %products.1), channel_id=1, replica_groups=mesh['walk'=128,'chol'=8] {'chol'}, dimensions={0} | all-to-all | bytes 1114112 | tf_op jit(solution)/shard_map/all_to_all | solution.py:256
  128.1 1.9 %finish.1 = (bf16[4,64,128]{2,1,0:T(8,128)(2,1)}, f32[4]{0:T(128)}) custom-call(s32[128]{0:T(128)} %counts.1, s32[128]{0:T(128)} %partner.1, bf16[8,272,128]{2,1,0:T(8,128)(2,1)} %all_to_all.5.got, bf16[1056,128]{1,0:T(8,128)(2,1)} %get-tuple-element.5.refs_0_.block), custom_call_target="tpu_custom_call" | custom-call | tf_op jit(solution)/shard_map/finish/pallas_call | solution.py:234
  (14 shorter events, 0.0 us)
Async XLA Ops:
  4.2 37.2 %collective-permute-start.6 = (bf16[560,128]{1,0:T(8,128)(2,1)}, bf16[560,128]{1,0:T(8,128)(2,1)S(1)}, u32[]{:S(2)}, u32[]{:S(2)}) collective-permute-start(bf16[560,128]{1,0:T(8,128)(2,1)} %pack.1), channel_id=1, source_target_pairs={{0,512},{8,520},{16,528},{24,536},{32,544},{40,552},{48,560},{56,5... | collective-permute-start | bytes 430088 | tf_op jit(solution)/shard_map/ppermute | solution.py:252
  23.6 26.2 %collective-permute-start.5 = (bf16[560,128]{1,0:T(8,128)(2,1)}, bf16[560,128]{1,0:T(8,128)(2,1)S(1)}, u32[]{:S(2)}, u32[]{:S(2)}) collective-permute-start(bf16[560,128]{1,0:T(8,128)(2,1)} %pack.1), channel_id=1, source_target_pairs={{0,256},{8,264},{16,272},{24,280},{32,288},{40,296},{48,304},{56,3... | collective-permute-start | bytes 430088 | tf_op jit(solution)/shard_map/ppermute | solution.py:252
  29.7 22.0 %collective-permute-start.4 = (bf16[560,128]{1,0:T(8,128)(2,1)}, bf16[560,128]{1,0:T(8,128)(2,1)S(1)}, u32[]{:S(2)}, u32[]{:S(2)}) collective-permute-start(bf16[560,128]{1,0:T(8,128)(2,1)} %pack.1), channel_id=1, source_target_pairs={{0,128},{8,136},{16,144},{24,152},{32,160},{40,168},{48,176},{56,1... | collective-permute-start | bytes 430088 | tf_op jit(solution)/shard_map/ppermute | solution.py:252
  34.0 17.7 %collective-permute-start.3 = (bf16[560,128]{1,0:T(8,128)(2,1)}, bf16[560,128]{1,0:T(8,128)(2,1)S(1)}, u32[]{:S(2)}, u32[]{:S(2)}) collective-permute-start(bf16[560,128]{1,0:T(8,128)(2,1)} %pack.1), channel_id=1, source_target_pairs={{0,64},{8,72},{16,80},{24,88},{32,96},{40,104},{48,112},{56,120},{... | collective-permute-start | bytes 430088 | tf_op jit(solution)/shard_map/ppermute | solution.py:252
  37.4 14.4 %collective-permute-start.2 = (bf16[560,128]{1,0:T(8,128)(2,1)}, bf16[560,128]{1,0:T(8,128)(2,1)S(1)}, u32[]{:S(2)}, u32[]{:S(2)}) collective-permute-start(bf16[560,128]{1,0:T(8,128)(2,1)} %pack.1), channel_id=1, source_target_pairs={{0,32},{8,40},{16,48},{24,56},{32,0},{40,8},{48,16},{56,24},{64,96... | collective-permute-start | bytes 430088 | tf_op jit(solution)/shard_map/ppermute | solution.py:252
  41.4 11.8 %copy-start = (bf16[560,128]{1,0:T(8,128)(2,1)}, bf16[560,128]{1,0:T(8,128)(2,1)S(1)}, u32[]{:S(2)}) copy-start(bf16[560,128]{1,0:T(8,128)(2,1)S(1)} %collective-permute-done.6.refs_11_) | copy-start | bytes 430084
  41.4 10.3 %collective-permute-start.1 = (bf16[560,128]{1,0:T(8,128)(2,1)}, bf16[560,128]{1,0:T(8,128)(2,1)S(1)}, u32[]{:S(2)}, u32[]{:S(2)}) collective-permute-start(bf16[560,128]{1,0:T(8,128)(2,1)} %pack.1), channel_id=1, source_target_pairs={{0,16},{8,24},{16,0},{24,8},{32,48},{40,56},{48,32},{56,40},{64,80... | collective-permute-start | bytes 430088 | tf_op jit(solution)/shard_map/ppermute | solution.py:252
  49.8 3.5 %copy-start.1 = (bf16[560,128]{1,0:T(8,128)(2,1)}, bf16[560,128]{1,0:T(8,128)(2,1)S(1)}, u32[]{:S(2)}) copy-start(bf16[560,128]{1,0:T(8,128)(2,1)S(1)} %collective-permute-done.5.refs_10_) | copy-start | bytes 430084
  49.8 3.5 %collective-permute-start = (bf16[560,128]{1,0:T(8,128)(2,1)}, bf16[560,128]{1,0:T(8,128)(2,1)S(1)}, u32[]{:S(2)}, u32[]{:S(2)}) collective-permute-start(bf16[560,128]{1,0:T(8,128)(2,1)} %pack.1), channel_id=1, source_target_pairs={{0,8},{8,0},{16,24},{24,16},{32,40},{40,32},{48,56},{56,48},{64,72... | collective-permute-start | bytes 430088 | tf_op jit(solution)/shard_map/ppermute | solution.py:252
  51.7 1.5 %copy-start.2 = (bf16[560,128]{1,0:T(8,128)(2,1)}, bf16[560,128]{1,0:T(8,128)(2,1)S(1)}, u32[]{:S(2)}) copy-start(bf16[560,128]{1,0:T(8,128)(2,1)S(1)} %collective-permute-done.4.refs_9_) | copy-start | bytes 430084
  51.7 1.5 %copy-start.3 = (bf16[560,128]{1,0:T(8,128)(2,1)}, bf16[560,128]{1,0:T(8,128)(2,1)S(1)}, u32[]{:S(2)}) copy-start(bf16[560,128]{1,0:T(8,128)(2,1)S(1)} %collective-permute-done.3.refs_8_) | copy-start | bytes 430084
  51.8 1.5 %copy-start.4 = (bf16[560,128]{1,0:T(8,128)(2,1)}, bf16[560,128]{1,0:T(8,128)(2,1)S(1)}, u32[]{:S(2)}) copy-start(bf16[560,128]{1,0:T(8,128)(2,1)S(1)} %collective-permute-done.2.refs_7_) | copy-start | bytes 430084
  51.8 1.5 %copy-start.5 = (bf16[560,128]{1,0:T(8,128)(2,1)}, bf16[560,128]{1,0:T(8,128)(2,1)S(1)}, u32[]{:S(2)}) copy-start(bf16[560,128]{1,0:T(8,128)(2,1)S(1)} %collective-permute-done.1.refs_6_) | copy-start | bytes 430084
  53.3 0.7 copy-start.6
  56.4 12.4 %collective-permute-start.7 = (bf16[1056,128]{1,0:T(8,128)(2,1)}, bf16[1056,128]{1,0:T(8,128)(2,1)S(1)}, u32[]{:S(2)}, u32[]{:S(2)}) collective-permute-start(bf16[1056,128]{1,0:T(8,128)(2,1)} %get-tuple-element.5.refs_0_.block), channel_id=1, source_target_pairs={{0,1},{1,2},{2,3},{3,4},{4,5},{5,6},{6,7},{7,0},{8,9},{9,10},{10,1... | collective-permute-start | bytes 811016 | tf_op jit(solution)/shard_map/ppermute | solution.py:33
  59.9 10.8 %collective-permute-start.8 = (bf16[1056,128]{1,0:T(8,128)(2,1)}, bf16[1056,128]{1,0:T(8,128)(2,1)S(1)}, u32[]{:S(2)}, u32[]{:S(2)}) collective-permute-start(bf16[1056,128]{1,0:T(8,128)(2,1)} %get-tuple-element.5.refs_0_.block), channel_id=1, source_target_pairs={{0,7},{1,0},{2,1},{3,2},{4,3},{5,4},{6,5},{7,6},{8,15},{9,8},{10,9... | collective-permute-start | bytes 811016 | tf_op jit(solution)/shard_map/ppermute | solution.py:36
  68.7 30.8 %copy-start.7 = (bf16[1056,128]{1,0:T(8,128)(2,1)}, bf16[1056,128]{1,0:T(8,128)(2,1)S(1)}, u32[]{:S(2)}) copy-start(bf16[1056,128]{1,0:T(8,128)(2,1)S(1)} %collective-permute-done.7.refs_1_) | copy-start | bytes 811012
  68.7 11.0 %collective-permute-start.9 = (bf16[1056,128]{1,0:T(8,128)(2,1)S(1)}, bf16[1056,128]{1,0:T(8,128)(2,1)S(1)}, u32[]{:S(2)}, u32[]{:S(2)}) collective-permute-start(bf16[1056,128]{1,0:T(8,128)(2,1)S(1)} %collective-permute-done.7.refs_1_), channel_id=1, source_target_pairs={{0,1},{1,2},{2,3},{3,4},{4,5},{5,6},{6,7},{7,0},{8,9},{9,10},{10,1... | collective-permute-start | bytes 811016 | tf_op jit(solution)/shard_map/ppermute | solution.py:33
  70.7 28.9 %copy-start.8 = (bf16[1056,128]{1,0:T(8,128)(2,1)}, bf16[1056,128]{1,0:T(8,128)(2,1)S(1)}, u32[]{:S(2)}) copy-start(bf16[1056,128]{1,0:T(8,128)(2,1)S(1)} %collective-permute-done.8.refs_2_) | copy-start | bytes 811012
  70.7 11.0 %collective-permute-start.10 = (bf16[1056,128]{1,0:T(8,128)(2,1)S(1)}, bf16[1056,128]{1,0:T(8,128)(2,1)S(1)}, u32[]{:S(2)}, u32[]{:S(2)}) collective-permute-start(bf16[1056,128]{1,0:T(8,128)(2,1)S(1)} %collective-permute-done.8.refs_2_), channel_id=1, source_target_pairs={{0,7},{1,0},{2,1},{3,2},{4,3},{5,4},{6,5},{7,6},{8,15},{9,8},{10,9... | collective-permute-start | bytes 811016 | tf_op jit(solution)/shard_map/ppermute | solution.py:36
  79.8 19.8 %copy-start.9 = (bf16[1056,128]{1,0:T(8,128)(2,1)}, bf16[1056,128]{1,0:T(8,128)(2,1)S(1)}, u32[]{:S(2)}) copy-start(bf16[1056,128]{1,0:T(8,128)(2,1)S(1)} %collective-permute-done.9.refs_3_) | copy-start | bytes 811012
  79.8 10.2 %collective-permute-start.11 = (bf16[1056,128]{1,0:T(8,128)(2,1)S(1)}, bf16[1056,128]{1,0:T(8,128)(2,1)S(1)}, u32[]{:S(2)}, u32[]{:S(2)}) collective-permute-start(bf16[1056,128]{1,0:T(8,128)(2,1)S(1)} %collective-permute-done.9.refs_3_), channel_id=1, source_target_pairs={{0,1},{1,2},{2,3},{3,4},{4,5},{5,6},{6,7},{7,0},{8,9},{9,10},{10,1... | collective-permute-start | bytes 811016 | tf_op jit(solution)/shard_map/ppermute | solution.py:33
  81.7 17.8 %copy-start.10 = (bf16[1056,128]{1,0:T(8,128)(2,1)}, bf16[1056,128]{1,0:T(8,128)(2,1)S(1)}, u32[]{:S(2)}) copy-start(bf16[1056,128]{1,0:T(8,128)(2,1)S(1)} %collective-permute-done.10.refs_4_) | copy-start | bytes 811012
  81.7 10.2 %collective-permute-start.12 = (bf16[1056,128]{1,0:T(8,128)(2,1)S(1)}, bf16[1056,128]{1,0:T(8,128)(2,1)S(1)}, u32[]{:S(2)}, u32[]{:S(2)}) collective-permute-start(bf16[1056,128]{1,0:T(8,128)(2,1)S(1)} %collective-permute-done.10.refs_4_), channel_id=1, source_target_pairs={{0,7},{1,0},{2,1},{3,2},{4,3},{5,4},{6,5},{7,6},{8,15},{9,8},{10,9... | collective-permute-start | bytes 811016 | tf_op jit(solution)/shard_map/ppermute | solution.py:36
  90.0 9.6 %copy-start.11 = (bf16[1056,128]{1,0:T(8,128)(2,1)}, bf16[1056,128]{1,0:T(8,128)(2,1)S(1)}, u32[]{:S(2)}) copy-start(bf16[1056,128]{1,0:T(8,128)(2,1)S(1)} %collective-permute-done.11.refs_5_) | copy-start | bytes 811012
  90.0 9.6 %collective-permute-start.13 = (bf16[1056,128]{1,0:T(8,128)(2,1)S(1)}, bf16[1056,128]{1,0:T(8,128)(2,1)S(1)}, u32[]{:S(2)}, u32[]{:S(2)}) collective-permute-start(bf16[1056,128]{1,0:T(8,128)(2,1)S(1)} %collective-permute-done.11.refs_5_), channel_id=1, source_target_pairs={{0,1},{1,2},{2,3},{3,4},{4,5},{5,6},{6,7},{7,0},{8,9},{9,10},{10,1... | collective-permute-start | bytes 811016 | tf_op jit(solution)/shard_map/ppermute | solution.py:33
  91.9 7.7 %copy-start.12 = (bf16[1056,128]{1,0:T(8,128)(2,1)}, bf16[1056,128]{1,0:T(8,128)(2,1)S(1)}, u32[]{:S(2)}) copy-start(bf16[1056,128]{1,0:T(8,128)(2,1)S(1)} %collective-permute-done.12.refs_6_) | copy-start | bytes 811012
  99.5 0.7 copy-start.13

commit v3 on v2

v3 whole, which is shorter than its diff:
```python
import jax
import jax.numpy as jnp
from jax import lax
from jax.experimental import pallas as pl
from jax.experimental.pallas import tpu as pltpu
from jax.sharding import PartitionSpec as P


ROWS_DEV = 64
LIVE = 4
MOVE = 2
STEP_ROOT = 0.1
N_CHOL = 8
OFFSETS = (0, -1, 1, -2, 2, -3, 3, -4)
TILE = 16
ORBS = 256
STRIDE = ORBS + TILE
RING_ROWS = 2 * STRIDE
FIELD_ROW = MOVE * STRIDE

ANY = pl.BlockSpec(memory_space=pl.ANY)
HBM = pl.BlockSpec(memory_space=pltpu.HBM)
WHOLE = pl.BlockSpec(memory_space=pltpu.VMEM)
SCALARS = pl.BlockSpec(memory_space=pltpu.SMEM)
F32 = jnp.float32
BF16 = jnp.bfloat16


def params(megabytes):
    return pltpu.CompilerParams(vmem_limit_bytes=megabytes << 20)


def after(value, *others):
    return lax.optimization_barrier((value, *others))[0]


def ring(block, gate=None):
    up = [(i, (i + 1) % N_CHOL) for i in range(N_CHOL)]
    down = [(i, (i - 1) % N_CHOL) for i in range(N_CHOL)]
    parts, low, high = [block], block, block
    for step in range(N_CHOL // 2):
        if step == 1 and gate is not None:
            low, high = after(low, gate), after(high, gate)
        low = lax.ppermute(low, "chol", up)
        parts.append(low)
        if step < N_CHOL // 2 - 1:
            high = lax.ppermute(high, "chol", down)
            parts.append(high)
    return parts


def inv_rows(inv, slot):
    share = pl.multiple_of(lax.axis_index("chol") * TILE, TILE)
    return inv.at[slot, pl.ds(share, TILE)]


def pack_kernel(counts, partner, walkers, inv, fields, out, early, kept, plan, sems):
    copies = []

    def add(source, target, first, size):
        copies.append(
            pltpu.make_async_copy(source, target.at[pl.ds(first, size)], sems.at[len(copies)])
        )

    for j in range(MOVE):
        add(walkers.at[LIVE + j], out, j * STRIDE, ORBS)
        add(inv_rows(inv, LIVE + j), out, j * STRIDE + ORBS, TILE)
    for j in range(MOVE):
        add(walkers.at[j], early, j * ORBS, ORBS)
        add(walkers.at[2 + j], kept, j * STRIDE, ORBS)
        add(inv_rows(inv, 2 + j), kept, j * STRIDE + ORBS, TILE)
    for copy in copies:
        copy.start()
    out[FIELD_ROW:] = jnp.zeros((TILE, out.shape[1]), BF16)
    out[FIELD_ROW : FIELD_ROW + fields.shape[0], : fields.shape[1]] = fields[...]
    walk = lax.axis_index("walk")
    mate = partner[walk]
    row_id = lax.broadcasted_iota(jnp.int32, plan.shape, 0)
    arriving = jnp.maximum(counts[mate] - LIVE, 0)
    rest = jnp.where(row_id == 1, counts[walk], arriving)
    plan[...] = jnp.where(row_id == 0, jnp.bitwise_xor(mate, walk), rest)
    for copy in copies:
        copy.wait()


def pack_call(counts, partner, walkers, inv, fields):
    lanes = walkers.shape[2]
    return pl.pallas_call(
        pack_kernel,
        in_specs=[SCALARS, SCALARS, HBM, HBM, WHOLE],
        out_specs=(WHOLE,) * 4,
        out_shape=(
            jax.ShapeDtypeStruct((FIELD_ROW + TILE, lanes), BF16),
            jax.ShapeDtypeStruct((2 * ORBS, lanes), BF16),
            jax.ShapeDtypeStruct((RING_ROWS, lanes), BF16),
            jax.ShapeDtypeStruct((8, lanes), jnp.int32),
        ),
        scratch_shapes=[pltpu.SemaphoreType.DMA((5 * MOVE,))],
        name="pack",
    )(counts, partner, walkers, inv, fields)


def merge_kernel(bits, plan, outgoing, kept, *refs):
    received, (out, x) = refs[:bits], refs[bits:]
    distance, own = plan[0:1], plan[1:2]

    def sent(rows, width):
        block = jnp.zeros((rows.stop - rows.start, width), F32)
        for bit in range(bits):
            here = distance[:, :width] == 1 << bit
            block = jnp.where(here, received[bit][rows, :width].astype(F32), block)
        return block

    lanes = out.shape[1]
    for q in range(2):
        for first in range(0, STRIDE, TILE):
            mine = kept[q * STRIDE + first : q * STRIDE + first + TILE].astype(F32)
            start = (1 - q) * STRIDE + first
            theirs = sent(slice(start, start + TILE), lanes)
            rows = slice(q * STRIDE + first, q * STRIDE + first + TILE)
            out[rows] = jnp.where(own > 2 + q, mine, theirs).astype(BF16)
    rows = slice(FIELD_ROW, FIELD_ROW + TILE)
    mine, theirs = outgoing[rows].astype(F32), sent(rows, lanes)
    for q in range(2):
        mask = own[:, q : q + 1] > 2 + q
        column = jnp.where(mask, mine[:, 2 + q : 3 + q], theirs[:, LIVE + 1 - q : LIVE + 2 - q])
        x[:, q : q + 1] = column


def merge_call(plan, outgoing, kept, received):
    bits, lanes = len(received), kept.shape[1]

    def body(*refs):
        merge_kernel(bits, *refs)

    return pl.pallas_call(
        body,
        in_specs=[WHOLE] * (3 + bits),
        out_specs=(WHOLE, WHOLE),
        out_shape=(
            jax.ShapeDtypeStruct((RING_ROWS, lanes), BF16),
            jax.ShapeDtypeStruct((TILE, lanes), F32),
        ),
        compiler_params=params(4),
        name="merge",
    )(plan, outgoing, kept, *received)


def product_kernel(late, x, chol, trial, extra, *refs):
    parts, out, minv = refs[:N_CHOL], refs[N_CHOL], refs[N_CHOL + 1]
    lanes = out.shape[2]
    stride, base = (STRIDE, 2) if late else (ORBS, 0)
    me = lax.axis_index("chol")
    owners = [jnp.bitwise_and(me + offset, N_CHOL - 1) for offset in OFFSETS]
    columns = [pl.ds(pl.multiple_of(owner * ORBS, ORBS), ORBS) for owner in owners]
    row_id = lax.broadcasted_iota(jnp.int32, (TILE, lanes), 0)
    lane_id = lax.broadcasted_iota(jnp.int32, (TILE, lanes), 1)
    logs = jnp.zeros((TILE, lanes), F32)
    if late:
        logs = extra[0, base * ROWS_DEV :].astype(F32)
        out[:, : base * ROWS_DEV] = extra[:, : base * ROWS_DEV]
        for owner, part in zip(owners, parts):
            share = pl.ds(pl.multiple_of(owner * TILE, TILE), TILE)
            for q in range(2):
                minv[q, share] = part[q * stride + ORBS : (q + 1) * stride]
    phi = jnp.concatenate(
        [
            jnp.concatenate([part[q * stride : q * stride + ORBS] for q in range(2)], axis=1)
            for part in parts
        ],
        axis=0,
    )
    products = []
    for g in range(chol.shape[0]):
        rows = jnp.concatenate([chol[g, :, spot] for spot in columns], axis=1)
        products.append(jnp.dot(rows, phi, preferred_element_type=F32))
    for q in range(2):
        weighted = lax.dot_general(
            trial[...],
            minv[q] if late else extra[q],
            (((1,), (1,)), ((), ())),
            preferred_element_type=F32,
        )
        total = jnp.zeros_like(weighted)
        log = jnp.zeros((1, 1), F32)
        for g, both in enumerate(products):
            product = both[:, q * lanes : (q + 1) * lanes]
            bias = -STEP_ROOT * jnp.sum(product * weighted, keepdims=True)
            field = x[g : g + 1, q : q + 1].astype(F32)
            total += STEP_ROOT * (field - bias) * product
            log += field * bias - 0.5 * bias * bias
        spread = total.astype(BF16).reshape(N_CHOL, ROWS_DEV, lanes)
        slot = base + q
        out[:, slot * ROWS_DEV : (slot + 1) * ROWS_DEV] = spread
        high = log.astype(BF16).astype(F32)
        here = row_id == slot
        logs = jnp.where(here & (lane_id == 0), high, logs)
        logs = jnp.where(here & (lane_id == 1), log - high, logs)
    for k in range(N_CHOL):
        out[k, (base + 2) * ROWS_DEV :] = logs.astype(BF16)


def product_call(late, x, cholesky, trial, extra, parts):
    lanes = trial.shape[1]
    vectors, window, orbitals = cholesky.shape
    flops = 4 * vectors * window * orbitals * lanes
    out_rows = (LIVE if late else 2) * ROWS_DEV + TILE

    def body(*refs):
        product_kernel(late, *refs)

    return pl.pallas_call(
        body,
        in_specs=[WHOLE] * (4 + N_CHOL),
        out_specs=WHOLE,
        out_shape=jax.ShapeDtypeStruct((N_CHOL, out_rows, lanes), BF16),
        scratch_shapes=[pltpu.VMEM((2, lanes, lanes), BF16)],
        compiler_params=params(24),
        name="late_products" if late else "early_products",
        cost_estimate=pl.CostEstimate(flops=flops, bytes_accessed=6 << 20, transcendentals=0),
    )(x, cholesky, trial, extra, *parts)


def finish_kernel(plan, got, early, late, out, log_out):
    own, arriving = plan[1:2], plan[2:3]
    tile = jnp.zeros((TILE, got.shape[2]), F32)
    for k in range(N_CHOL):
        tile += got[k, LIVE * ROWS_DEV :].astype(F32)
    walkers, logs = [], []
    for spot in range(LIVE):
        block, first = (early, spot * ORBS) if spot < 2 else (late, (spot - 2) * STRIDE)
        total = block[first : first + ROWS_DEV].astype(F32)
        for k in range(N_CHOL):
            total += got[k, spot * ROWS_DEV : (spot + 1) * ROWS_DEV].astype(F32)
        walkers.append(total)
        logs.append(tile[spot : spot + 1])
    for slot in range(LIVE):
        for values, store in ((walkers, True), (logs, False)):
            value = jnp.zeros_like(values[slot])
            for j in range(MOVE):
                moved = (own == slot - j) & (arriving > j)
                value = jnp.where(moved, values[LIVE - 1 - j], value)
            value = jnp.where(own > slot, values[slot], value)
            if store:
                out[slot] = value.astype(BF16)
            else:
                log_out[slot] = jnp.sum(value)


def finish_call(plan, got, early, late):
    lanes = got.shape[2]
    return pl.pallas_call(
        finish_kernel,
        in_specs=[WHOLE] * 4,
        out_specs=(WHOLE, SCALARS),
        out_shape=(
            jax.ShapeDtypeStruct((LIVE, ROWS_DEV, lanes), BF16),
            jax.ShapeDtypeStruct((LIVE,), F32),
        ),
        compiler_params=params(8),
        name="finish",
    )(plan, got, early, late)


def shards(walkers, inv_intersection, fields, cholesky, trial_rows, counts, partner):
    walk_size = lax.axis_size("walk")
    fields = fields.T
    outgoing, early, kept, plan = pack_call(
        counts, partner, walkers, inv_intersection, fields
    )
    received = []
    for bit in range(walk_size.bit_length() - 1):
        route = [(i, i ^ 1 << bit) for i in range(walk_size)]
        received.append(lax.ppermute(outgoing, "walk", route))
    early_parts = ring(early)
    late, x = merge_call(plan, outgoing, kept, received)
    first = product_call(
        False, fields, cholesky, trial_rows, inv_intersection, early_parts
    )
    late_parts = ring(late, first)
    sums = product_call(True, x, cholesky, trial_rows, first, late_parts)
    sums = lax.all_to_all(sums, "chol", 0, 0, tiled=True)
    return tuple(finish_call(plan, sums, early, late))


def solution(mesh):
    in_specs = (
        P("walk", "chol", None),
        P("walk", None, None),
        P("walk", "chol"),
        P("chol", None, None),
        P(),
        P(),
        P(),
    )
    out_specs = (P("walk", "chol", None), P("walk"))
    return jax.shard_map(shards, mesh=mesh, in_specs=in_specs, out_specs=out_specs, check_vma=False)
```

time: 131 us -> 137 us (1.046)
  starting transfers between devices: 65.7 us -> 87.8 us
  waiting for transfers between devices: 26.2 us -> 11.7 us
  Pallas kernels: 13.5 us -> 7.31 us
  local copies, waits for them, and re-layouts: 2.71 us -> 8.07 us
    ppermute x3 -> x6, starting transfers between devices: 14.1 us -> 28.3 us  [ring(): high = lax.ppermute(high, 'chol', down)]
    ppermute x4 -> x8, waiting for transfers between devices: 19.7 us -> 8.57 us  [ring(): low = lax.ppermute(low, 'chol', up)]
    ppermute x4 -> x8, starting transfers between devices: 9.21 us -> 17.1 us  [ring(): low = lax.ppermute(low, 'chol', up)]
    pallas_call x4 -> x5, Pallas kernels: 13.5 us -> 7.31 us  [the longest x2 3.75 us: product_call(): pl.pallas_call(body, in_specs=[WHOLE] * (4 + N_CHOL), out_specs=WHOLE, ou...]
    unnamed x29 -> x18, local copies, waits for them, and re-layouts: 2.71 us -> 8.07 us
    ppermute x7, waiting for transfers between devices: 6.47 us -> 3.08 us  [shards(): received.append(lax.ppermute(outgoing, 'walk', route))]
  transfers between devices with their start and end apart: 14 -> 21, of which waited for: 6 -> 4; matrix products, arithmetic and copies ran while one was open for 0% -> 0% of each run, Pallas kernels for 0% -> 2%
where the time goes in v3:
time: 137 us; the launch traced here: 136 us
  starting transfers between devices  87.8 us (64%)
  blocking collectives  20.2 us (15%)
  waiting for transfers between devices  11.7 us (9%)
  local copies, waits for them, and re-layouts  8.07 us (6%)
  Pallas kernels  7.31 us (5%)
    ppermute x7, starting transfers between devices, shards(): received.append(lax.ppermute(outgoing, 'walk', route))  42.4 us
    ppermute x6, starting transfers between devices, ring(): high = lax.ppermute(high, 'chol', down)  28.3 us
    all_to_all x1, blocking collectives, shards(): sums = lax.all_to_all(sums, 'chol', 0, 0, tiled=True)  20.2 us
    ppermute x8, starting transfers between devices, ring(): low = lax.ppermute(low, 'chol', up)  17.1 us
    ppermute x8, waiting for transfers between devices, ring(): low = lax.ppermute(low, 'chol', up)  8.57 us
    unnamed x18, local copies, waits for them, and re-layouts  8.07 us
    pallas_call x2, Pallas kernels, product_call(): pl.pallas_call(body, in_specs=[WHOLE] * (4 + N_CHOL), out_specs=WHOLE, ou...  3.75 us
    ppermute x7, waiting for transfers between devices, shards(): received.append(lax.ppermute(outgoing, 'walk', route))  3.08 us
  transfers between devices with their start and end apart: 21, of which 4 were waited for; matrix products, arithmetic and copies ran while one was open for 0% of the time, Pallas kernels for 2%

profile of v3, /device:TPU:2, one launch (start us, length us, event | category | flops | bytes accessed | tf_op | source)
XLA Modules:
  0.0 136.0 jit_solution(2463564925231654141)
XLA Ops:
  0.6 2.6 %pack.1 = (bf16[560,128]{1,0:T(8,128)(2,1)}, bf16[512,128]{1,0:T(8,128)(2,1)}, bf16[544,128]{1,0:T(8,128)(2,1)}, s32[8,128]{1,0:T(8,128)}) custom-call(s32[128]{0:T(128)} %counts.1, s32[128]{0:T(128)} %partner.1, bf16[6,256,128]{2,1,0:T(8,128)(2,1)} %walkers.1, bf16[6,128,128]{2,1,0:T(8,128)(2,1)} %refs_3_.1, bf16[2,6]{1,0:T(2,128)(2,1)} %bitcast.1), custom_call_target="tpu_custom_call" | custom-call | tf_op jit(solution)/shard_map/pack/pallas_call | solution.py:88
  3.2 3.5 %collective-permute-start.7 = (bf16[512,128]{1,0:T(8,128)(2,1)}, bf16[512,128]{1,0:T(8,128)(2,1)S(1)}, u32[]{:S(2)}, u32[]{:S(2)}) collective-permute-start(bf16[512,128]{1,0:T(8,128)(2,1)} %get-tuple-element.14.refs_4_.early), channel_id=1, source_target_pairs={{0,1},{1,2},{2,3},{3,4},{4,5},{5,6},{6,7},{7,0},{8,9},{9,10},{10,1... | collective-permute-start | bytes 393224 | tf_op jit(solution)/shard_map/ppermute | solution.py:44
  6.7 3.8 %collective-permute-start.8 = (bf16[512,128]{1,0:T(8,128)(2,1)}, bf16[512,128]{1,0:T(8,128)(2,1)S(1)}, u32[]{:S(2)}, u32[]{:S(2)}) collective-permute-start(bf16[512,128]{1,0:T(8,128)(2,1)} %get-tuple-element.14.refs_4_.early), channel_id=1, source_target_pairs={{0,7},{1,0},{2,1},{3,2},{4,3},{5,4},{6,5},{7,6},{8,15},{9,8},{10,9... | collective-permute-start | bytes 393224 | tf_op jit(solution)/shard_map/ppermute | solution.py:47
  10.5 19.4 %collective-permute-start.6 = (bf16[560,128]{1,0:T(8,128)(2,1)}, bf16[560,128]{1,0:T(8,128)(2,1)S(1)}, u32[]{:S(2)}, u32[]{:S(2)}) collective-permute-start(bf16[560,128]{1,0:T(8,128)(2,1)} %get-tuple-element.11.refs_1_), channel_id=1, source_target_pairs={{0,512},{8,520},{16,528},{24,536},{32,544},{40,552},{48,560},{56,5... | collective-permute-start | bytes 430088 | tf_op jit(solution)/shard_map/ppermute | solution.py:274
  29.9 0.0 collective-permute-done.7.refs_5_
  29.9 2.0 %collective-permute-start.9 = (bf16[512,128]{1,0:T(8,128)(2,1)S(1)}, bf16[512,128]{1,0:T(8,128)(2,1)S(1)}, u32[]{:S(2)}, u32[]{:S(2)}) collective-permute-start(bf16[512,128]{1,0:T(8,128)(2,1)S(1)} %collective-permute-done.7.refs_5_), channel_id=1, source_target_pairs={{0,1},{1,2},{2,3},{3,4},{4,5},{5,6},{6,7},{7,0},{8,9},{9,10},{10,1... | collective-permute-start | bytes 393224 | tf_op jit(solution)/shard_map/ppermute | solution.py:44
  31.9 6.1 %collective-permute-start.5 = (bf16[560,128]{1,0:T(8,128)(2,1)}, bf16[560,128]{1,0:T(8,128)(2,1)S(1)}, u32[]{:S(2)}, u32[]{:S(2)}) collective-permute-start(bf16[560,128]{1,0:T(8,128)(2,1)} %get-tuple-element.11.refs_1_), channel_id=1, source_target_pairs={{0,256},{8,264},{16,272},{24,280},{32,288},{40,296},{48,304},{56,3... | collective-permute-start | bytes 430088 | tf_op jit(solution)/shard_map/ppermute | solution.py:274
  38.1 4.3 %collective-permute-start.4 = (bf16[560,128]{1,0:T(8,128)(2,1)}, bf16[560,128]{1,0:T(8,128)(2,1)S(1)}, u32[]{:S(2)}, u32[]{:S(2)}) collective-permute-start(bf16[560,128]{1,0:T(8,128)(2,1)} %get-tuple-element.11.refs_1_), channel_id=1, source_target_pairs={{0,128},{8,136},{16,144},{24,152},{32,160},{40,168},{48,176},{56,1... | collective-permute-start | bytes 430088 | tf_op jit(solution)/shard_map/ppermute | solution.py:274
  42.4 0.0 collective-permute-done.8.refs_6_
  42.4 3.4 %collective-permute-start.3 = (bf16[560,128]{1,0:T(8,128)(2,1)}, bf16[560,128]{1,0:T(8,128)(2,1)S(1)}, u32[]{:S(2)}, u32[]{:S(2)}) collective-permute-start(bf16[560,128]{1,0:T(8,128)(2,1)} %get-tuple-element.11.refs_1_), channel_id=1, source_target_pairs={{0,64},{8,72},{16,80},{24,88},{32,96},{40,104},{48,112},{56,120},{... | collective-permute-start | bytes 430088 | tf_op jit(solution)/shard_map/ppermute | solution.py:274
  45.8 0.0 collective-permute-done.6.refs_9_
  45.8 5.0 %collective-permute-start.10 = (bf16[512,128]{1,0:T(8,128)(2,1)S(1)}, bf16[512,128]{1,0:T(8,128)(2,1)S(1)}, u32[]{:S(2)}, u32[]{:S(2)}) collective-permute-start(bf16[512,128]{1,0:T(8,128)(2,1)S(1)} %collective-permute-done.8.refs_6_), channel_id=1, source_target_pairs={{0,7},{1,0},{2,1},{3,2},{4,3},{5,4},{6,5},{7,6},{8,15},{9,8},{10,9... | collective-permute-start | bytes 393224 | tf_op jit(solution)/shard_map/ppermute | solution.py:47
  50.8 0.0 collective-permute-done.9.refs_7_
  50.8 1.9 %collective-permute-start.11 = (bf16[512,128]{1,0:T(8,128)(2,1)S(1)}, bf16[512,128]{1,0:T(8,128)(2,1)S(1)}, u32[]{:S(2)}, u32[]{:S(2)}) collective-permute-start(bf16[512,128]{1,0:T(8,128)(2,1)S(1)} %collective-permute-done.9.refs_7_), channel_id=1, source_target_pairs={{0,1},{1,2},{2,3},{3,4},{4,5},{5,6},{6,7},{7,0},{8,9},{9,10},{10,1... | collective-permute-start | bytes 393224 | tf_op jit(solution)/shard_map/ppermute | solution.py:44
  52.7 3.1 %collective-permute-done.5.refs_8_ = bf16[560,128]{1,0:T(8,128)(2,1)S(1)} collective-permute-done((bf16[560,128]{1,0:T(8,128)(2,1)}, bf16[560,128]{1,0:T(8,128)(2,1)S(1)}, u32[]{:S(2)}, u32[]{:S(2)}) %collective-permute-start.5) | collective-permute-done | bytes 143392 | tf_op jit(solution)/shard_map/ppermute | solution.py:274
  55.8 4.0 %collective-permute-start.2 = (bf16[560,128]{1,0:T(8,128)(2,1)}, bf16[560,128]{1,0:T(8,128)(2,1)S(1)}, u32[]{:S(2)}, u32[]{:S(2)}) collective-permute-start(bf16[560,128]{1,0:T(8,128)(2,1)} %get-tuple-element.11.refs_1_), channel_id=1, source_target_pairs={{0,32},{8,40},{16,48},{24,56},{32,0},{40,8},{48,16},{56,24},{64,96... | collective-permute-start | bytes 430088 | tf_op jit(solution)/shard_map/ppermute | solution.py:274
  59.8 0.0 collective-permute-done.4.refs_7_
  59.8 3.3 %collective-permute-start.1 = (bf16[560,128]{1,0:T(8,128)(2,1)}, bf16[560,128]{1,0:T(8,128)(2,1)S(1)}, u32[]{:S(2)}, u32[]{:S(2)}) collective-permute-start(bf16[560,128]{1,0:T(8,128)(2,1)} %get-tuple-element.11.refs_1_), channel_id=1, source_target_pairs={{0,16},{8,24},{16,0},{24,8},{32,48},{40,56},{48,32},{56,40},{64,80... | collective-permute-start | bytes 430088 | tf_op jit(solution)/shard_map/ppermute | solution.py:274
  63.2 0.0 collective-permute-done.3.refs_6_
  63.2 1.9 %collective-permute-start = (bf16[560,128]{1,0:T(8,128)(2,1)}, bf16[560,128]{1,0:T(8,128)(2,1)S(1)}, u32[]{:S(2)}, u32[]{:S(2)}) collective-permute-start(bf16[560,128]{1,0:T(8,128)(2,1)} %get-tuple-element.11.refs_1_), channel_id=1, source_target_pairs={{0,8},{8,0},{16,24},{24,16},{32,40},{40,32},{48,56},{56,48},{64,72... | collective-permute-start | bytes 430088 | tf_op jit(solution)/shard_map/ppermute | solution.py:274
  65.1 0.0 collective-permute-done.10.refs_8_
  65.1 4.1 %collective-permute-start.12 = (bf16[512,128]{1,0:T(8,128)(2,1)S(1)}, bf16[512,128]{1,0:T(8,128)(2,1)S(1)}, u32[]{:S(2)}, u32[]{:S(2)}) collective-permute-start(bf16[512,128]{1,0:T(8,128)(2,1)S(1)} %collective-permute-done.10.refs_8_), channel_id=1, source_target_pairs={{0,7},{1,0},{2,1},{3,2},{4,3},{5,4},{6,5},{7,6},{8,15},{9,8},{10,9... | collective-permute-start | bytes 393224 | tf_op jit(solution)/shard_map/ppermute | solution.py:47
  69.3 0.0 collective-permute-done.11.refs_9_
  69.3 1.9 %collective-permute-start.13 = (bf16[512,128]{1,0:T(8,128)(2,1)S(1)}, bf16[512,128]{1,0:T(8,128)(2,1)S(1)}, u32[]{:S(2)}, u32[]{:S(2)}) collective-permute-start(bf16[512,128]{1,0:T(8,128)(2,1)S(1)} %collective-permute-done.11.refs_9_), channel_id=1, source_target_pairs={{0,1},{1,2},{2,3},{3,4},{4,5},{5,6},{6,7},{7,0},{8,9},{9,10},{10,1... | collective-permute-start | bytes 393224 | tf_op jit(solution)/shard_map/ppermute | solution.py:44
  71.3 0.9 copy-done.5
  72.2 0.9 copy-done.6
  73.1 0.7 copy-done.7
  73.8 0.2 merge.1
  74.0 2.0 %collective-permute-start.14 = (bf16[544,128]{1,0:T(8,128)(2,1)S(1)}, bf16[544,128]{1,0:T(8,128)(2,1)S(1)}, u32[]{:S(2)}, u32[]{:S(2)}) collective-permute-start(bf16[544,128]{1,0:T(8,128)(2,1)S(1)} %get-tuple-element.15.refs_4_.late), channel_id=1, source_target_pairs={{0,1},{1,2},{2,3},{3,4},{4,5},{5,6},{6,7},{7,0},{8,9},{9,10},{10,1... | collective-permute-start | bytes 417800 | tf_op jit(solution)/shard_map/ppermute | solution.py:44
  76.0 5.0 %collective-permute-start.15 = (bf16[544,128]{1,0:T(8,128)(2,1)S(1)}, bf16[544,128]{1,0:T(8,128)(2,1)S(1)}, u32[]{:S(2)}, u32[]{:S(2)}) collective-permute-start(bf16[544,128]{1,0:T(8,128)(2,1)S(1)} %get-tuple-element.15.refs_4_.late), channel_id=1, source_target_pairs={{0,7},{1,0},{2,1},{3,2},{4,3},{5,4},{6,5},{7,6},{8,15},{9,8},{10,9... | collective-permute-start | bytes 417800 | tf_op jit(solution)/shard_map/ppermute | solution.py:47
  81.1 0.0 copy-start
  81.1 2.2 %copy-done = bf16[2,512,2048]{2,1,0:T(8,128)(2,1)S(1)} copy-done((bf16[2,512,2048]{2,1,0:T(8,128)(2,1)S(1)}, bf16[2,512,2048]{2,1,0:T(8,128)(2,1)}, u32[]{:S(2)}) %copy-start) | copy-done | bytes 4194328
  83.3 0.9 copy-done.2
  84.2 0.9 copy-done.3
  85.1 0.9 copy-done.4
  86.0 0.7 copy-done.8
  86.7 1.9 %early_products.1.refs_3_ = bf16[8,144,128]{2,1,0:T(8,128)(2,1)S(1)} custom-call(bf16[2,6]{1,0:T(2,128)(2,1)S(1)} %bitcast.2, bf16[2,512,2048]{2,1,0:T(8,128)(2,1)S(1)} %copy-done, bf16[512,128]{1,0:T(8,128)(2,1)S(1)} %copy-done.3, bf16[6,128,128]{2,1,0:T(8,128)(2,1)S(1)} %copy-done.2, bf16[512,128]{1,0:T(8,128)(2,1)S(1)} %copy-done.4, ...), custom_call_target="tpu_custom_call" | custom-call | flops 1073741824 | bytes 6291456 | tf_op jit(solution)/shard_map/early_products/pallas_call | solution.py:212
  88.6 1.9 %collective-permute-start.16 = (bf16[544,128]{1,0:T(8,128)(2,1)S(1)}, bf16[544,128]{1,0:T(8,128)(2,1)S(1)}, u32[]{:S(2)}, u32[]{:S(2)}) collective-permute-start(bf16[544,128]{1,0:T(8,128)(2,1)S(1)} %collective-permute-done.14.refs_5_), channel_id=1, source_target_pairs={{0,1},{1,2},{2,3},{3,4},{4,5},{5,6},{6,7},{7,0},{8,9},{9,10},{10,1... | collective-permute-start | bytes 417800 | tf_op jit(solution)/shard_map/ppermute | solution.py:44
  90.5 5.1 %collective-permute-start.17 = (bf16[544,128]{1,0:T(8,128)(2,1)S(1)}, bf16[544,128]{1,0:T(8,128)(2,1)S(1)}, u32[]{:S(2)}, u32[]{:S(2)}) collective-permute-start(bf16[544,128]{1,0:T(8,128)(2,1)S(1)} %collective-permute-done.15.refs_6_), channel_id=1, source_target_pairs={{0,7},{1,0},{2,1},{3,2},{4,3},{5,4},{6,5},{7,6},{8,15},{9,8},{10,9... | collective-permute-start | bytes 417800 | tf_op jit(solution)/shard_map/ppermute | solution.py:47
  95.6 1.3 collective-permute-done.16.refs_7_
  96.9 1.9 %collective-permute-start.18 = (bf16[544,128]{1,0:T(8,128)(2,1)S(1)}, bf16[544,128]{1,0:T(8,128)(2,1)S(1)}, u32[]{:S(2)}, u32[]{:S(2)}) collective-permute-start(bf16[544,128]{1,0:T(8,128)(2,1)S(1)} %collective-permute-done.16.refs_7_), channel_id=1, source_target_pairs={{0,1},{1,2},{2,3},{3,4},{4,5},{5,6},{6,7},{7,0},{8,9},{9,10},{10,1... | collective-permute-start | bytes 417800 | tf_op jit(solution)/shard_map/ppermute | solution.py:44
  98.8 5.1 %collective-permute-start.19 = (bf16[544,128]{1,0:T(8,128)(2,1)S(1)}, bf16[544,128]{1,0:T(8,128)(2,1)S(1)}, u32[]{:S(2)}, u32[]{:S(2)}) collective-permute-start(bf16[544,128]{1,0:T(8,128)(2,1)S(1)} %collective-permute-done.17.refs_8_), channel_id=1, source_target_pairs={{0,7},{1,0},{2,1},{3,2},{4,3},{5,4},{6,5},{7,6},{8,15},{9,8},{10,9... | collective-permute-start | bytes 417800 | tf_op jit(solution)/shard_map/ppermute | solution.py:47
  104.0 1.1 collective-permute-done.18.refs_9_
  105.1 1.9 %collective-permute-start.20 = (bf16[544,128]{1,0:T(8,128)(2,1)S(1)}, bf16[544,128]{1,0:T(8,128)(2,1)S(1)}, u32[]{:S(2)}, u32[]{:S(2)}) collective-permute-start(bf16[544,128]{1,0:T(8,128)(2,1)S(1)} %collective-permute-done.18.refs_9_), channel_id=1, source_target_pairs={{0,1},{1,2},{2,3},{3,4},{4,5},{5,6},{6,7},{7,0},{8,9},{9,10},{10,1... | collective-permute-start | bytes 417800 | tf_op jit(solution)/shard_map/ppermute | solution.py:44
  107.0 6.2 %collective-permute-done.20.refs_11_ = bf16[544,128]{1,0:T(8,128)(2,1)S(1)} collective-permute-done((bf16[544,128]{1,0:T(8,128)(2,1)S(1)}, bf16[544,128]{1,0:T(8,128)(2,1)S(1)}, u32[]{:S(2)}, u32[]{:S(2)}) %collective-permute-start.20) | collective-permute-done | bytes 139296 | tf_op jit(solution)/shard_map/ppermute | solution.py:44
  113.2 1.9 %late_products.1 = bf16[8,272,128]{2,1,0:T(8,128)(2,1)S(1)} custom-call(f32[16,128]{1,0:T(8,128)S(1)} %get-tuple-element.13.refs_0_, bf16[2,512,2048]{2,1,0:T(8,128)(2,1)S(1)} %copy-done.1, bf16[512,128]{1,0:T(8,128)(2,1)S(1)} %copy-done.3, bf16[8,144,128]{2,1,0:T(8,128)(2,1)S(1)} %early_products.1.refs_3_, ...), custom_call_target="tpu_custom_call" | custom-call | flops 1073741824 | bytes 6291456 | tf_op jit(solution)/shard_map/late_products/pallas_call | solution.py:212
  115.1 20.2 %all_to_all.5.got = bf16[8,272,128]{2,1,0:T(8,128)(2,1)S(1)} all-to-all(bf16[8,272,128]{2,1,0:T(8,128)(2,1)S(1)} %late_products.1), channel_id=1, replica_groups=mesh['walk'=128,'chol'=8] {'chol'}, dimensions={0} | all-to-all | bytes 1114112 | tf_op jit(solution)/shard_map/all_to_all | solution.py:282
  135.3 0.7 finish.1
  (18 shorter events, 0.0 us)
Async XLA Ops:
  3.2 26.7 %collective-permute-start.7 = (bf16[512,128]{1,0:T(8,128)(2,1)}, bf16[512,128]{1,0:T(8,128)(2,1)S(1)}, u32[]{:S(2)}, u32[]{:S(2)}) collective-permute-start(bf16[512,128]{1,0:T(8,128)(2,1)} %get-tuple-element.14.refs_4_.early), channel_id=1, source_target_pairs={{0,1},{1,2},{2,3},{3,4},{4,5},{5,6},{6,7},{7,0},{8,9},{9,10},{10,1... | collective-permute-start | bytes 393224 | tf_op jit(solution)/shard_map/ppermute | solution.py:44
  6.7 35.7 %collective-permute-start.8 = (bf16[512,128]{1,0:T(8,128)(2,1)}, bf16[512,128]{1,0:T(8,128)(2,1)S(1)}, u32[]{:S(2)}, u32[]{:S(2)}) collective-permute-start(bf16[512,128]{1,0:T(8,128)(2,1)} %get-tuple-element.14.refs_4_.early), channel_id=1, source_target_pairs={{0,7},{1,0},{2,1},{3,2},{4,3},{5,4},{6,5},{7,6},{8,15},{9,8},{10,9... | collective-permute-start | bytes 393224 | tf_op jit(solution)/shard_map/ppermute | solution.py:47
  10.5 35.2 %collective-permute-start.6 = (bf16[560,128]{1,0:T(8,128)(2,1)}, bf16[560,128]{1,0:T(8,128)(2,1)S(1)}, u32[]{:S(2)}, u32[]{:S(2)}) collective-permute-start(bf16[560,128]{1,0:T(8,128)(2,1)} %get-tuple-element.11.refs_1_), channel_id=1, source_target_pairs={{0,512},{8,520},{16,528},{24,536},{32,544},{40,552},{48,560},{56,5... | collective-permute-start | bytes 430088 | tf_op jit(solution)/shard_map/ppermute | solution.py:274
  29.9 20.9 %collective-permute-start.9 = (bf16[512,128]{1,0:T(8,128)(2,1)S(1)}, bf16[512,128]{1,0:T(8,128)(2,1)S(1)}, u32[]{:S(2)}, u32[]{:S(2)}) collective-permute-start(bf16[512,128]{1,0:T(8,128)(2,1)S(1)} %collective-permute-done.7.refs_5_), channel_id=1, source_target_pairs={{0,1},{1,2},{2,3},{3,4},{4,5},{5,6},{6,7},{7,0},{8,9},{9,10},{10,1... | collective-permute-start | bytes 393224 | tf_op jit(solution)/shard_map/ppermute | solution.py:44
  31.9 23.9 %collective-permute-start.5 = (bf16[560,128]{1,0:T(8,128)(2,1)}, bf16[560,128]{1,0:T(8,128)(2,1)S(1)}, u32[]{:S(2)}, u32[]{:S(2)}) collective-permute-start(bf16[560,128]{1,0:T(8,128)(2,1)} %get-tuple-element.11.refs_1_), channel_id=1, source_target_pairs={{0,256},{8,264},{16,272},{24,280},{32,288},{40,296},{48,304},{56,3... | collective-permute-start | bytes 430088 | tf_op jit(solution)/shard_map/ppermute | solution.py:274
  38.1 21.8 %collective-permute-start.4 = (bf16[560,128]{1,0:T(8,128)(2,1)}, bf16[560,128]{1,0:T(8,128)(2,1)S(1)}, u32[]{:S(2)}, u32[]{:S(2)}) collective-permute-start(bf16[560,128]{1,0:T(8,128)(2,1)} %get-tuple-element.11.refs_1_), channel_id=1, source_target_pairs={{0,128},{8,136},{16,144},{24,152},{32,160},{40,168},{48,176},{56,1... | collective-permute-start | bytes 430088 | tf_op jit(solution)/shard_map/ppermute | solution.py:274
  42.4 20.8 %collective-permute-start.3 = (bf16[560,128]{1,0:T(8,128)(2,1)}, bf16[560,128]{1,0:T(8,128)(2,1)S(1)}, u32[]{:S(2)}, u32[]{:S(2)}) collective-permute-start(bf16[560,128]{1,0:T(8,128)(2,1)} %get-tuple-element.11.refs_1_), channel_id=1, source_target_pairs={{0,64},{8,72},{16,80},{24,88},{32,96},{40,104},{48,112},{56,120},{... | collective-permute-start | bytes 430088 | tf_op jit(solution)/shard_map/ppermute | solution.py:274
  45.8 19.4 %collective-permute-start.10 = (bf16[512,128]{1,0:T(8,128)(2,1)S(1)}, bf16[512,128]{1,0:T(8,128)(2,1)S(1)}, u32[]{:S(2)}, u32[]{:S(2)}) collective-permute-start(bf16[512,128]{1,0:T(8,128)(2,1)S(1)} %collective-permute-done.8.refs_6_), channel_id=1, source_target_pairs={{0,7},{1,0},{2,1},{3,2},{4,3},{5,4},{6,5},{7,6},{8,15},{9,8},{10,9... | collective-permute-start | bytes 393224 | tf_op jit(solution)/shard_map/ppermute | solution.py:47
  50.8 18.5 %collective-permute-start.11 = (bf16[512,128]{1,0:T(8,128)(2,1)S(1)}, bf16[512,128]{1,0:T(8,128)(2,1)S(1)}, u32[]{:S(2)}, u32[]{:S(2)}) collective-permute-start(bf16[512,128]{1,0:T(8,128)(2,1)S(1)} %collective-permute-done.9.refs_7_), channel_id=1, source_target_pairs={{0,1},{1,2},{2,3},{3,4},{4,5},{5,6},{6,7},{7,0},{8,9},{9,10},{10,1... | collective-permute-start | bytes 393224 | tf_op jit(solution)/shard_map/ppermute | solution.py:44
  55.8 15.4 %collective-permute-start.2 = (bf16[560,128]{1,0:T(8,128)(2,1)}, bf16[560,128]{1,0:T(8,128)(2,1)S(1)}, u32[]{:S(2)}, u32[]{:S(2)}) collective-permute-start(bf16[560,128]{1,0:T(8,128)(2,1)} %get-tuple-element.11.refs_1_), channel_id=1, source_target_pairs={{0,32},{8,40},{16,48},{24,56},{32,0},{40,8},{48,16},{56,24},{64,96... | collective-permute-start | bytes 430088 | tf_op jit(solution)/shard_map/ppermute | solution.py:274
  59.8 11.4 %collective-permute-start.1 = (bf16[560,128]{1,0:T(8,128)(2,1)}, bf16[560,128]{1,0:T(8,128)(2,1)S(1)}, u32[]{:S(2)}, u32[]{:S(2)}) collective-permute-start(bf16[560,128]{1,0:T(8,128)(2,1)} %get-tuple-element.11.refs_1_), channel_id=1, source_target_pairs={{0,16},{8,24},{16,0},{24,8},{32,48},{40,56},{48,32},{56,40},{64,80... | collective-permute-start | bytes 430088 | tf_op jit(solution)/shard_map/ppermute | solution.py:274
  63.2 8.0 %collective-permute-start = (bf16[560,128]{1,0:T(8,128)(2,1)}, bf16[560,128]{1,0:T(8,128)(2,1)S(1)}, u32[]{:S(2)}, u32[]{:S(2)}) collective-permute-start(bf16[560,128]{1,0:T(8,128)(2,1)} %get-tuple-element.11.refs_1_), channel_id=1, source_target_pairs={{0,8},{8,0},{16,24},{24,16},{32,40},{40,32},{48,56},{56,48},{64,72... | collective-permute-start | bytes 430088 | tf_op jit(solution)/shard_map/ppermute | solution.py:274
  65.1 15.9 %collective-permute-start.12 = (bf16[512,128]{1,0:T(8,128)(2,1)S(1)}, bf16[512,128]{1,0:T(8,128)(2,1)S(1)}, u32[]{:S(2)}, u32[]{:S(2)}) collective-permute-start(bf16[512,128]{1,0:T(8,128)(2,1)S(1)} %collective-permute-done.10.refs_8_), channel_id=1, source_target_pairs={{0,7},{1,0},{2,1},{3,2},{4,3},{5,4},{6,5},{7,6},{8,15},{9,8},{10,9... | collective-permute-start | bytes 393224 | tf_op jit(solution)/shard_map/ppermute | solution.py:47
  69.3 11.8 %collective-permute-start.13 = (bf16[512,128]{1,0:T(8,128)(2,1)S(1)}, bf16[512,128]{1,0:T(8,128)(2,1)S(1)}, u32[]{:S(2)}, u32[]{:S(2)}) collective-permute-start(bf16[512,128]{1,0:T(8,128)(2,1)S(1)} %collective-permute-done.11.refs_9_), channel_id=1, source_target_pairs={{0,1},{1,2},{2,3},{3,4},{4,5},{5,6},{6,7},{7,0},{8,9},{9,10},{10,1... | collective-permute-start | bytes 393224 | tf_op jit(solution)/shard_map/ppermute | solution.py:44
  71.3 0.9 copy-start.5
  72.2 0.9 copy-start.6
  73.1 0.7 copy-start.7
  74.0 14.6 %collective-permute-start.14 = (bf16[544,128]{1,0:T(8,128)(2,1)S(1)}, bf16[544,128]{1,0:T(8,128)(2,1)S(1)}, u32[]{:S(2)}, u32[]{:S(2)}) collective-permute-start(bf16[544,128]{1,0:T(8,128)(2,1)S(1)} %get-tuple-element.15.refs_4_.late), channel_id=1, source_target_pairs={{0,1},{1,2},{2,3},{3,4},{4,5},{5,6},{6,7},{7,0},{8,9},{9,10},{10,1... | collective-permute-start | bytes 417800 | tf_op jit(solution)/shard_map/ppermute | solution.py:44
  76.0 14.5 %collective-permute-start.15 = (bf16[544,128]{1,0:T(8,128)(2,1)S(1)}, bf16[544,128]{1,0:T(8,128)(2,1)S(1)}, u32[]{:S(2)}, u32[]{:S(2)}) collective-permute-start(bf16[544,128]{1,0:T(8,128)(2,1)S(1)} %get-tuple-element.15.refs_4_.late), channel_id=1, source_target_pairs={{0,7},{1,0},{2,1},{3,2},{4,3},{5,4},{6,5},{7,6},{8,15},{9,8},{10,9... | collective-permute-start | bytes 417800 | tf_op jit(solution)/shard_map/ppermute | solution.py:47
  81.1 2.2 %copy-start = (bf16[2,512,2048]{2,1,0:T(8,128)(2,1)S(1)}, bf16[2,512,2048]{2,1,0:T(8,128)(2,1)}, u32[]{:S(2)}) copy-start(bf16[2,512,2048]{2,1,0:T(8,128)(2,1)} %refs_1_.3) | copy-start | bytes 12582916
  83.3 0.9 copy-start.2
  84.2 0.9 copy-start.3
  85.1 0.9 copy-start.4
  86.0 0.7 copy-start.8
  86.7 26.5 %copy-start.1 = (bf16[2,512,2048]{2,1,0:T(8,128)(2,1)S(1)}, bf16[2,512,2048]{2,1,0:T(8,128)(2,1)}, u32[]{:S(2)}) copy-start(bf16[2,512,2048]{2,1,0:T(8,128)(2,1)} %refs_1_.3) | copy-start | bytes 12582916
  88.6 8.3 %collective-permute-start.16 = (bf16[544,128]{1,0:T(8,128)(2,1)S(1)}, bf16[544,128]{1,0:T(8,128)(2,1)S(1)}, u32[]{:S(2)}, u32[]{:S(2)}) collective-permute-start(bf16[544,128]{1,0:T(8,128)(2,1)S(1)} %collective-permute-done.14.refs_5_), channel_id=1, source_target_pairs={{0,1},{1,2},{2,3},{3,4},{4,5},{5,6},{6,7},{7,0},{8,9},{9,10},{10,1... | collective-permute-start | bytes 417800 | tf_op jit(solution)/shard_map/ppermute | solution.py:44
  90.5 8.3 %collective-permute-start.17 = (bf16[544,128]{1,0:T(8,128)(2,1)S(1)}, bf16[544,128]{1,0:T(8,128)(2,1)S(1)}, u32[]{:S(2)}, u32[]{:S(2)}) collective-permute-start(bf16[544,128]{1,0:T(8,128)(2,1)S(1)} %collective-permute-done.15.refs_6_), channel_id=1, source_target_pairs={{0,7},{1,0},{2,1},{3,2},{4,3},{5,4},{6,5},{7,6},{8,15},{9,8},{10,9... | collective-permute-start | bytes 417800 | tf_op jit(solution)/shard_map/ppermute | solution.py:47
  96.9 8.1 %collective-permute-start.18 = (bf16[544,128]{1,0:T(8,128)(2,1)S(1)}, bf16[544,128]{1,0:T(8,128)(2,1)S(1)}, u32[]{:S(2)}, u32[]{:S(2)}) collective-permute-start(bf16[544,128]{1,0:T(8,128)(2,1)S(1)} %collective-permute-done.16.refs_7_), channel_id=1, source_target_pairs={{0,1},{1,2},{2,3},{3,4},{4,5},{5,6},{6,7},{7,0},{8,9},{9,10},{10,1... | collective-permute-start | bytes 417800 | tf_op jit(solution)/shard_map/ppermute | solution.py:44
  98.8 8.1 %collective-permute-start.19 = (bf16[544,128]{1,0:T(8,128)(2,1)S(1)}, bf16[544,128]{1,0:T(8,128)(2,1)S(1)}, u32[]{:S(2)}, u32[]{:S(2)}) collective-permute-start(bf16[544,128]{1,0:T(8,128)(2,1)S(1)} %collective-permute-done.17.refs_8_), channel_id=1, source_target_pairs={{0,7},{1,0},{2,1},{3,2},{4,3},{5,4},{6,5},{7,6},{8,15},{9,8},{10,9... | collective-permute-start | bytes 417800 | tf_op jit(solution)/shard_map/ppermute | solution.py:47
  105.1 8.1 %collective-permute-start.20 = (bf16[544,128]{1,0:T(8,128)(2,1)S(1)}, bf16[544,128]{1,0:T(8,128)(2,1)S(1)}, u32[]{:S(2)}, u32[]{:S(2)}) collective-permute-start(bf16[544,128]{1,0:T(8,128)(2,1)S(1)} %collective-permute-done.18.refs_9_), channel_id=1, source_target_pairs={{0,1},{1,2},{2,3},{3,4},{4,5},{5,6},{6,7},{7,0},{8,9},{9,10},{10,1... | collective-permute-start | bytes 417800 | tf_op jit(solution)/shard_map/ppermute | solution.py:44

commit v4 on v3

--- a/solution.py
+++ b/solution.py
@@ -11,7 +11,6 @@
 MOVE = 2
 STEP_ROOT = 0.1
 N_CHOL = 8
-OFFSETS = (0, -1, 1, -2, 2, -3, 3, -4)
 TILE = 16
 ORBS = 256
 STRIDE = ORBS + TILE
@@ -30,23 +29,8 @@
     return pltpu.CompilerParams(vmem_limit_bytes=megabytes << 20)
 
 
-def after(value, *others):
-    return lax.optimization_barrier((value, *others))[0]
-
-
-def ring(block, gate=None):
-    up = [(i, (i + 1) % N_CHOL) for i in range(N_CHOL)]
-    down = [(i, (i - 1) % N_CHOL) for i in range(N_CHOL)]
-    parts, low, high = [block], block, block
-    for step in range(N_CHOL // 2):
-        if step == 1 and gate is not None:
-            low, high = after(low, gate), after(high, gate)
-        low = lax.ppermute(low, "chol", up)
-        parts.append(low)
-        if step < N_CHOL // 2 - 1:
-            high = lax.ppermute(high, "chol", down)
-            parts.append(high)
-    return parts
+def gather(copies):
+    return lax.all_to_all(copies, "chol", 0, 0, tiled=True)
 
 
 def inv_rows(inv, slot):
@@ -66,7 +50,8 @@
         add(walkers.at[LIVE + j], out, j * STRIDE, ORBS)
         add(inv_rows(inv, LIVE + j), out, j * STRIDE + ORBS, TILE)
     for j in range(MOVE):
-        add(walkers.at[j], early, j * ORBS, ORBS)
+        for k in range(N_CHOL):
+            add(walkers.at[j], early.at[k], j * ORBS, ORBS)
         add(walkers.at[2 + j], kept, j * STRIDE, ORBS)
         add(inv_rows(inv, 2 + j), kept, j * STRIDE + ORBS, TILE)
     for copy in copies:
@@ -91,11 +76,11 @@
         out_specs=(WHOLE,) * 4,
         out_shape=(
             jax.ShapeDtypeStruct((FIELD_ROW + TILE, lanes), BF16),
-            jax.ShapeDtypeStruct((2 * ORBS, lanes), BF16),
+            jax.ShapeDtypeStruct((N_CHOL, 2 * ORBS, lanes), BF16),
             jax.ShapeDtypeStruct((RING_ROWS, lanes), BF16),
             jax.ShapeDtypeStruct((8, lanes), jnp.int32),
         ),
-        scratch_shapes=[pltpu.SemaphoreType.DMA((5 * MOVE,))],
+        scratch_shapes=[pltpu.SemaphoreType.DMA(((4 + N_CHOL) * MOVE,))],
         name="pack",
     )(counts, partner, walkers, inv, fields)
 
@@ -111,14 +96,16 @@
             block = jnp.where(here, received[bit][rows, :width].astype(F32), block)
         return block
 
-    lanes = out.shape[1]
+    lanes = kept.shape[1]
     for q in range(2):
         for first in range(0, STRIDE, TILE):
             mine = kept[q * STRIDE + first : q * STRIDE + first + TILE].astype(F32)
             start = (1 - q) * STRIDE + first
             theirs = sent(slice(start, start + TILE), lanes)
             rows = slice(q * STRIDE + first, q * STRIDE + first + TILE)
-            out[rows] = jnp.where(own > 2 + q, mine, theirs).astype(BF16)
+            block = jnp.where(own > 2 + q, mine, theirs).astype(BF16)
+            for k in range(N_CHOL):
+                out[k, rows] = block
     rows = slice(FIELD_ROW, FIELD_ROW + TILE)
     mine, theirs = outgoing[rows].astype(F32), sent(rows, lanes)
     for q in range(2):
@@ -138,7 +125,7 @@
         in_specs=[WHOLE] * (3 + bits),
         out_specs=(WHOLE, WHOLE),
         out_shape=(
-            jax.ShapeDtypeStruct((RING_ROWS, lanes), BF16),
+            jax.ShapeDtypeStruct((N_CHOL, RING_ROWS, lanes), BF16),
             jax.ShapeDtypeStruct((TILE, lanes), F32),
         ),
         compiler_params=params(4),
@@ -146,34 +133,29 @@
     )(plan, outgoing, kept, *received)
 
 
-def product_kernel(late, x, chol, trial, extra, *refs):
-    parts, out, minv = refs[:N_CHOL], refs[N_CHOL], refs[N_CHOL + 1]
+def product_kernel(late, x, chol, trial, extra, parts, out, minv):
     lanes = out.shape[2]
     stride, base = (STRIDE, 2) if late else (ORBS, 0)
-    me = lax.axis_index("chol")
-    owners = [jnp.bitwise_and(me + offset, N_CHOL - 1) for offset in OFFSETS]
-    columns = [pl.ds(pl.multiple_of(owner * ORBS, ORBS), ORBS) for owner in owners]
     row_id = lax.broadcasted_iota(jnp.int32, (TILE, lanes), 0)
     lane_id = lax.broadcasted_iota(jnp.int32, (TILE, lanes), 1)
     logs = jnp.zeros((TILE, lanes), F32)
     if late:
         logs = extra[0, base * ROWS_DEV :].astype(F32)
         out[:, : base * ROWS_DEV] = extra[:, : base * ROWS_DEV]
-        for owner, part in zip(owners, parts):
-            share = pl.ds(pl.multiple_of(owner * TILE, TILE), TILE)
+        for k in range(N_CHOL):
             for q in range(2):
-                minv[q, share] = part[q * stride + ORBS : (q + 1) * stride]
+                rows = parts[k, q * stride + ORBS : (q + 1) * stride]
+                minv[q, k * TILE : (k + 1) * TILE] = rows
     phi = jnp.concatenate(
         [
-            jnp.concatenate([part[q * stride : q * stride + ORBS] for q in range(2)], axis=1)
-            for part in parts
+            jnp.concatenate([parts[k, q * stride : q * stride + ORBS] for q in range(2)], axis=1)
+            for k in range(N_CHOL)
         ],
         axis=0,
     )
     products = []
     for g in range(chol.shape[0]):
-        rows = jnp.concatenate([chol[g, :, spot] for spot in columns], axis=1)
-        products.append(jnp.dot(rows, phi, preferred_element_type=F32))
+        products.append(jnp.dot(chol[g], phi, preferred_element_type=F32))
     for q in range(2):
         weighted = lax.dot_general(
             trial[...],
@@ -211,14 +193,14 @@
 
     return pl.pallas_call(
         body,
-        in_specs=[WHOLE] * (4 + N_CHOL),
+        in_specs=[WHOLE] * 5,
         out_specs=WHOLE,
         out_shape=jax.ShapeDtypeStruct((N_CHOL, out_rows, lanes), BF16),
         scratch_shapes=[pltpu.VMEM((2, lanes, lanes), BF16)],
         compiler_params=params(24),
         name="late_products" if late else "early_products",
         cost_estimate=pl.CostEstimate(flops=flops, bytes_accessed=6 << 20, transcendentals=0),
-    )(x, cholesky, trial, extra, *parts)
+    )(x, cholesky, trial, extra, parts)
 
 
 def finish_kernel(plan, got, early, late, out, log_out):
@@ -229,7 +211,7 @@
     walkers, logs = [], []
     for spot in range(LIVE):
         block, first = (early, spot * ORBS) if spot < 2 else (late, (spot - 2) * STRIDE)
-        total = block[first : first + ROWS_DEV].astype(F32)
+        total = block[0, first : first + ROWS_DEV].astype(F32)
         for k in range(N_CHOL):
             total += got[k, spot * ROWS_DEV : (spot + 1) * ROWS_DEV].astype(F32)
         walkers.append(total)
@@ -268,16 +250,16 @@
     outgoing, early, kept, plan = pack_call(
         counts, partner, walkers, inv_intersection, fields
     )
+    early_parts = gather(early)
     received = []
     for bit in range(walk_size.bit_length() - 1):
         route = [(i, i ^ 1 << bit) for i in range(walk_size)]
         received.append(lax.ppermute(outgoing, "walk", route))
-    early_parts = ring(early)
     late, x = merge_call(plan, outgoing, kept, received)
+    late_parts = gather(late)
     first = product_call(
         False, fields, cholesky, trial_rows, inv_intersection, early_parts
     )
-    late_parts = ring(late, first)
     sums = product_call(True, x, cholesky, trial_rows, first, late_parts)
     sums = lax.all_to_all(sums, "chol", 0, 0, tiled=True)
     return tuple(finish_call(plan, sums, early, late))

time: 137 us -> 127 us (0.927)
  the two profiles are of different devices: /device:TPU:2 before, /device:TPU:1 now
where the time goes in v4:
time: 127 us
  starting transfers between devices  55.8 us (44%)
  waiting for transfers between devices  34.1 us (27%)
  blocking collectives  20.9 us (16%)
  Pallas kernels  10.5 us (8%)
  local copies, waits for them, and re-layouts  4.4 us (3%)
    ppermute x7, starting transfers between devices, shards(): received.append(lax.ppermute(outgoing, 'walk', route))  41.3 us
    all_to_all x2, waiting for transfers between devices, gather(): return lax.all_to_all(copies, 'chol', 0, 0, tiled=True)  26.6 us
    all_to_all x1, blocking collectives, shards(): sums = lax.all_to_all(sums, 'chol', 0, 0, tiled=True)  20.9 us
    all_to_all x2, starting transfers between devices, gather(): return lax.all_to_all(copies, 'chol', 0, 0, tiled=True)  14.5 us
    ppermute x7, waiting for transfers between devices, shards(): received.append(lax.ppermute(outgoing, 'walk', route))  7.54 us
    unnamed x18, local copies, waits for them, and re-layouts  4.4 us
    pallas_call x2, Pallas kernels, product_call(): pl.pallas_call(body, in_specs=[WHOLE] * 5, out_specs=WHOLE, out_shape=jax...  3.74 us
    pallas_call x1, Pallas kernels, pack_call(): pl.pallas_call(pack_kernel, in_specs=[SCALARS, SCALARS, HBM, HBM, WHOLE],...  3.56 us
  transfers between devices with their start and end apart: 9, of which 3 were waited for; matrix products, arithmetic and copies ran while one was open for 0% of the time, Pallas kernels for 2%

profile of v4, /device:TPU:1, one launch (start us, length us, event | category | flops | bytes accessed | tf_op | source)
XLA Modules:
  0.0 126.5 jit_solution(18092278970335187126)
XLA Ops:
  0.6 3.6 %pack.1 = (bf16[560,128]{1,0:T(8,128)(2,1)}, bf16[8,512,128]{2,1,0:T(8,128)(2,1)}, bf16[544,128]{1,0:T(8,128)(2,1)}, s32[8,128]{1,0:T(8,128)}) custom-call(s32[128]{0:T(128)} %counts.1, s32[128]{0:T(128)} %partner.1, bf16[6,256,128]{2,1,0:T(8,128)(2,1)} %walkers.1, bf16[6,128,128]{2,1,0:T(8,128)(2,1)} %refs_3_.1, bf16[2,6]{1,0:T(2,128)(2,1)} %bitcast.1), custom_call_target="tpu_custom_call" | custom-call | tf_op jit(solution)/shard_map/pack/pallas_call | solution.py:73
  4.2 0.0 copy-start.5
  4.2 0.0 copy-start.6
  4.2 0.0 copy-start.7
  4.2 7.8 %all-to-all-start = ((bf16[8,512,128]{2,1,0:T(8,128)(2,1)}), bf16[8,512,128]{2,1,0:T(8,128)(2,1)S(1)}, u32[]{:S(2)}, u32[]{:S(2)}) async-start(bf16[8,512,128]{2,1,0:T(8,128)(2,1)} %get-tuple-element.12.early), calls=%async_computation | async-start | bytes 2097152 | tf_op jit(solution)/shard_map/all_to_all | solution.py:33
  12.1 0.0 copy-done.5
  12.1 19.1 %collective-permute-start.6 = (bf16[560,128]{1,0:T(8,128)(2,1)S(1)}, bf16[560,128]{1,0:T(8,128)(2,1)S(1)}, u32[]{:S(2)}, u32[]{:S(2)}) collective-permute-start(bf16[560,128]{1,0:T(8,128)(2,1)S(1)} %copy-done.5), channel_id=1, source_target_pairs={{0,512},{8,520},{16,528},{24,536},{32,544},{40,552},{48,560},{56,5... | collective-permute-start | bytes 430088 | tf_op jit(solution)/shard_map/ppermute | solution.py:257
  31.1 5.8 %collective-permute-start.5 = (bf16[560,128]{1,0:T(8,128)(2,1)S(1)}, bf16[560,128]{1,0:T(8,128)(2,1)S(1)}, u32[]{:S(2)}, u32[]{:S(2)}) collective-permute-start(bf16[560,128]{1,0:T(8,128)(2,1)S(1)} %copy-done.5), channel_id=1, source_target_pairs={{0,256},{8,264},{16,272},{24,280},{32,288},{40,296},{48,304},{56,3... | collective-permute-start | bytes 430088 | tf_op jit(solution)/shard_map/ppermute | solution.py:257
  37.0 4.0 %collective-permute-start.4 = (bf16[560,128]{1,0:T(8,128)(2,1)S(1)}, bf16[560,128]{1,0:T(8,128)(2,1)S(1)}, u32[]{:S(2)}, u32[]{:S(2)}) collective-permute-start(bf16[560,128]{1,0:T(8,128)(2,1)S(1)} %copy-done.5), channel_id=1, source_target_pairs={{0,128},{8,136},{16,144},{24,152},{32,160},{40,168},{48,176},{56,1... | collective-permute-start | bytes 430088 | tf_op jit(solution)/shard_map/ppermute | solution.py:257
  41.0 3.1 %collective-permute-start.3 = (bf16[560,128]{1,0:T(8,128)(2,1)S(1)}, bf16[560,128]{1,0:T(8,128)(2,1)S(1)}, u32[]{:S(2)}, u32[]{:S(2)}) collective-permute-start(bf16[560,128]{1,0:T(8,128)(2,1)S(1)} %copy-done.5), channel_id=1, source_target_pairs={{0,64},{8,72},{16,80},{24,88},{32,96},{40,104},{48,112},{56,120},{... | collective-permute-start | bytes 430088 | tf_op jit(solution)/shard_map/ppermute | solution.py:257
  44.1 4.7 %collective-permute-start.2 = (bf16[560,128]{1,0:T(8,128)(2,1)S(1)}, bf16[560,128]{1,0:T(8,128)(2,1)S(1)}, u32[]{:S(2)}, u32[]{:S(2)}) collective-permute-start(bf16[560,128]{1,0:T(8,128)(2,1)S(1)} %copy-done.5), channel_id=1, source_target_pairs={{0,32},{8,40},{16,48},{24,56},{32,0},{40,8},{48,16},{56,24},{64,96... | collective-permute-start | bytes 430088 | tf_op jit(solution)/shard_map/ppermute | solution.py:257
  48.8 0.0 collective-permute-done.6.refs_9_
  48.8 2.2 %collective-permute-start.1 = (bf16[560,128]{1,0:T(8,128)(2,1)S(1)}, bf16[560,128]{1,0:T(8,128)(2,1)S(1)}, u32[]{:S(2)}, u32[]{:S(2)}) collective-permute-start(bf16[560,128]{1,0:T(8,128)(2,1)S(1)} %copy-done.5), channel_id=1, source_target_pairs={{0,16},{8,24},{16,0},{24,8},{32,48},{40,56},{48,32},{56,40},{64,80... | collective-permute-start | bytes 430088 | tf_op jit(solution)/shard_map/ppermute | solution.py:257
  51.0 6.6 %collective-permute-done.5.refs_8_ = bf16[560,128]{1,0:T(8,128)(2,1)S(1)} collective-permute-done((bf16[560,128]{1,0:T(8,128)(2,1)S(1)}, bf16[560,128]{1,0:T(8,128)(2,1)S(1)}, u32[]{:S(2)}, u32[]{:S(2)}) %collective-permute-start.5) | collective-permute-done | bytes 143392 | tf_op jit(solution)/shard_map/ppermute | solution.py:257
  57.6 2.4 %collective-permute-start = (bf16[560,128]{1,0:T(8,128)(2,1)S(1)}, bf16[560,128]{1,0:T(8,128)(2,1)S(1)}, u32[]{:S(2)}, u32[]{:S(2)}) collective-permute-start(bf16[560,128]{1,0:T(8,128)(2,1)S(1)} %copy-done.5), channel_id=1, source_target_pairs={{0,8},{8,0},{16,24},{24,16},{32,40},{40,32},{48,56},{56,48},{64,72... | collective-permute-start | bytes 430088 | tf_op jit(solution)/shard_map/ppermute | solution.py:257
  60.0 0.0 collective-permute-done.4.refs_7_
  60.0 0.0 collective-permute-done.3.refs_6_
  60.0 0.0 collective-permute-done.2.refs_5_
  60.0 0.0 collective-permute-done.1.refs_4_
  60.0 0.9 collective-permute-done.refs_3_
  61.0 0.0 copy-done.6
  61.0 0.0 copy-done.7
  61.0 1.2 merge.1
  62.2 0.0 all-to-all-done.refs_4_
  62.2 0.0 copy-start.3
  62.2 0.0 copy-start.4
  62.2 0.0 copy-start.8
  62.2 6.7 %all-to-all-start.1 = ((bf16[8,544,128]{2,1,0:T(8,128)(2,1)}), bf16[8,544,128]{2,1,0:T(8,128)(2,1)S(1)}, u32[]{:S(2)}, u32[]{:S(2)}) async-start(bf16[8,544,128]{2,1,0:T(8,128)(2,1)} %get-tuple-element.13.late), calls=%async_computation.1 | async-start | bytes 2228224 | tf_op jit(solution)/shard_map/all_to_all | solution.py:33
  68.9 0.0 copy-done.3
  68.9 0.0 copy-done.4
  68.9 0.0 copy-done.8
  68.9 0.0 copy-start
  69.0 2.2 %copy-done = bf16[2,512,2048]{2,1,0:T(8,128)(2,1)S(1)} copy-done((bf16[2,512,2048]{2,1,0:T(8,128)(2,1)S(1)}, bf16[2,512,2048]{2,1,0:T(8,128)(2,1)}, u32[]{:S(2)}) %copy-start) | copy-done | bytes 4194328
  71.1 1.9 %early_products.1.refs_3_ = bf16[8,144,128]{2,1,0:T(8,128)(2,1)S(1)} custom-call(bf16[2,6]{1,0:T(2,128)(2,1)S(1)} %bitcast.2, bf16[2,512,2048]{2,1,0:T(8,128)(2,1)S(1)} %copy-done, bf16[512,128]{1,0:T(8,128)(2,1)S(1)} %copy-done.4, bf16[6,128,128]{2,1,0:T(8,128)(2,1)S(1)} %copy-done.3, bf16[8,512,128]{2,1,0:T(8,128)(2,1)S(1)} %all-to-all-done.refs_4_), custom_call_target="tpu_custom_call" | custom-call | flops 1073741824 | bytes 6291456 | tf_op jit(solution)/shard_map/early_products/pallas_call | solution.py:194
  73.0 26.6 %all-to-all-done.1.refs_4_ = bf16[8,544,128]{2,1,0:T(8,128)(2,1)S(1)} async-done(((bf16[8,544,128]{2,1,0:T(8,128)(2,1)}), bf16[8,544,128]{2,1,0:T(8,128)(2,1)S(1)}, u32[]{:S(2)}, u32[]{:S(2)}) %all-to-all-start.1) | async-done | bytes 1114144 | tf_op jit(solution)/shard_map/all_to_all | solution.py:33
  99.6 0.0 copy-start.1
  99.6 2.2 %copy-done.1 = bf16[2,512,2048]{2,1,0:T(8,128)(2,1)S(1)} copy-done((bf16[2,512,2048]{2,1,0:T(8,128)(2,1)S(1)}, bf16[2,512,2048]{2,1,0:T(8,128)(2,1)}, u32[]{:S(2)}) %copy-start.1) | copy-done | bytes 4194328
  101.8 1.9 %late_products.1 = bf16[8,272,128]{2,1,0:T(8,128)(2,1)S(1)} custom-call(f32[16,128]{1,0:T(8,128)S(1)} %get-tuple-element.11.refs_0_, bf16[2,512,2048]{2,1,0:T(8,128)(2,1)S(1)} %copy-done.1, bf16[512,128]{1,0:T(8,128)(2,1)S(1)} %copy-done.4, bf16[8,144,128]{2,1,0:T(8,128)(2,1)S(1)} %early_products.1.refs_3_, bf16[8,544,128]{2,1,0:T(8,128)(2,1)S(1)} %all-to-all-done.1.refs_4_), custom_call_target="tpu_custom_call" | custom-call | flops 1073741824 | bytes 6291456 | tf_op jit(solution)/shard_map/late_products/pallas_call | solution.py:194
  103.6 0.0 copy-start.2
  103.6 20.9 %all_to_all.15.got = bf16[8,272,128]{2,1,0:T(8,128)(2,1)S(1)} all-to-all(bf16[8,272,128]{2,1,0:T(8,128)(2,1)S(1)} %late_products.1), channel_id=1, replica_groups=mesh['walk'=128,'chol'=8] {'chol'}, dimensions={0} | all-to-all | bytes 1114112 | tf_op jit(solution)/shard_map/all_to_all | solution.py:264
  124.5 0.0 copy-done.2
  124.5 2.0 %finish.1 = (bf16[4,64,128]{2,1,0:T(8,128)(2,1)}, f32[4]{0:T(128)}) custom-call(s32[8,128]{1,0:T(8,128)S(1)} %copy-done.7, bf16[8,272,128]{2,1,0:T(8,128)(2,1)S(1)} %all_to_all.15.got, bf16[8,512,128]{2,1,0:T(8,128)(2,1)S(1)} %copy-done.2, bf16[8,544,128]{2,1,0:T(8,128)(2,1)} %get-tuple-element.13.late), custom_call_target="tpu_custom_call" | custom-call | tf_op jit(solution)/shard_map/finish/pallas_call | solution.py:234
Async XLA Ops:
  4.2 7.9 %copy-start.5 = (bf16[560,128]{1,0:T(8,128)(2,1)S(1)}, bf16[560,128]{1,0:T(8,128)(2,1)}, u32[]{:S(2)}) copy-start(bf16[560,128]{1,0:T(8,128)(2,1)} %get-tuple-element.9.refs_1_) | copy-start | bytes 430084
  4.2 56.8 %copy-start.6 = (bf16[544,128]{1,0:T(8,128)(2,1)S(1)}, bf16[544,128]{1,0:T(8,128)(2,1)}, u32[]{:S(2)}) copy-start(bf16[544,128]{1,0:T(8,128)(2,1)} %get-tuple-element.10.refs_2_) | copy-start | bytes 417796
  4.2 56.8 %copy-start.7 = (s32[8,128]{1,0:T(8,128)S(1)}, s32[8,128]{1,0:T(8,128)}, u32[]{:S(2)}) copy-start(s32[8,128]{1,0:T(8,128)} %get-tuple-element.8.refs_0_.plan) | copy-start | bytes 12292
  4.2 58.0 %all-to-all-start = ((bf16[8,512,128]{2,1,0:T(8,128)(2,1)}), bf16[8,512,128]{2,1,0:T(8,128)(2,1)S(1)}, u32[]{:S(2)}, u32[]{:S(2)}) async-start(bf16[8,512,128]{2,1,0:T(8,128)(2,1)} %get-tuple-element.12.early), calls=%async_computation | async-start | bytes 2097152 | tf_op jit(solution)/shard_map/all_to_all | solution.py:33
  12.1 36.7 %collective-permute-start.6 = (bf16[560,128]{1,0:T(8,128)(2,1)S(1)}, bf16[560,128]{1,0:T(8,128)(2,1)S(1)}, u32[]{:S(2)}, u32[]{:S(2)}) collective-permute-start(bf16[560,128]{1,0:T(8,128)(2,1)S(1)} %copy-done.5), channel_id=1, source_target_pairs={{0,512},{8,520},{16,528},{24,536},{32,544},{40,552},{48,560},{56,5... | collective-permute-start | bytes 430088 | tf_op jit(solution)/shard_map/ppermute | solution.py:257
  31.1 26.5 %collective-permute-start.5 = (bf16[560,128]{1,0:T(8,128)(2,1)S(1)}, bf16[560,128]{1,0:T(8,128)(2,1)S(1)}, u32[]{:S(2)}, u32[]{:S(2)}) collective-permute-start(bf16[560,128]{1,0:T(8,128)(2,1)S(1)} %copy-done.5), channel_id=1, source_target_pairs={{0,256},{8,264},{16,272},{24,280},{32,288},{40,296},{48,304},{56,3... | collective-permute-start | bytes 430088 | tf_op jit(solution)/shard_map/ppermute | solution.py:257
  37.0 23.0 %collective-permute-start.4 = (bf16[560,128]{1,0:T(8,128)(2,1)S(1)}, bf16[560,128]{1,0:T(8,128)(2,1)S(1)}, u32[]{:S(2)}, u32[]{:S(2)}) collective-permute-start(bf16[560,128]{1,0:T(8,128)(2,1)S(1)} %copy-done.5), channel_id=1, source_target_pairs={{0,128},{8,136},{16,144},{24,152},{32,160},{40,168},{48,176},{56,1... | collective-permute-start | bytes 430088 | tf_op jit(solution)/shard_map/ppermute | solution.py:257
  41.0 19.0 %collective-permute-start.3 = (bf16[560,128]{1,0:T(8,128)(2,1)S(1)}, bf16[560,128]{1,0:T(8,128)(2,1)S(1)}, u32[]{:S(2)}, u32[]{:S(2)}) collective-permute-start(bf16[560,128]{1,0:T(8,128)(2,1)S(1)} %copy-done.5), channel_id=1, source_target_pairs={{0,64},{8,72},{16,80},{24,88},{32,96},{40,104},{48,112},{56,120},{... | collective-permute-start | bytes 430088 | tf_op jit(solution)/shard_map/ppermute | solution.py:257
  44.1 15.9 %collective-permute-start.2 = (bf16[560,128]{1,0:T(8,128)(2,1)S(1)}, bf16[560,128]{1,0:T(8,128)(2,1)S(1)}, u32[]{:S(2)}, u32[]{:S(2)}) collective-permute-start(bf16[560,128]{1,0:T(8,128)(2,1)S(1)} %copy-done.5), channel_id=1, source_target_pairs={{0,32},{8,40},{16,48},{24,56},{32,0},{40,8},{48,16},{56,24},{64,96... | collective-permute-start | bytes 430088 | tf_op jit(solution)/shard_map/ppermute | solution.py:257
  48.8 11.3 %collective-permute-start.1 = (bf16[560,128]{1,0:T(8,128)(2,1)S(1)}, bf16[560,128]{1,0:T(8,128)(2,1)S(1)}, u32[]{:S(2)}, u32[]{:S(2)}) collective-permute-start(bf16[560,128]{1,0:T(8,128)(2,1)S(1)} %copy-done.5), channel_id=1, source_target_pairs={{0,16},{8,24},{16,0},{24,8},{32,48},{40,56},{48,32},{56,40},{64,80... | collective-permute-start | bytes 430088 | tf_op jit(solution)/shard_map/ppermute | solution.py:257
  57.6 3.4 %collective-permute-start = (bf16[560,128]{1,0:T(8,128)(2,1)S(1)}, bf16[560,128]{1,0:T(8,128)(2,1)S(1)}, u32[]{:S(2)}, u32[]{:S(2)}) collective-permute-start(bf16[560,128]{1,0:T(8,128)(2,1)S(1)} %copy-done.5), channel_id=1, source_target_pairs={{0,8},{8,0},{16,24},{24,16},{32,40},{40,32},{48,56},{56,48},{64,72... | collective-permute-start | bytes 430088 | tf_op jit(solution)/shard_map/ppermute | solution.py:257
  62.2 6.7 %copy-start.3 = (bf16[6,128,128]{2,1,0:T(8,128)(2,1)S(1)}, bf16[6,128,128]{2,1,0:T(8,128)(2,1)}, u32[]{:S(2)}) copy-start(bf16[6,128,128]{2,1,0:T(8,128)(2,1)} %refs_3_.1) | copy-start | bytes 589828
  62.2 6.7 %copy-start.4 = (bf16[512,128]{1,0:T(8,128)(2,1)S(1)}, bf16[512,128]{1,0:T(8,128)(2,1)}, u32[]{:S(2)}) copy-start(bf16[512,128]{1,0:T(8,128)(2,1)} %refs_2_.3) | copy-start | bytes 393220
  62.2 6.8 %copy-start.8 = (bf16[6,2]{0,1:T(2,128)(2,1)S(1)}, bf16[6,2]{0,1:T(2,128)(2,1)}, u32[]{:S(2)}) copy-start(bf16[6,2]{0,1:T(2,128)(2,1)} %param.9) | copy-start | bytes 76
  62.2 37.4 %all-to-all-start.1 = ((bf16[8,544,128]{2,1,0:T(8,128)(2,1)}), bf16[8,544,128]{2,1,0:T(8,128)(2,1)S(1)}, u32[]{:S(2)}, u32[]{:S(2)}) async-start(bf16[8,544,128]{2,1,0:T(8,128)(2,1)} %get-tuple-element.13.late), calls=%async_computation.1 | async-start | bytes 2228224 | tf_op jit(solution)/shard_map/all_to_all | solution.py:33
  68.9 2.2 %copy-start = (bf16[2,512,2048]{2,1,0:T(8,128)(2,1)S(1)}, bf16[2,512,2048]{2,1,0:T(8,128)(2,1)}, u32[]{:S(2)}) copy-start(bf16[2,512,2048]{2,1,0:T(8,128)(2,1)} %refs_1_.3) | copy-start | bytes 12582916
  99.6 2.2 %copy-start.1 = (bf16[2,512,2048]{2,1,0:T(8,128)(2,1)S(1)}, bf16[2,512,2048]{2,1,0:T(8,128)(2,1)}, u32[]{:S(2)}) copy-start(bf16[2,512,2048]{2,1,0:T(8,128)(2,1)} %refs_1_.3) | copy-start | bytes 12582916
  103.6 20.9 %copy-start.2 = (bf16[8,512,128]{2,1,0:T(8,128)(2,1)S(1)}, bf16[8,512,128]{2,1,0:T(8,128)(2,1)}, u32[]{:S(2)}) copy-start(bf16[8,512,128]{2,1,0:T(8,128)(2,1)} %get-tuple-element.12.early) | copy-start | bytes 3145732

commit v5 on v4

--- a/solution.py
+++ b/solution.py
@@ -11,11 +11,13 @@
 MOVE = 2
 STEP_ROOT = 0.1
 N_CHOL = 8
+OFFSETS = (0, -1, 1, -2, 2, -3, 3, -4)
 TILE = 16
 ORBS = 256
 STRIDE = ORBS + TILE
 RING_ROWS = 2 * STRIDE
 FIELD_ROW = MOVE * STRIDE
+DISTANCE, OWN, ARRIVING = 8, 9, 10
 
 ANY = pl.BlockSpec(memory_space=pl.ANY)
 HBM = pl.BlockSpec(memory_space=pltpu.HBM)
@@ -33,12 +35,25 @@
     return lax.all_to_all(copies, "chol", 0, 0, tiled=True)
 
 
+def gather_in_two(block):
+    def shift(value, distance):
+        route = [(i, (i + distance) % N_CHOL) for i in range(N_CHOL)]
+        return lax.ppermute(value, "chol", route)
+
+    low = shift(block, 2)
+    high = shift(block, -2)
+    below = shift(block, 1)
+    above = shift(block, -1)
+    far = shift(low, 2)
+    return [block, below, above, low, high, shift(low, 1), shift(high, -1), far]
+
+
 def inv_rows(inv, slot):
     share = pl.multiple_of(lax.axis_index("chol") * TILE, TILE)
     return inv.at[slot, pl.ds(share, TILE)]
 
 
-def pack_kernel(counts, partner, walkers, inv, fields, out, early, kept, plan, sems):
+def pack_kernel(counts, partner, walkers, inv, fields, out, early, kept, sems):
     copies = []
 
     def add(source, target, first, size):
@@ -60,10 +75,13 @@
     out[FIELD_ROW : FIELD_ROW + fields.shape[0], : fields.shape[1]] = fields[...]
     walk = lax.axis_index("walk")
     mate = partner[walk]
-    row_id = lax.broadcasted_iota(jnp.int32, plan.shape, 0)
-    arriving = jnp.maximum(counts[mate] - LIVE, 0)
-    rest = jnp.where(row_id == 1, counts[walk], arriving)
-    plan[...] = jnp.where(row_id == 0, jnp.bitwise_xor(mate, walk), rest)
+    row_id = lax.broadcasted_iota(jnp.int32, (TILE, kept.shape[1]), 0)
+    plan = (jnp.bitwise_xor(mate, walk), counts[walk], jnp.maximum(counts[mate] - LIVE, 0))
+    tile = jnp.zeros(row_id.shape, jnp.int32)
+    for row, value in zip((DISTANCE, OWN, ARRIVING), plan):
+        tile = jnp.where(row_id == row, value, tile)
+    kept[FIELD_ROW:] = tile.astype(F32).astype(BF16)
+    kept[FIELD_ROW : FIELD_ROW + fields.shape[0], : fields.shape[1]] = fields[...]
     for copy in copies:
         copy.wait()
 
@@ -73,21 +91,21 @@
     return pl.pallas_call(
         pack_kernel,
         in_specs=[SCALARS, SCALARS, HBM, HBM, WHOLE],
-        out_specs=(WHOLE,) * 4,
+        out_specs=(WHOLE,) * 3,
         out_shape=(
             jax.ShapeDtypeStruct((FIELD_ROW + TILE, lanes), BF16),
             jax.ShapeDtypeStruct((N_CHOL, 2 * ORBS, lanes), BF16),
-            jax.ShapeDtypeStruct((RING_ROWS, lanes), BF16),
-            jax.ShapeDtypeStruct((8, lanes), jnp.int32),
+            jax.ShapeDtypeStruct((FIELD_ROW + TILE, lanes), BF16),
         ),
         scratch_shapes=[pltpu.SemaphoreType.DMA(((4 + N_CHOL) * MOVE,))],
         name="pack",
     )(counts, partner, walkers, inv, fields)
 
 
-def merge_kernel(bits, plan, outgoing, kept, *refs):
+def merge_kernel(bits, kept, *refs):
     received, (out, x) = refs[:bits], refs[bits:]
-    distance, own = plan[0:1], plan[1:2]
+    tile = kept[FIELD_ROW:].astype(F32)
+    distance, own = tile[DISTANCE : DISTANCE + 1], tile[OWN : OWN + 1]
 
     def sent(rows, width):
         block = jnp.zeros((rows.stop - rows.start, width), F32)
@@ -97,6 +115,7 @@
         return block
 
     lanes = kept.shape[1]
+    row_id = lax.broadcasted_iota(jnp.int32, (TILE, 1), 0)
     for q in range(2):
         for first in range(0, STRIDE, TILE):
             mine = kept[q * STRIDE + first : q * STRIDE + first + TILE].astype(F32)
@@ -104,17 +123,16 @@
             theirs = sent(slice(start, start + TILE), lanes)
             rows = slice(q * STRIDE + first, q * STRIDE + first + TILE)
             block = jnp.where(own > 2 + q, mine, theirs).astype(BF16)
-            for k in range(N_CHOL):
-                out[k, rows] = block
-    rows = slice(FIELD_ROW, FIELD_ROW + TILE)
-    mine, theirs = outgoing[rows].astype(F32), sent(rows, lanes)
+            out[rows] = block
+    theirs = sent(slice(FIELD_ROW, FIELD_ROW + TILE), lanes)
+    x[...] = tile
     for q in range(2):
-        mask = own[:, q : q + 1] > 2 + q
-        column = jnp.where(mask, mine[:, 2 + q : 3 + q], theirs[:, LIVE + 1 - q : LIVE + 2 - q])
+        mask = (own[:, q : q + 1] > 2 + q) | (row_id >= DISTANCE)
+        column = jnp.where(mask, tile[:, 2 + q : 3 + q], theirs[:, LIVE + 1 - q : LIVE + 2 - q])
         x[:, q : q + 1] = column
 
 
-def merge_call(plan, outgoing, kept, received):
+def merge_call(kept, received):
     bits, lanes = len(received), kept.shape[1]
 
     def body(*refs):
@@ -122,40 +140,50 @@
 
     return pl.pallas_call(
         body,
-        in_specs=[WHOLE] * (3 + bits),
+        in_specs=[WHOLE] * (1 + bits),
         out_specs=(WHOLE, WHOLE),
         out_shape=(
-            jax.ShapeDtypeStruct((N_CHOL, RING_ROWS, lanes), BF16),
+            jax.ShapeDtypeStruct((RING_ROWS, lanes), BF16),
             jax.ShapeDtypeStruct((TILE, lanes), F32),
         ),
         compiler_params=params(4),
         name="merge",
-    )(plan, outgoing, kept, *received)
-
-
-def product_kernel(late, x, chol, trial, extra, parts, out, minv):
+    )(kept, *received)
+
+
+def product_kernel(late, x, chol, trial, extra, *refs):
+    parts, (out, minv) = refs[:-2], refs[-2:]
     lanes = out.shape[2]
     stride, base = (STRIDE, 2) if late else (ORBS, 0)
+    if late:
+        me = lax.axis_index("chol")
+        owners = [jnp.bitwise_and(me + offset, N_CHOL - 1) for offset in OFFSETS]
+        columns = [pl.ds(pl.multiple_of(owner * ORBS, ORBS), ORBS) for owner in owners]
+    else:
+        parts = [parts[0].at[k] for k in range(N_CHOL)]
     row_id = lax.broadcasted_iota(jnp.int32, (TILE, lanes), 0)
     lane_id = lax.broadcasted_iota(jnp.int32, (TILE, lanes), 1)
     logs = jnp.zeros((TILE, lanes), F32)
     if late:
         logs = extra[0, base * ROWS_DEV :].astype(F32)
         out[:, : base * ROWS_DEV] = extra[:, : base * ROWS_DEV]
-        for k in range(N_CHOL):
+        for owner, part in zip(owners, parts):
+            share = pl.ds(pl.multiple_of(owner * TILE, TILE), TILE)
             for q in range(2):
-                rows = parts[k, q * stride + ORBS : (q + 1) * stride]
-                minv[q, k * TILE : (k + 1) * TILE] = rows
+                minv[q, share] = part[q * stride + ORBS : (q + 1) * stride]
     phi = jnp.concatenate(
         [
-            jnp.concatenate([parts[k, q * stride : q * stride + ORBS] for q in range(2)], axis=1)
-            for k in range(N_CHOL)
+            jnp.concatenate([part[q * stride : q * stride + ORBS] for q in range(2)], axis=1)
+            for part in parts
         ],
         axis=0,
     )
     products = []
     for g in range(chol.shape[0]):
-        products.append(jnp.dot(chol[g], phi, preferred_element_type=F32))
+        rows = chol[g]
+        if late:
+            rows = jnp.concatenate([chol[g, :, spot] for spot in columns], axis=1)
+        products.append(jnp.dot(rows, phi, preferred_element_type=F32))
     for q in range(2):
         weighted = lax.dot_general(
             trial[...],
@@ -193,25 +221,27 @@
 
     return pl.pallas_call(
         body,
-        in_specs=[WHOLE] * 5,
+        in_specs=[WHOLE] * (4 + len(parts)),
         out_specs=WHOLE,
         out_shape=jax.ShapeDtypeStruct((N_CHOL, out_rows, lanes), BF16),
         scratch_shapes=[pltpu.VMEM((2, lanes, lanes), BF16)],
         compiler_params=params(24),
         name="late_products" if late else "early_products",
         cost_estimate=pl.CostEstimate(flops=flops, bytes_accessed=6 << 20, transcendentals=0),
-    )(x, cholesky, trial, extra, parts)
-
-
-def finish_kernel(plan, got, early, late, out, log_out):
-    own, arriving = plan[1:2], plan[2:3]
+    )(x, cholesky, trial, extra, *parts)
+
+
+def finish_kernel(x, got, early, late, out, log_out):
+    own, arriving = x[OWN : OWN + 1], x[ARRIVING : ARRIVING + 1]
     tile = jnp.zeros((TILE, got.shape[2]), F32)
     for k in range(N_CHOL):
         tile += got[k, LIVE * ROWS_DEV :].astype(F32)
     walkers, logs = [], []
     for spot in range(LIVE):
-        block, first = (early, spot * ORBS) if spot < 2 else (late, (spot - 2) * STRIDE)
-        total = block[0, first : first + ROWS_DEV].astype(F32)
+        if spot < 2:
+            total = early[0, spot * ORBS : spot * ORBS + ROWS_DEV].astype(F32)
+        else:
+            total = late[(spot - 2) * STRIDE : (spot - 2) * STRIDE + ROWS_DEV].astype(F32)
         for k in range(N_CHOL):
             total += got[k, spot * ROWS_DEV : (spot + 1) * ROWS_DEV].astype(F32)
         walkers.append(total)
@@ -229,7 +259,7 @@
                 log_out[slot] = jnp.sum(value)
 
 
-def finish_call(plan, got, early, late):
+def finish_call(x, got, early, late):
     lanes = got.shape[2]
     return pl.pallas_call(
         finish_kernel,
@@ -241,13 +271,13 @@
         ),
         compiler_params=params(8),
         name="finish",
-    )(plan, got, early, late)
+    )(x, got, early, late)
 
 
 def shards(walkers, inv_intersection, fields, cholesky, trial_rows, counts, partner):
     walk_size = lax.axis_size("walk")
     fields = fields.T
-    outgoing, early, kept, plan = pack_call(
+    outgoing, early, kept = pack_call(
         counts, partner, walkers, inv_intersection, fields
     )
     early_parts = gather(early)
@@ -255,14 +285,14 @@
     for bit in range(walk_size.bit_length() - 1):
         route = [(i, i ^ 1 << bit) for i in range(walk_size)]
         received.append(lax.ppermute(outgoing, "walk", route))
-    late, x = merge_call(plan, outgoing, kept, received)
-    late_parts = gather(late)
+    late, x = merge_call(kept, received)
+    late_parts = gather_in_two(late)
     first = product_call(
-        False, fields, cholesky, trial_rows, inv_intersection, early_parts
+        False, fields, cholesky, trial_rows, inv_intersection, [early_parts]
     )
     sums = product_call(True, x, cholesky, trial_rows, first, late_parts)
     sums = lax.all_to_all(sums, "chol", 0, 0, tiled=True)
-    return tuple(finish_call(plan, sums, early, late))
+    return tuple(finish_call(x, sums, early[:1], late))
 
 
 def solution(mesh):

time: 127 us -> 121 us (0.953)
  the two profiles are of different devices: /device:TPU:1 before, /device:TPU:4 now
where the time goes in v5:
time: 121 us; the launch traced here: 120 us
  starting transfers between devices  78.5 us (65%)
  waiting for transfers between devices  24.8 us (20%)
  Pallas kernels  9.04 us (7%)
  local copies, waits for them, and re-layouts  6.49 us (5%)
    ppermute x7, starting transfers between devices, shards(): received.append(lax.ppermute(outgoing, 'walk', route))  41.5 us
    ppermute x7, starting transfers between devices, shift(): return lax.ppermute(value, 'chol', route)  24.8 us
    all_to_all x1, waiting for transfers between devices, shards(): sums = lax.all_to_all(sums, 'chol', 0, 0, tiled=True)  16.8 us
    ppermute x7, waiting for transfers between devices, shards(): received.append(lax.ppermute(outgoing, 'walk', route))  7.19 us
    all_to_all x1, starting transfers between devices, gather(): return lax.all_to_all(copies, 'chol', 0, 0, tiled=True)  7.15 us
    unnamed x12, local copies, waits for them, and re-layouts  5.58 us
    all_to_all x1, starting transfers between devices, shards(): sums = lax.all_to_all(sums, 'chol', 0, 0, tiled=True)  5.09 us
    pallas_call x2, Pallas kernels, product_call(): pl.pallas_call(body, in_specs=[WHOLE] * (4 + len(parts)), out_specs=WHOLE...  4.56 us
  transfers between devices with their start and end apart: 16, of which 4 were waited for; matrix products, arithmetic and copies ran while one was open for 1% of the time, Pallas kernels for 2%

profile of v5, /device:TPU:4, one launch (start us, length us, event | category | flops | bytes accessed | tf_op | source)
XLA Modules:
  0.0 119.8 jit_solution(6071471488717842738)
XLA Ops:
  0.6 3.6 %pack.1 = (bf16[560,128]{1,0:T(8,128)(2,1)}, bf16[8,512,128]{2,1,0:T(8,128)(2,1)}, bf16[560,128]{1,0:T(8,128)(2,1)}) custom-call(s32[128]{0:T(128)} %counts.1, s32[128]{0:T(128)} %partner.1, bf16[6,256,128]{2,1,0:T(8,128)(2,1)} %walkers.1, bf16[6,128,128]{2,1,0:T(8,128)(2,1)} %refs_3_.1, bf16[2,6]{1,0:T(2,128)(2,1)} %bitcast.1), custom_call_target="tpu_custom_call" | custom-call | tf_op jit(solution)/shard_map/pack/pallas_call | solution.py:91
  4.2 7.1 %all-to-all-start = ((bf16[8,512,128]{2,1,0:T(8,128)(2,1)}), bf16[8,512,128]{2,1,0:T(8,128)(2,1)S(1)}, u32[]{:S(2)}, u32[]{:S(2)}) async-start(bf16[8,512,128]{2,1,0:T(8,128)(2,1)} %get-tuple-element.10), calls=%async_computation | async-start | bytes 2097152 | tf_op jit(solution)/shard_map/all_to_all | solution.py:35
  11.4 19.3 %collective-permute-start.6 = (bf16[560,128]{1,0:T(8,128)(2,1)}, bf16[560,128]{1,0:T(8,128)(2,1)S(1)}, u32[]{:S(2)}, u32[]{:S(2)}) collective-permute-start(bf16[560,128]{1,0:T(8,128)(2,1)} %get-tuple-element.8), channel_id=1, source_target_pairs={{0,512},{8,520},{16,528},{24,536},{32,544},{40,552},{48,560},{56,5... | collective-permute-start | bytes 430088 | tf_op jit(solution)/shard_map/ppermute | solution.py:287
  30.7 6.1 %collective-permute-start.5 = (bf16[560,128]{1,0:T(8,128)(2,1)}, bf16[560,128]{1,0:T(8,128)(2,1)S(1)}, u32[]{:S(2)}, u32[]{:S(2)}) collective-permute-start(bf16[560,128]{1,0:T(8,128)(2,1)} %get-tuple-element.8), channel_id=1, source_target_pairs={{0,256},{8,264},{16,272},{24,280},{32,288},{40,296},{48,304},{56,3... | collective-permute-start | bytes 430088 | tf_op jit(solution)/shard_map/ppermute | solution.py:287
  36.8 4.3 %collective-permute-start.4 = (bf16[560,128]{1,0:T(8,128)(2,1)}, bf16[560,128]{1,0:T(8,128)(2,1)S(1)}, u32[]{:S(2)}, u32[]{:S(2)}) collective-permute-start(bf16[560,128]{1,0:T(8,128)(2,1)} %get-tuple-element.8), channel_id=1, source_target_pairs={{0,128},{8,136},{16,144},{24,152},{32,160},{40,168},{48,176},{56,1... | collective-permute-start | bytes 430088 | tf_op jit(solution)/shard_map/ppermute | solution.py:287
  41.1 3.4 %collective-permute-start.3 = (bf16[560,128]{1,0:T(8,128)(2,1)}, bf16[560,128]{1,0:T(8,128)(2,1)S(1)}, u32[]{:S(2)}, u32[]{:S(2)}) collective-permute-start(bf16[560,128]{1,0:T(8,128)(2,1)} %get-tuple-element.8), channel_id=1, source_target_pairs={{0,64},{8,72},{16,80},{24,88},{32,96},{40,104},{48,112},{56,120},{... | collective-permute-start | bytes 430088 | tf_op jit(solution)/shard_map/ppermute | solution.py:287
  44.5 2.4 %collective-permute-start.2 = (bf16[560,128]{1,0:T(8,128)(2,1)}, bf16[560,128]{1,0:T(8,128)(2,1)S(1)}, u32[]{:S(2)}, u32[]{:S(2)}) collective-permute-start(bf16[560,128]{1,0:T(8,128)(2,1)} %get-tuple-element.8), channel_id=1, source_target_pairs={{0,32},{8,40},{16,48},{24,56},{32,0},{40,8},{48,16},{56,24},{64,96... | collective-permute-start | bytes 430088 | tf_op jit(solution)/shard_map/ppermute | solution.py:287
  46.9 0.0 collective-permute-done.6.refs_7_
  47.0 4.0 %collective-permute-start.1 = (bf16[560,128]{1,0:T(8,128)(2,1)}, bf16[560,128]{1,0:T(8,128)(2,1)S(1)}, u32[]{:S(2)}, u32[]{:S(2)}) collective-permute-start(bf16[560,128]{1,0:T(8,128)(2,1)} %get-tuple-element.8), channel_id=1, source_target_pairs={{0,16},{8,24},{16,0},{24,8},{32,48},{40,56},{48,32},{56,40},{64,80... | collective-permute-start | bytes 430088 | tf_op jit(solution)/shard_map/ppermute | solution.py:287
  51.0 5.7 %collective-permute-done.5.refs_6_ = bf16[560,128]{1,0:T(8,128)(2,1)S(1)} collective-permute-done((bf16[560,128]{1,0:T(8,128)(2,1)}, bf16[560,128]{1,0:T(8,128)(2,1)S(1)}, u32[]{:S(2)}, u32[]{:S(2)}) %collective-permute-start.5) | collective-permute-done | bytes 143392 | tf_op jit(solution)/shard_map/ppermute | solution.py:287
  56.6 1.9 %collective-permute-start = (bf16[560,128]{1,0:T(8,128)(2,1)}, bf16[560,128]{1,0:T(8,128)(2,1)S(1)}, u32[]{:S(2)}, u32[]{:S(2)}) collective-permute-start(bf16[560,128]{1,0:T(8,128)(2,1)} %get-tuple-element.8), channel_id=1, source_target_pairs={{0,8},{8,0},{16,24},{24,16},{32,40},{40,32},{48,56},{56,48},{64,72... | collective-permute-start | bytes 430088 | tf_op jit(solution)/shard_map/ppermute | solution.py:287
  58.6 0.0 collective-permute-done.4.refs_5_
  58.6 0.0 collective-permute-done.3.refs_4_
  58.6 0.0 collective-permute-done.2.refs_3_
  58.6 0.0 collective-permute-done.1.refs_2_
  58.6 1.5 %collective-permute-done.refs_1_ = bf16[560,128]{1,0:T(8,128)(2,1)S(1)} collective-permute-done((bf16[560,128]{1,0:T(8,128)(2,1)}, bf16[560,128]{1,0:T(8,128)(2,1)S(1)}, u32[]{:S(2)}, u32[]{:S(2)}) %collective-permute-start) | collective-permute-done | bytes 143392 | tf_op jit(solution)/shard_map/ppermute | solution.py:287
  60.1 0.0 copy-start.4
  60.1 0.9 copy-done.4
  61.0 0.2 merge.1
  61.2 5.7 %collective-permute-start.10 = (bf16[544,128]{1,0:T(8,128)(2,1)S(1)}, bf16[544,128]{1,0:T(8,128)(2,1)S(1)}, u32[]{:S(2)}, u32[]{:S(2)}) collective-permute-start(bf16[544,128]{1,0:T(8,128)(2,1)S(1)} %get-tuple-element.11.refs_4_.late), channel_id=1, source_target_pairs={{0,6},{1,7},{2,0},{3,1},{4,2},{5,3},{6,4},{7,5},{8,14},{9,15},{10,... | collective-permute-start | bytes 417800 | tf_op jit(solution)/shard_map/ppermute | solution.py:41
  66.9 1.9 %collective-permute-start.9 = (bf16[544,128]{1,0:T(8,128)(2,1)S(1)}, bf16[544,128]{1,0:T(8,128)(2,1)S(1)}, u32[]{:S(2)}, u32[]{:S(2)}) collective-permute-start(bf16[544,128]{1,0:T(8,128)(2,1)S(1)} %get-tuple-element.11.refs_4_.late), channel_id=1, source_target_pairs={{0,2},{1,3},{2,4},{3,5},{4,6},{5,7},{6,0},{7,1},{8,10},{9,11},{10,... | collective-permute-start | bytes 417800 | tf_op jit(solution)/shard_map/ppermute | solution.py:41
  68.8 5.1 %collective-permute-start.8 = (bf16[544,128]{1,0:T(8,128)(2,1)S(1)}, bf16[544,128]{1,0:T(8,128)(2,1)S(1)}, u32[]{:S(2)}, u32[]{:S(2)}) collective-permute-start(bf16[544,128]{1,0:T(8,128)(2,1)S(1)} %get-tuple-element.11.refs_4_.late), channel_id=1, source_target_pairs={{0,7},{1,0},{2,1},{3,2},{4,3},{5,4},{6,5},{7,6},{8,15},{9,8},{10,9... | collective-permute-start | bytes 417800 | tf_op jit(solution)/shard_map/ppermute | solution.py:41
  74.0 1.9 %collective-permute-start.7 = (bf16[544,128]{1,0:T(8,128)(2,1)S(1)}, bf16[544,128]{1,0:T(8,128)(2,1)S(1)}, u32[]{:S(2)}, u32[]{:S(2)}) collective-permute-start(bf16[544,128]{1,0:T(8,128)(2,1)S(1)} %get-tuple-element.11.refs_4_.late), channel_id=1, source_target_pairs={{0,1},{1,2},{2,3},{3,4},{4,5},{5,6},{6,7},{7,0},{8,9},{9,10},{10,1... | collective-permute-start | bytes 417800 | tf_op jit(solution)/shard_map/ppermute | solution.py:41
  75.9 0.0 collective-permute-done.10.refs_8_
  75.9 5.1 %collective-permute-start.12 = (bf16[544,128]{1,0:T(8,128)(2,1)S(1)}, bf16[544,128]{1,0:T(8,128)(2,1)S(1)}, u32[]{:S(2)}, u32[]{:S(2)}) collective-permute-start(bf16[544,128]{1,0:T(8,128)(2,1)S(1)} %collective-permute-done.10.refs_8_), channel_id=1, source_target_pairs={{0,7},{1,0},{2,1},{3,2},{4,3},{5,4},{6,5},{7,6},{8,15},{9,8},{10,9... | collective-permute-start | bytes 417800 | tf_op jit(solution)/shard_map/ppermute | solution.py:41
  81.1 0.0 collective-permute-done.9.refs_7_
  81.1 1.9 %collective-permute-start.13 = (bf16[544,128]{1,0:T(8,128)(2,1)S(1)}, bf16[544,128]{1,0:T(8,128)(2,1)S(1)}, u32[]{:S(2)}, u32[]{:S(2)}) collective-permute-start(bf16[544,128]{1,0:T(8,128)(2,1)S(1)} %collective-permute-done.9.refs_7_), channel_id=1, source_target_pairs={{0,2},{1,3},{2,4},{3,5},{4,6},{5,7},{6,0},{7,1},{8,10},{9,11},{10,... | collective-permute-start | bytes 417800 | tf_op jit(solution)/shard_map/ppermute | solution.py:41
  83.0 3.1 %collective-permute-start.11 = (bf16[544,128]{1,0:T(8,128)(2,1)S(1)}, bf16[544,128]{1,0:T(8,128)(2,1)S(1)}, u32[]{:S(2)}, u32[]{:S(2)}) collective-permute-start(bf16[544,128]{1,0:T(8,128)(2,1)S(1)} %collective-permute-done.9.refs_7_), channel_id=1, source_target_pairs={{0,1},{1,2},{2,3},{3,4},{4,5},{5,6},{6,7},{7,0},{8,9},{9,10},{10,1... | collective-permute-start | bytes 417800 | tf_op jit(solution)/shard_map/ppermute | solution.py:41
  86.1 0.0 all-to-all-done.refs_4_
  86.1 0.0 copy-start
  86.1 2.2 %copy-done = bf16[2,512,2048]{2,1,0:T(8,128)(2,1)S(1)} copy-done((bf16[2,512,2048]{2,1,0:T(8,128)(2,1)S(1)}, bf16[2,512,2048]{2,1,0:T(8,128)(2,1)}, u32[]{:S(2)}) %copy-start) | copy-done | bytes 4194328
  88.3 0.0 copy-start.2
  88.3 0.9 copy-done.2
  89.2 0.0 copy-start.3
  89.2 0.9 copy-done.3
  90.1 0.7 copy-done.5
  90.8 1.9 %early_products.1.refs_3_ = bf16[8,144,128]{2,1,0:T(8,128)(2,1)S(1)} custom-call(bf16[2,6]{1,0:T(2,128)(2,1)S(1)} %bitcast.2, bf16[2,512,2048]{2,1,0:T(8,128)(2,1)S(1)} %copy-done, bf16[512,128]{1,0:T(8,128)(2,1)S(1)} %copy-done.3, bf16[6,128,128]{2,1,0:T(8,128)(2,1)S(1)} %copy-done.2, bf16[8,512,128]{2,1,0:T(8,128)(2,1)S(1)} %all-to-all-done.refs_4_), custom_call_target="tpu_custom_call" | custom-call | flops 1073741824 | bytes 6291456 | tf_op jit(solution)/shard_map/early_products/pallas_call | solution.py:222
  92.6 0.0 collective-permute-done.8.refs_6_
  92.6 0.0 collective-permute-done.7.refs_5_
  92.7 0.0 collective-permute-done.12.refs_10_
  92.7 0.0 collective-permute-done.13.refs_11_
  92.7 0.9 collective-permute-done.11.refs_9_
  93.6 0.0 copy-done.1
  93.6 2.7 %late_products.1 = bf16[8,272,128]{2,1,0:T(8,128)(2,1)} custom-call(f32[16,128]{1,0:T(8,128)S(1)} %get-tuple-element.9.refs_0_.x, bf16[2,512,2048]{2,1,0:T(8,128)(2,1)S(1)} %copy-done.1, bf16[512,128]{1,0:T(8,128)(2,1)S(1)} %copy-done.3, bf16[8,144,128]{2,1,0:T(8,128)(2,1)S(1)} %early_products.1.refs_3_, ...), custom_call_target="tpu_custom_call" | custom-call | flops 1073741824 | bytes 6291456 | tf_op jit(solution)/shard_map/late_products/pallas_call | solution.py:222
  96.3 5.1 %all-to-all-start.1 = ((bf16[8,272,128]{2,1,0:T(8,128)(2,1)}), bf16[8,272,128]{2,1,0:T(8,128)(2,1)S(1)}, u32[]{:S(2)}, u32[]{:S(2)}) async-start(bf16[8,272,128]{2,1,0:T(8,128)(2,1)} %late_products.1), calls=%async_computation.1 | async-start | bytes 1114112 | tf_op jit(solution)/shard_map/all_to_all | solution.py:294
  101.3 0.9 slice.3.early
  102.3 16.8 %all-to-all-done.1.got = bf16[8,272,128]{2,1,0:T(8,128)(2,1)S(1)} async-done(((bf16[8,272,128]{2,1,0:T(8,128)(2,1)}), bf16[8,272,128]{2,1,0:T(8,128)(2,1)S(1)}, u32[]{:S(2)}, u32[]{:S(2)}) %all-to-all-start.1) | async-done | bytes 557088 | tf_op jit(solution)/shard_map/all_to_all | solution.py:294
  119.0 0.7 finish.1
  (2 shorter events, 0.0 us)
Async XLA Ops:
  4.2 81.9 %all-to-all-start = ((bf16[8,512,128]{2,1,0:T(8,128)(2,1)}), bf16[8,512,128]{2,1,0:T(8,128)(2,1)S(1)}, u32[]{:S(2)}, u32[]{:S(2)}) async-start(bf16[8,512,128]{2,1,0:T(8,128)(2,1)} %get-tuple-element.10), calls=%async_computation | async-start | bytes 2097152 | tf_op jit(solution)/shard_map/all_to_all | solution.py:35
  11.4 35.6 %collective-permute-start.6 = (bf16[560,128]{1,0:T(8,128)(2,1)}, bf16[560,128]{1,0:T(8,128)(2,1)S(1)}, u32[]{:S(2)}, u32[]{:S(2)}) collective-permute-start(bf16[560,128]{1,0:T(8,128)(2,1)} %get-tuple-element.8), channel_id=1, source_target_pairs={{0,512},{8,520},{16,528},{24,536},{32,544},{40,552},{48,560},{56,5... | collective-permute-start | bytes 430088 | tf_op jit(solution)/shard_map/ppermute | solution.py:287
  30.7 25.9 %collective-permute-start.5 = (bf16[560,128]{1,0:T(8,128)(2,1)}, bf16[560,128]{1,0:T(8,128)(2,1)S(1)}, u32[]{:S(2)}, u32[]{:S(2)}) collective-permute-start(bf16[560,128]{1,0:T(8,128)(2,1)} %get-tuple-element.8), channel_id=1, source_target_pairs={{0,256},{8,264},{16,272},{24,280},{32,288},{40,296},{48,304},{56,3... | collective-permute-start | bytes 430088 | tf_op jit(solution)/shard_map/ppermute | solution.py:287
  36.8 21.7 %collective-permute-start.4 = (bf16[560,128]{1,0:T(8,128)(2,1)}, bf16[560,128]{1,0:T(8,128)(2,1)S(1)}, u32[]{:S(2)}, u32[]{:S(2)}) collective-permute-start(bf16[560,128]{1,0:T(8,128)(2,1)} %get-tuple-element.8), channel_id=1, source_target_pairs={{0,128},{8,136},{16,144},{24,152},{32,160},{40,168},{48,176},{56,1... | collective-permute-start | bytes 430088 | tf_op jit(solution)/shard_map/ppermute | solution.py:287
  41.1 17.4 %collective-permute-start.3 = (bf16[560,128]{1,0:T(8,128)(2,1)}, bf16[560,128]{1,0:T(8,128)(2,1)S(1)}, u32[]{:S(2)}, u32[]{:S(2)}) collective-permute-start(bf16[560,128]{1,0:T(8,128)(2,1)} %get-tuple-element.8), channel_id=1, source_target_pairs={{0,64},{8,72},{16,80},{24,88},{32,96},{40,104},{48,112},{56,120},{... | collective-permute-start | bytes 430088 | tf_op jit(solution)/shard_map/ppermute | solution.py:287
  44.5 14.1 %collective-permute-start.2 = (bf16[560,128]{1,0:T(8,128)(2,1)}, bf16[560,128]{1,0:T(8,128)(2,1)S(1)}, u32[]{:S(2)}, u32[]{:S(2)}) collective-permute-start(bf16[560,128]{1,0:T(8,128)(2,1)} %get-tuple-element.8), channel_id=1, source_target_pairs={{0,32},{8,40},{16,48},{24,56},{32,0},{40,8},{48,16},{56,24},{64,96... | collective-permute-start | bytes 430088 | tf_op jit(solution)/shard_map/ppermute | solution.py:287
  47.0 11.6 %collective-permute-start.1 = (bf16[560,128]{1,0:T(8,128)(2,1)}, bf16[560,128]{1,0:T(8,128)(2,1)S(1)}, u32[]{:S(2)}, u32[]{:S(2)}) collective-permute-start(bf16[560,128]{1,0:T(8,128)(2,1)} %get-tuple-element.8), channel_id=1, source_target_pairs={{0,16},{8,24},{16,0},{24,8},{32,48},{40,56},{48,32},{56,40},{64,80... | collective-permute-start | bytes 430088 | tf_op jit(solution)/shard_map/ppermute | solution.py:287
  56.6 3.5 %collective-permute-start = (bf16[560,128]{1,0:T(8,128)(2,1)}, bf16[560,128]{1,0:T(8,128)(2,1)S(1)}, u32[]{:S(2)}, u32[]{:S(2)}) collective-permute-start(bf16[560,128]{1,0:T(8,128)(2,1)} %get-tuple-element.8), channel_id=1, source_target_pairs={{0,8},{8,0},{16,24},{24,16},{32,40},{40,32},{48,56},{56,48},{64,72... | collective-permute-start | bytes 430088 | tf_op jit(solution)/shard_map/ppermute | solution.py:287
  60.1 0.9 copy-start.4
  61.2 14.7 %collective-permute-start.10 = (bf16[544,128]{1,0:T(8,128)(2,1)S(1)}, bf16[544,128]{1,0:T(8,128)(2,1)S(1)}, u32[]{:S(2)}, u32[]{:S(2)}) collective-permute-start(bf16[544,128]{1,0:T(8,128)(2,1)S(1)} %get-tuple-element.11.refs_4_.late), channel_id=1, source_target_pairs={{0,6},{1,7},{2,0},{3,1},{4,2},{5,3},{6,4},{7,5},{8,14},{9,15},{10,... | collective-permute-start | bytes 417800 | tf_op jit(solution)/shard_map/ppermute | solution.py:41
  66.9 14.2 %collective-permute-start.9 = (bf16[544,128]{1,0:T(8,128)(2,1)S(1)}, bf16[544,128]{1,0:T(8,128)(2,1)S(1)}, u32[]{:S(2)}, u32[]{:S(2)}) collective-permute-start(bf16[544,128]{1,0:T(8,128)(2,1)S(1)} %get-tuple-element.11.refs_4_.late), channel_id=1, source_target_pairs={{0,2},{1,3},{2,4},{3,5},{4,6},{5,7},{6,0},{7,1},{8,10},{9,11},{10,... | collective-permute-start | bytes 417800 | tf_op jit(solution)/shard_map/ppermute | solution.py:41
  68.8 23.8 %collective-permute-start.8 = (bf16[544,128]{1,0:T(8,128)(2,1)S(1)}, bf16[544,128]{1,0:T(8,128)(2,1)S(1)}, u32[]{:S(2)}, u32[]{:S(2)}) collective-permute-start(bf16[544,128]{1,0:T(8,128)(2,1)S(1)} %get-tuple-element.11.refs_4_.late), channel_id=1, source_target_pairs={{0,7},{1,0},{2,1},{3,2},{4,3},{5,4},{6,5},{7,6},{8,15},{9,8},{10,9... | collective-permute-start | bytes 417800 | tf_op jit(solution)/shard_map/ppermute | solution.py:41
  74.0 18.7 %collective-permute-start.7 = (bf16[544,128]{1,0:T(8,128)(2,1)S(1)}, bf16[544,128]{1,0:T(8,128)(2,1)S(1)}, u32[]{:S(2)}, u32[]{:S(2)}) collective-permute-start(bf16[544,128]{1,0:T(8,128)(2,1)S(1)} %get-tuple-element.11.refs_4_.late), channel_id=1, source_target_pairs={{0,1},{1,2},{2,3},{3,4},{4,5},{5,6},{6,7},{7,0},{8,9},{9,10},{10,1... | collective-permute-start | bytes 417800 | tf_op jit(solution)/shard_map/ppermute | solution.py:41
  75.9 16.7 %collective-permute-start.12 = (bf16[544,128]{1,0:T(8,128)(2,1)S(1)}, bf16[544,128]{1,0:T(8,128)(2,1)S(1)}, u32[]{:S(2)}, u32[]{:S(2)}) collective-permute-start(bf16[544,128]{1,0:T(8,128)(2,1)S(1)} %collective-permute-done.10.refs_8_), channel_id=1, source_target_pairs={{0,7},{1,0},{2,1},{3,2},{4,3},{5,4},{6,5},{7,6},{8,15},{9,8},{10,9... | collective-permute-start | bytes 417800 | tf_op jit(solution)/shard_map/ppermute | solution.py:41
  81.1 11.6 %collective-permute-start.13 = (bf16[544,128]{1,0:T(8,128)(2,1)S(1)}, bf16[544,128]{1,0:T(8,128)(2,1)S(1)}, u32[]{:S(2)}, u32[]{:S(2)}) collective-permute-start(bf16[544,128]{1,0:T(8,128)(2,1)S(1)} %collective-permute-done.9.refs_7_), channel_id=1, source_target_pairs={{0,2},{1,3},{2,4},{3,5},{4,6},{5,7},{6,0},{7,1},{8,10},{9,11},{10,... | collective-permute-start | bytes 417800 | tf_op jit(solution)/shard_map/ppermute | solution.py:41
  83.0 10.6 %collective-permute-start.11 = (bf16[544,128]{1,0:T(8,128)(2,1)S(1)}, bf16[544,128]{1,0:T(8,128)(2,1)S(1)}, u32[]{:S(2)}, u32[]{:S(2)}) collective-permute-start(bf16[544,128]{1,0:T(8,128)(2,1)S(1)} %collective-permute-done.9.refs_7_), channel_id=1, source_target_pairs={{0,1},{1,2},{2,3},{3,4},{4,5},{5,6},{6,7},{7,0},{8,9},{9,10},{10,1... | collective-permute-start | bytes 417800 | tf_op jit(solution)/shard_map/ppermute | solution.py:41
  86.1 2.2 %copy-start = (bf16[2,512,2048]{2,1,0:T(8,128)(2,1)S(1)}, bf16[2,512,2048]{2,1,0:T(8,128)(2,1)}, u32[]{:S(2)}) copy-start(bf16[2,512,2048]{2,1,0:T(8,128)(2,1)} %refs_1_.3) | copy-start | bytes 12582916
  88.3 0.9 copy-start.2
  89.2 0.9 copy-start.3
  90.1 0.7 copy-start.5
  90.8 2.8 %copy-start.1 = (bf16[2,512,2048]{2,1,0:T(8,128)(2,1)S(1)}, bf16[2,512,2048]{2,1,0:T(8,128)(2,1)}, u32[]{:S(2)}) copy-start(bf16[2,512,2048]{2,1,0:T(8,128)(2,1)} %refs_1_.3) | copy-start | bytes 12582916
  96.3 22.8 %all-to-all-start.1 = ((bf16[8,272,128]{2,1,0:T(8,128)(2,1)}), bf16[8,272,128]{2,1,0:T(8,128)(2,1)S(1)}, u32[]{:S(2)}, u32[]{:S(2)}) async-start(bf16[8,272,128]{2,1,0:T(8,128)(2,1)} %late_products.1), calls=%async_computation.1 | async-start | bytes 1114112 | tf_op jit(solution)/shard_map/all_to_all | solution.py:294

commit v6 on v5

--- a/solution.py
+++ b/solution.py
@@ -129,7 +129,7 @@
     for q in range(2):
         mask = (own[:, q : q + 1] > 2 + q) | (row_id >= DISTANCE)
         column = jnp.where(mask, tile[:, 2 + q : 3 + q], theirs[:, LIVE + 1 - q : LIVE + 2 - q])
-        x[:, q : q + 1] = column
+        x[:, 2 + q : 3 + q] = column
 
 
 def merge_call(kept, received):
@@ -151,84 +151,87 @@
     )(kept, *received)
 
 
-def product_kernel(late, x, chol, trial, extra, *refs):
-    parts, (out, minv) = refs[:-2], refs[-2:]
+def product_kernel(x, chol, trial, inv, early, *refs):
+    parts, (out, vectors, products, minv, sems) = refs[:N_CHOL], refs[N_CHOL:]
     lanes = out.shape[2]
-    stride, base = (STRIDE, 2) if late else (ORBS, 0)
-    if late:
-        me = lax.axis_index("chol")
-        owners = [jnp.bitwise_and(me + offset, N_CHOL - 1) for offset in OFFSETS]
-        columns = [pl.ds(pl.multiple_of(owner * ORBS, ORBS), ORBS) for owner in owners]
-    else:
-        parts = [parts[0].at[k] for k in range(N_CHOL)]
+    half = chol.shape[1] // 2
+    copies = []
+    for g in range(chol.shape[0]):
+        for h in range(2):
+            rows = pl.ds(h * half, half)
+            copies.append(
+                pltpu.make_async_copy(chol.at[g, rows], vectors.at[g, rows], sems.at[g, h])
+            )
+    for copy in copies:
+        copy.start()
+    me = lax.axis_index("chol")
+    owners = [jnp.bitwise_and(me + offset, N_CHOL - 1) for offset in OFFSETS]
+    columns = [pl.ds(pl.multiple_of(owner * ORBS, ORBS), ORBS) for owner in owners]
+    for owner, part in zip(owners, parts):
+        share = pl.ds(pl.multiple_of(owner * TILE, TILE), TILE)
+        for q in range(2):
+            minv[q, share] = part[q * STRIDE + ORBS : (q + 1) * STRIDE]
+
+    def side_by_side(block, stride):
+        return jnp.concatenate([block[q * stride : q * stride + ORBS] for q in range(2)], axis=1)
+
+    first = jnp.concatenate([side_by_side(early.at[k], ORBS) for k in range(N_CHOL)], axis=0)
+    second = jnp.concatenate([side_by_side(part, STRIDE) for part in parts], axis=0)
+    for g in range(chol.shape[0]):
+        for h in range(2):
+            copies[2 * g + h].wait()
+            rows = slice(h * half, (h + 1) * half)
+            products[0, g, rows] = jnp.dot(vectors[g, rows], first, preferred_element_type=F32)
+            turned = jnp.concatenate([vectors[g, rows, spot] for spot in columns], axis=1)
+            products[1, g, rows] = jnp.dot(turned, second, preferred_element_type=F32)
     row_id = lax.broadcasted_iota(jnp.int32, (TILE, lanes), 0)
     lane_id = lax.broadcasted_iota(jnp.int32, (TILE, lanes), 1)
     logs = jnp.zeros((TILE, lanes), F32)
-    if late:
-        logs = extra[0, base * ROWS_DEV :].astype(F32)
-        out[:, : base * ROWS_DEV] = extra[:, : base * ROWS_DEV]
-        for owner, part in zip(owners, parts):
-            share = pl.ds(pl.multiple_of(owner * TILE, TILE), TILE)
-            for q in range(2):
-                minv[q, share] = part[q * stride + ORBS : (q + 1) * stride]
-    phi = jnp.concatenate(
-        [
-            jnp.concatenate([part[q * stride : q * stride + ORBS] for q in range(2)], axis=1)
-            for part in parts
-        ],
-        axis=0,
-    )
-    products = []
-    for g in range(chol.shape[0]):
-        rows = chol[g]
-        if late:
-            rows = jnp.concatenate([chol[g, :, spot] for spot in columns], axis=1)
-        products.append(jnp.dot(rows, phi, preferred_element_type=F32))
-    for q in range(2):
+    for slot in range(LIVE):
+        pair, q = divmod(slot, 2)
         weighted = lax.dot_general(
             trial[...],
-            minv[q] if late else extra[q],
+            minv[q] if pair else inv[q],
             (((1,), (1,)), ((), ())),
             preferred_element_type=F32,
         )
         total = jnp.zeros_like(weighted)
         log = jnp.zeros((1, 1), F32)
-        for g, both in enumerate(products):
-            product = both[:, q * lanes : (q + 1) * lanes]
+        for g in range(chol.shape[0]):
+            product = products[pair, g, :, q * lanes : (q + 1) * lanes]
             bias = -STEP_ROOT * jnp.sum(product * weighted, keepdims=True)
-            field = x[g : g + 1, q : q + 1].astype(F32)
+            field = x[g : g + 1, slot : slot + 1]
             total += STEP_ROOT * (field - bias) * product
             log += field * bias - 0.5 * bias * bias
         spread = total.astype(BF16).reshape(N_CHOL, ROWS_DEV, lanes)
-        slot = base + q
         out[:, slot * ROWS_DEV : (slot + 1) * ROWS_DEV] = spread
         high = log.astype(BF16).astype(F32)
         here = row_id == slot
         logs = jnp.where(here & (lane_id == 0), high, logs)
         logs = jnp.where(here & (lane_id == 1), log - high, logs)
     for k in range(N_CHOL):
-        out[k, (base + 2) * ROWS_DEV :] = logs.astype(BF16)
-
-
-def product_call(late, x, cholesky, trial, extra, parts):
+        out[k, LIVE * ROWS_DEV :] = logs.astype(BF16)
+
+
+def product_call(x, cholesky, trial, inv, early, parts):
     lanes = trial.shape[1]
     vectors, window, orbitals = cholesky.shape
-    flops = 4 * vectors * window * orbitals * lanes
-    out_rows = (LIVE if late else 2) * ROWS_DEV + TILE
-
-    def body(*refs):
-        product_kernel(late, *refs)
-
+    flops = 2 * LIVE * vectors * window * orbitals * lanes
     return pl.pallas_call(
-        body,
-        in_specs=[WHOLE] * (4 + len(parts)),
+        product_kernel,
+        in_specs=[WHOLE, HBM, WHOLE, WHOLE, WHOLE] + [WHOLE] * len(parts),
         out_specs=WHOLE,
-        out_shape=jax.ShapeDtypeStruct((N_CHOL, out_rows, lanes), BF16),
-        scratch_shapes=[pltpu.VMEM((2, lanes, lanes), BF16)],
-        compiler_params=params(24),
-        name="late_products" if late else "early_products",
+        out_shape=jax.ShapeDtypeStruct((N_CHOL, LIVE * ROWS_DEV + TILE, lanes), BF16),
+        scratch_shapes=[
+            pltpu.VMEM(cholesky.shape, BF16),
+            pltpu.VMEM((2, vectors, window, 2 * lanes), F32),
+            pltpu.VMEM((2, lanes, lanes), BF16),
+            pltpu.SemaphoreType.DMA((vectors, 2)),
+        ],
+        compiler_params=params(48),
+        name="products",
         cost_estimate=pl.CostEstimate(flops=flops, bytes_accessed=6 << 20, transcendentals=0),
-    )(x, cholesky, trial, extra, *parts)
+    )(x, cholesky, trial, inv, early, *parts)
 
 
 def finish_kernel(x, got, early, late, out, log_out):
@@ -287,10 +290,9 @@
         received.append(lax.ppermute(outgoing, "walk", route))
     late, x = merge_call(kept, received)
     late_parts = gather_in_two(late)
-    first = product_call(
-        False, fields, cholesky, trial_rows, inv_intersection, [early_parts]
+    sums = product_call(
+        x, cholesky, trial_rows, inv_intersection, early_parts, late_parts
     )
-    sums = product_call(True, x, cholesky, trial_rows, first, late_parts)
     sums = lax.all_to_all(sums, "chol", 0, 0, tiled=True)
     return tuple(finish_call(x, sums, early[:1], late))
 

time: 121 us -> 126 us (1.041)
  the two profiles are of different devices: /device:TPU:4 before, /device:TPU:6 now
where the time goes in v6:
time: 126 us; the launch traced here: 125 us
  starting transfers between devices  77.2 us (61%)
  waiting for transfers between devices  32.7 us (26%)
  Pallas kernels  10.4 us (8%)
  local copies, waits for them, and re-layouts  3.65 us (3%)
    ppermute x7, starting transfers between devices, shards(): received.append(lax.ppermute(outgoing, 'walk', route))  40.3 us
    ppermute x7, starting transfers between devices, shift(): return lax.ppermute(value, 'chol', route)  24.8 us
    all_to_all x1, waiting for transfers between devices, shards(): sums = lax.all_to_all(sums, 'chol', 0, 0, tiled=True)  16.9 us
    ppermute x7, waiting for transfers between devices, shards(): received.append(lax.ppermute(outgoing, 'walk', route))  8.38 us
    ppermute x7, waiting for transfers between devices, shift(): return lax.ppermute(value, 'chol', route)  7.48 us
    all_to_all x1, starting transfers between devices, gather(): return lax.all_to_all(copies, 'chol', 0, 0, tiled=True)  7.15 us
    pallas_call x1, Pallas kernels, product_call(): pl.pallas_call(product_kernel, in_specs=[WHOLE, HBM, WHOLE, WHOLE, WHOLE]...  5.87 us
    all_to_all x1, starting transfers between devices, shards(): sums = lax.all_to_all(sums, 'chol', 0, 0, tiled=True)  4.99 us
  transfers between devices with their start and end apart: 16, of which 5 were waited for; matrix products, arithmetic and copies ran while one was open for 1% of the time, Pallas kernels for 0%

profile of v6, /device:TPU:6, one launch (start us, length us, event | category | flops | bytes accessed | tf_op | source)
XLA Modules:
  0.0 124.8 jit_solution(16544956387035187640)
XLA Ops:
  0.6 3.6 %pack.1 = (bf16[560,128]{1,0:T(8,128)(2,1)}, bf16[8,512,128]{2,1,0:T(8,128)(2,1)}, bf16[560,128]{1,0:T(8,128)(2,1)}) custom-call(s32[128]{0:T(128)} %counts.1, s32[128]{0:T(128)} %partner.1, bf16[6,256,128]{2,1,0:T(8,128)(2,1)} %walkers.1, bf16[6,128,128]{2,1,0:T(8,128)(2,1)} %inv.3, bf16[2,6]{1,0:T(2,128)(2,1)} %bitcast.1), custom_call_target="tpu_custom_call" | custom-call | tf_op jit(solution)/shard_map/pack/pallas_call | solution.py:91
  4.2 7.1 %all-to-all-start = ((bf16[8,512,128]{2,1,0:T(8,128)(2,1)}), bf16[8,512,128]{2,1,0:T(8,128)(2,1)S(1)}, u32[]{:S(2)}, u32[]{:S(2)}) async-start(bf16[8,512,128]{2,1,0:T(8,128)(2,1)} %get-tuple-element.10), calls=%async_computation | async-start | bytes 2097152 | tf_op jit(solution)/shard_map/all_to_all | solution.py:35
  11.4 19.3 %collective-permute-start.6 = (bf16[560,128]{1,0:T(8,128)(2,1)}, bf16[560,128]{1,0:T(8,128)(2,1)S(1)}, u32[]{:S(2)}, u32[]{:S(2)}) collective-permute-start(bf16[560,128]{1,0:T(8,128)(2,1)} %get-tuple-element.8), channel_id=1, source_target_pairs={{0,512},{8,520},{16,528},{24,536},{32,544},{40,552},{48,560},{56,5... | collective-permute-start | bytes 430088 | tf_op jit(solution)/shard_map/ppermute | solution.py:290
  30.7 6.1 %collective-permute-start.5 = (bf16[560,128]{1,0:T(8,128)(2,1)}, bf16[560,128]{1,0:T(8,128)(2,1)S(1)}, u32[]{:S(2)}, u32[]{:S(2)}) collective-permute-start(bf16[560,128]{1,0:T(8,128)(2,1)} %get-tuple-element.8), channel_id=1, source_target_pairs={{0,256},{8,264},{16,272},{24,280},{32,288},{40,296},{48,304},{56,3... | collective-permute-start | bytes 430088 | tf_op jit(solution)/shard_map/ppermute | solution.py:290
  36.8 4.3 %collective-permute-start.4 = (bf16[560,128]{1,0:T(8,128)(2,1)}, bf16[560,128]{1,0:T(8,128)(2,1)S(1)}, u32[]{:S(2)}, u32[]{:S(2)}) collective-permute-start(bf16[560,128]{1,0:T(8,128)(2,1)} %get-tuple-element.8), channel_id=1, source_target_pairs={{0,128},{8,136},{16,144},{24,152},{32,160},{40,168},{48,176},{56,1... | collective-permute-start | bytes 430088 | tf_op jit(solution)/shard_map/ppermute | solution.py:290
  41.1 3.4 %collective-permute-start.3 = (bf16[560,128]{1,0:T(8,128)(2,1)}, bf16[560,128]{1,0:T(8,128)(2,1)S(1)}, u32[]{:S(2)}, u32[]{:S(2)}) collective-permute-start(bf16[560,128]{1,0:T(8,128)(2,1)} %get-tuple-element.8), channel_id=1, source_target_pairs={{0,64},{8,72},{16,80},{24,88},{32,96},{40,104},{48,112},{56,120},{... | collective-permute-start | bytes 430088 | tf_op jit(solution)/shard_map/ppermute | solution.py:290
  44.5 3.3 %collective-permute-start.2 = (bf16[560,128]{1,0:T(8,128)(2,1)}, bf16[560,128]{1,0:T(8,128)(2,1)S(1)}, u32[]{:S(2)}, u32[]{:S(2)}) collective-permute-start(bf16[560,128]{1,0:T(8,128)(2,1)} %get-tuple-element.8), channel_id=1, source_target_pairs={{0,32},{8,40},{16,48},{24,56},{32,0},{40,8},{48,16},{56,24},{64,96... | collective-permute-start | bytes 430088 | tf_op jit(solution)/shard_map/ppermute | solution.py:290
  47.8 0.0 collective-permute-done.6.refs_7_
  47.8 1.9 %collective-permute-start.1 = (bf16[560,128]{1,0:T(8,128)(2,1)}, bf16[560,128]{1,0:T(8,128)(2,1)S(1)}, u32[]{:S(2)}, u32[]{:S(2)}) collective-permute-start(bf16[560,128]{1,0:T(8,128)(2,1)} %get-tuple-element.8), channel_id=1, source_target_pairs={{0,16},{8,24},{16,0},{24,8},{32,48},{40,56},{48,32},{56,40},{64,80... | collective-permute-start | bytes 430088 | tf_op jit(solution)/shard_map/ppermute | solution.py:290
  49.8 6.9 %collective-permute-done.5.refs_6_ = bf16[560,128]{1,0:T(8,128)(2,1)S(1)} collective-permute-done((bf16[560,128]{1,0:T(8,128)(2,1)}, bf16[560,128]{1,0:T(8,128)(2,1)S(1)}, u32[]{:S(2)}, u32[]{:S(2)}) %collective-permute-start.5) | collective-permute-done | bytes 143392 | tf_op jit(solution)/shard_map/ppermute | solution.py:290
  56.6 1.9 %collective-permute-start = (bf16[560,128]{1,0:T(8,128)(2,1)}, bf16[560,128]{1,0:T(8,128)(2,1)S(1)}, u32[]{:S(2)}, u32[]{:S(2)}) collective-permute-start(bf16[560,128]{1,0:T(8,128)(2,1)} %get-tuple-element.8), channel_id=1, source_target_pairs={{0,8},{8,0},{16,24},{24,16},{32,40},{40,32},{48,56},{56,48},{64,72... | collective-permute-start | bytes 430088 | tf_op jit(solution)/shard_map/ppermute | solution.py:290
  58.6 0.0 collective-permute-done.4.refs_5_
  58.6 0.0 collective-permute-done.3.refs_4_
  58.6 0.0 collective-permute-done.2.refs_3_
  58.6 0.0 collective-permute-done.1.refs_2_
  58.6 1.5 %collective-permute-done.refs_1_ = bf16[560,128]{1,0:T(8,128)(2,1)S(1)} collective-permute-done((bf16[560,128]{1,0:T(8,128)(2,1)}, bf16[560,128]{1,0:T(8,128)(2,1)S(1)}, u32[]{:S(2)}, u32[]{:S(2)}) %collective-permute-start) | collective-permute-done | bytes 143392 | tf_op jit(solution)/shard_map/ppermute | solution.py:290
  60.1 0.0 copy-start.1
  60.1 0.9 copy-done.1
  61.0 0.2 merge.1
  61.2 5.7 %collective-permute-start.10 = (bf16[544,128]{1,0:T(8,128)(2,1)S(1)}, bf16[544,128]{1,0:T(8,128)(2,1)S(1)}, u32[]{:S(2)}, u32[]{:S(2)}) collective-permute-start(bf16[544,128]{1,0:T(8,128)(2,1)S(1)} %get-tuple-element.11.refs_0_.late), channel_id=1, source_target_pairs={{0,6},{1,7},{2,0},{3,1},{4,2},{5,3},{6,4},{7,5},{8,14},{9,15},{10,... | collective-permute-start | bytes 417800 | tf_op jit(solution)/shard_map/ppermute | solution.py:41
  67.0 1.9 %collective-permute-start.9 = (bf16[544,128]{1,0:T(8,128)(2,1)S(1)}, bf16[544,128]{1,0:T(8,128)(2,1)S(1)}, u32[]{:S(2)}, u32[]{:S(2)}) collective-permute-start(bf16[544,128]{1,0:T(8,128)(2,1)S(1)} %get-tuple-element.11.refs_0_.late), channel_id=1, source_target_pairs={{0,2},{1,3},{2,4},{3,5},{4,6},{5,7},{6,0},{7,1},{8,10},{9,11},{10,... | collective-permute-start | bytes 417800 | tf_op jit(solution)/shard_map/ppermute | solution.py:41
  68.9 5.1 %collective-permute-start.8 = (bf16[544,128]{1,0:T(8,128)(2,1)S(1)}, bf16[544,128]{1,0:T(8,128)(2,1)S(1)}, u32[]{:S(2)}, u32[]{:S(2)}) collective-permute-start(bf16[544,128]{1,0:T(8,128)(2,1)S(1)} %get-tuple-element.11.refs_0_.late), channel_id=1, source_target_pairs={{0,7},{1,0},{2,1},{3,2},{4,3},{5,4},{6,5},{7,6},{8,15},{9,8},{10,9... | collective-permute-start | bytes 417800 | tf_op jit(solution)/shard_map/ppermute | solution.py:41
  74.0 1.9 %collective-permute-start.7 = (bf16[544,128]{1,0:T(8,128)(2,1)S(1)}, bf16[544,128]{1,0:T(8,128)(2,1)S(1)}, u32[]{:S(2)}, u32[]{:S(2)}) collective-permute-start(bf16[544,128]{1,0:T(8,128)(2,1)S(1)} %get-tuple-element.11.refs_0_.late), channel_id=1, source_target_pairs={{0,1},{1,2},{2,3},{3,4},{4,5},{5,6},{6,7},{7,0},{8,9},{9,10},{10,1... | collective-permute-start | bytes 417800 | tf_op jit(solution)/shard_map/ppermute | solution.py:41
  76.0 0.0 collective-permute-done.10.refs_4_
  76.0 5.1 %collective-permute-start.12 = (bf16[544,128]{1,0:T(8,128)(2,1)S(1)}, bf16[544,128]{1,0:T(8,128)(2,1)S(1)}, u32[]{:S(2)}, u32[]{:S(2)}) collective-permute-start(bf16[544,128]{1,0:T(8,128)(2,1)S(1)} %collective-permute-done.10.refs_4_), channel_id=1, source_target_pairs={{0,7},{1,0},{2,1},{3,2},{4,3},{5,4},{6,5},{7,6},{8,15},{9,8},{10,9... | collective-permute-start | bytes 417800 | tf_op jit(solution)/shard_map/ppermute | solution.py:41
  81.1 0.0 collective-permute-done.9.refs_3_
  81.1 1.9 %collective-permute-start.13 = (bf16[544,128]{1,0:T(8,128)(2,1)S(1)}, bf16[544,128]{1,0:T(8,128)(2,1)S(1)}, u32[]{:S(2)}, u32[]{:S(2)}) collective-permute-start(bf16[544,128]{1,0:T(8,128)(2,1)S(1)} %collective-permute-done.9.refs_3_), channel_id=1, source_target_pairs={{0,2},{1,3},{2,4},{3,5},{4,6},{5,7},{6,0},{7,1},{8,10},{9,11},{10,... | collective-permute-start | bytes 417800 | tf_op jit(solution)/shard_map/ppermute | solution.py:41
  83.0 3.1 %collective-permute-start.11 = (bf16[544,128]{1,0:T(8,128)(2,1)S(1)}, bf16[544,128]{1,0:T(8,128)(2,1)S(1)}, u32[]{:S(2)}, u32[]{:S(2)}) collective-permute-start(bf16[544,128]{1,0:T(8,128)(2,1)S(1)} %collective-permute-done.9.refs_3_), channel_id=1, source_target_pairs={{0,1},{1,2},{2,3},{3,4},{4,5},{5,6},{6,7},{7,0},{8,9},{9,10},{10,1... | collective-permute-start | bytes 417800 | tf_op jit(solution)/shard_map/ppermute | solution.py:41
  86.1 0.0 collective-permute-done.8.refs_2_
  86.1 0.0 collective-permute-done.7.refs_1_
  86.1 0.0 collective-permute-done.12.refs_6_
  86.1 6.4 %collective-permute-done.13.refs_7_ = bf16[544,128]{1,0:T(8,128)(2,1)S(1)} collective-permute-done((bf16[544,128]{1,0:T(8,128)(2,1)S(1)}, bf16[544,128]{1,0:T(8,128)(2,1)S(1)}, u32[]{:S(2)}, u32[]{:S(2)}) %collective-permute-start.13) | collective-permute-done | bytes 139296 | tf_op jit(solution)/shard_map/ppermute | solution.py:41
  92.5 1.1 collective-permute-done.11.refs_5_
  93.6 0.0 all-to-all-done.early
  93.6 0.0 copy-start
  93.6 0.9 copy-done
  94.5 0.0 copy-start.2
  94.5 0.9 copy-done.2
  95.5 5.9 %products.1 = bf16[8,272,128]{2,1,0:T(8,128)(2,1)} custom-call(f32[16,128]{1,0:T(8,128)S(1)} %get-tuple-element.9.x, bf16[2,512,2048]{2,1,0:T(8,128)(2,1)} %chol.1, bf16[512,128]{1,0:T(8,128)(2,1)S(1)} %copy-done.2, bf16[6,128,128]{2,1,0:T(8,128)(2,1)S(1)} %copy-done, bf16[8,512,128]{2,1,0:T(8,128)(2,1)S(1)} %all-to-all-done.early, ...), custom_call_target="tpu_custom_call" | custom-call | flops 2147483648 | bytes 6291456 | tf_op jit(solution)/shard_map/products/pallas_call | solution.py:220
  101.3 5.0 %all-to-all-start.1 = ((bf16[8,272,128]{2,1,0:T(8,128)(2,1)}), bf16[8,272,128]{2,1,0:T(8,128)(2,1)S(1)}, u32[]{:S(2)}, u32[]{:S(2)}) async-start(bf16[8,272,128]{2,1,0:T(8,128)(2,1)} %products.1), calls=%async_computation.1 | async-start | bytes 1114112 | tf_op jit(solution)/shard_map/all_to_all | solution.py:296
  106.3 0.9 slice.3.early
  107.2 16.9 %all-to-all-done.1.got = bf16[8,272,128]{2,1,0:T(8,128)(2,1)S(1)} async-done(((bf16[8,272,128]{2,1,0:T(8,128)(2,1)}), bf16[8,272,128]{2,1,0:T(8,128)(2,1)S(1)}, u32[]{:S(2)}, u32[]{:S(2)}) %all-to-all-start.1) | async-done | bytes 557088 | tf_op jit(solution)/shard_map/all_to_all | solution.py:296
  124.1 0.7 finish.1
Async XLA Ops:
  4.2 89.4 %all-to-all-start = ((bf16[8,512,128]{2,1,0:T(8,128)(2,1)}), bf16[8,512,128]{2,1,0:T(8,128)(2,1)S(1)}, u32[]{:S(2)}, u32[]{:S(2)}) async-start(bf16[8,512,128]{2,1,0:T(8,128)(2,1)} %get-tuple-element.10), calls=%async_computation | async-start | bytes 2097152 | tf_op jit(solution)/shard_map/all_to_all | solution.py:35
  11.4 36.5 %collective-permute-start.6 = (bf16[560,128]{1,0:T(8,128)(2,1)}, bf16[560,128]{1,0:T(8,128)(2,1)S(1)}, u32[]{:S(2)}, u32[]{:S(2)}) collective-permute-start(bf16[560,128]{1,0:T(8,128)(2,1)} %get-tuple-element.8), channel_id=1, source_target_pairs={{0,512},{8,520},{16,528},{24,536},{32,544},{40,552},{48,560},{56,5... | collective-permute-start | bytes 430088 | tf_op jit(solution)/shard_map/ppermute | solution.py:290
  30.7 25.9 %collective-permute-start.5 = (bf16[560,128]{1,0:T(8,128)(2,1)}, bf16[560,128]{1,0:T(8,128)(2,1)S(1)}, u32[]{:S(2)}, u32[]{:S(2)}) collective-permute-start(bf16[560,128]{1,0:T(8,128)(2,1)} %get-tuple-element.8), channel_id=1, source_target_pairs={{0,256},{8,264},{16,272},{24,280},{32,288},{40,296},{48,304},{56,3... | collective-permute-start | bytes 430088 | tf_op jit(solution)/shard_map/ppermute | solution.py:290
  36.8 21.7 %collective-permute-start.4 = (bf16[560,128]{1,0:T(8,128)(2,1)}, bf16[560,128]{1,0:T(8,128)(2,1)S(1)}, u32[]{:S(2)}, u32[]{:S(2)}) collective-permute-start(bf16[560,128]{1,0:T(8,128)(2,1)} %get-tuple-element.8), channel_id=1, source_target_pairs={{0,128},{8,136},{16,144},{24,152},{32,160},{40,168},{48,176},{56,1... | collective-permute-start | bytes 430088 | tf_op jit(solution)/shard_map/ppermute | solution.py:290
  41.1 17.4 %collective-permute-start.3 = (bf16[560,128]{1,0:T(8,128)(2,1)}, bf16[560,128]{1,0:T(8,128)(2,1)S(1)}, u32[]{:S(2)}, u32[]{:S(2)}) collective-permute-start(bf16[560,128]{1,0:T(8,128)(2,1)} %get-tuple-element.8), channel_id=1, source_target_pairs={{0,64},{8,72},{16,80},{24,88},{32,96},{40,104},{48,112},{56,120},{... | collective-permute-start | bytes 430088 | tf_op jit(solution)/shard_map/ppermute | solution.py:290
  44.5 14.1 %collective-permute-start.2 = (bf16[560,128]{1,0:T(8,128)(2,1)}, bf16[560,128]{1,0:T(8,128)(2,1)S(1)}, u32[]{:S(2)}, u32[]{:S(2)}) collective-permute-start(bf16[560,128]{1,0:T(8,128)(2,1)} %get-tuple-element.8), channel_id=1, source_target_pairs={{0,32},{8,40},{16,48},{24,56},{32,0},{40,8},{48,16},{56,24},{64,96... | collective-permute-start | bytes 430088 | tf_op jit(solution)/shard_map/ppermute | solution.py:290
  47.8 10.7 %collective-permute-start.1 = (bf16[560,128]{1,0:T(8,128)(2,1)}, bf16[560,128]{1,0:T(8,128)(2,1)S(1)}, u32[]{:S(2)}, u32[]{:S(2)}) collective-permute-start(bf16[560,128]{1,0:T(8,128)(2,1)} %get-tuple-element.8), channel_id=1, source_target_pairs={{0,16},{8,24},{16,0},{24,8},{32,48},{40,56},{48,32},{56,40},{64,80... | collective-permute-start | bytes 430088 | tf_op jit(solution)/shard_map/ppermute | solution.py:290
  56.6 3.5 %collective-permute-start = (bf16[560,128]{1,0:T(8,128)(2,1)}, bf16[560,128]{1,0:T(8,128)(2,1)S(1)}, u32[]{:S(2)}, u32[]{:S(2)}) collective-permute-start(bf16[560,128]{1,0:T(8,128)(2,1)} %get-tuple-element.8), channel_id=1, source_target_pairs={{0,8},{8,0},{16,24},{24,16},{32,40},{40,32},{48,56},{56,48},{64,72... | collective-permute-start | bytes 430088 | tf_op jit(solution)/shard_map/ppermute | solution.py:290
  60.1 0.9 copy-start.1
  61.2 14.7 %collective-permute-start.10 = (bf16[544,128]{1,0:T(8,128)(2,1)S(1)}, bf16[544,128]{1,0:T(8,128)(2,1)S(1)}, u32[]{:S(2)}, u32[]{:S(2)}) collective-permute-start(bf16[544,128]{1,0:T(8,128)(2,1)S(1)} %get-tuple-element.11.refs_0_.late), channel_id=1, source_target_pairs={{0,6},{1,7},{2,0},{3,1},{4,2},{5,3},{6,4},{7,5},{8,14},{9,15},{10,... | collective-permute-start | bytes 417800 | tf_op jit(solution)/shard_map/ppermute | solution.py:41
  67.0 14.2 %collective-permute-start.9 = (bf16[544,128]{1,0:T(8,128)(2,1)S(1)}, bf16[544,128]{1,0:T(8,128)(2,1)S(1)}, u32[]{:S(2)}, u32[]{:S(2)}) collective-permute-start(bf16[544,128]{1,0:T(8,128)(2,1)S(1)} %get-tuple-element.11.refs_0_.late), channel_id=1, source_target_pairs={{0,2},{1,3},{2,4},{3,5},{4,6},{5,7},{6,0},{7,1},{8,10},{9,11},{10,... | collective-permute-start | bytes 417800 | tf_op jit(solution)/shard_map/ppermute | solution.py:41
  68.9 17.2 %collective-permute-start.8 = (bf16[544,128]{1,0:T(8,128)(2,1)S(1)}, bf16[544,128]{1,0:T(8,128)(2,1)S(1)}, u32[]{:S(2)}, u32[]{:S(2)}) collective-permute-start(bf16[544,128]{1,0:T(8,128)(2,1)S(1)} %get-tuple-element.11.refs_0_.late), channel_id=1, source_target_pairs={{0,7},{1,0},{2,1},{3,2},{4,3},{5,4},{6,5},{7,6},{8,15},{9,8},{10,9... | collective-permute-start | bytes 417800 | tf_op jit(solution)/shard_map/ppermute | solution.py:41
  74.0 12.1 %collective-permute-start.7 = (bf16[544,128]{1,0:T(8,128)(2,1)S(1)}, bf16[544,128]{1,0:T(8,128)(2,1)S(1)}, u32[]{:S(2)}, u32[]{:S(2)}) collective-permute-start(bf16[544,128]{1,0:T(8,128)(2,1)S(1)} %get-tuple-element.11.refs_0_.late), channel_id=1, source_target_pairs={{0,1},{1,2},{2,3},{3,4},{4,5},{5,6},{6,7},{7,0},{8,9},{9,10},{10,1... | collective-permute-start | bytes 417800 | tf_op jit(solution)/shard_map/ppermute | solution.py:41
  76.0 10.2 %collective-permute-start.12 = (bf16[544,128]{1,0:T(8,128)(2,1)S(1)}, bf16[544,128]{1,0:T(8,128)(2,1)S(1)}, u32[]{:S(2)}, u32[]{:S(2)}) collective-permute-start(bf16[544,128]{1,0:T(8,128)(2,1)S(1)} %collective-permute-done.10.refs_4_), channel_id=1, source_target_pairs={{0,7},{1,0},{2,1},{3,2},{4,3},{5,4},{6,5},{7,6},{8,15},{9,8},{10,9... | collective-permute-start | bytes 417800 | tf_op jit(solution)/shard_map/ppermute | solution.py:41
  81.1 11.4 %collective-permute-start.13 = (bf16[544,128]{1,0:T(8,128)(2,1)S(1)}, bf16[544,128]{1,0:T(8,128)(2,1)S(1)}, u32[]{:S(2)}, u32[]{:S(2)}) collective-permute-start(bf16[544,128]{1,0:T(8,128)(2,1)S(1)} %collective-permute-done.9.refs_3_), channel_id=1, source_target_pairs={{0,2},{1,3},{2,4},{3,5},{4,6},{5,7},{6,0},{7,1},{8,10},{9,11},{10,... | collective-permute-start | bytes 417800 | tf_op jit(solution)/shard_map/ppermute | solution.py:41
  83.0 10.6 %collective-permute-start.11 = (bf16[544,128]{1,0:T(8,128)(2,1)S(1)}, bf16[544,128]{1,0:T(8,128)(2,1)S(1)}, u32[]{:S(2)}, u32[]{:S(2)}) collective-permute-start(bf16[544,128]{1,0:T(8,128)(2,1)S(1)} %collective-permute-done.9.refs_3_), channel_id=1, source_target_pairs={{0,1},{1,2},{2,3},{3,4},{4,5},{5,6},{6,7},{7,0},{8,9},{9,10},{10,1... | collective-permute-start | bytes 417800 | tf_op jit(solution)/shard_map/ppermute | solution.py:41
  93.6 0.9 copy-start
  94.5 0.9 copy-start.2
  101.3 22.8 %all-to-all-start.1 = ((bf16[8,272,128]{2,1,0:T(8,128)(2,1)}), bf16[8,272,128]{2,1,0:T(8,128)(2,1)S(1)}, u32[]{:S(2)}, u32[]{:S(2)}) async-start(bf16[8,272,128]{2,1,0:T(8,128)(2,1)} %products.1), calls=%async_computation.1 | async-start | bytes 1114112 | tf_op jit(solution)/shard_map/all_to_all | solution.py:296

commit v7 on v5

--- a/solution.py
+++ b/solution.py
@@ -53,7 +53,41 @@
     return inv.at[slot, pl.ds(share, TILE)]
 
 
-def pack_kernel(counts, partner, walkers, inv, fields, out, early, kept, sems):
+def run_copies(copies, between):
+    for copy in copies:
+        copy.start()
+    between()
+    for copy in copies:
+        copy.wait()
+
+
+def pack_kernel(walkers, inv, fields, out, sems):
+    copies = []
+    for j in range(MOVE):
+        rows = out.at[pl.ds(j * STRIDE, ORBS)]
+        copies.append(pltpu.make_async_copy(walkers.at[LIVE + j], rows, sems.at[2 * j]))
+        rows = out.at[pl.ds(j * STRIDE + ORBS, TILE)]
+        copies.append(pltpu.make_async_copy(inv_rows(inv, LIVE + j), rows, sems.at[2 * j + 1]))
+
+    def rest():
+        out[FIELD_ROW:] = jnp.zeros((TILE, out.shape[1]), BF16)
+        out[FIELD_ROW : FIELD_ROW + fields.shape[0], : fields.shape[1]] = fields[...]
+
+    run_copies(copies, rest)
+
+
+def pack_call(walkers, inv, fields):
+    return pl.pallas_call(
+        pack_kernel,
+        in_specs=[HBM, HBM, WHOLE],
+        out_specs=WHOLE,
+        out_shape=jax.ShapeDtypeStruct((FIELD_ROW + TILE, walkers.shape[2]), BF16),
+        scratch_shapes=[pltpu.SemaphoreType.DMA((2 * MOVE,))],
+        name="pack",
+    )(walkers, inv, fields)
+
+
+def keep_kernel(counts, partner, walkers, inv, fields, early, kept, sems):
     copies = []
 
     def add(source, target, first, size):
@@ -61,44 +95,38 @@
             pltpu.make_async_copy(source, target.at[pl.ds(first, size)], sems.at[len(copies)])
         )
 
-    for j in range(MOVE):
-        add(walkers.at[LIVE + j], out, j * STRIDE, ORBS)
-        add(inv_rows(inv, LIVE + j), out, j * STRIDE + ORBS, TILE)
     for j in range(MOVE):
         for k in range(N_CHOL):
             add(walkers.at[j], early.at[k], j * ORBS, ORBS)
         add(walkers.at[2 + j], kept, j * STRIDE, ORBS)
         add(inv_rows(inv, 2 + j), kept, j * STRIDE + ORBS, TILE)
-    for copy in copies:
-        copy.start()
-    out[FIELD_ROW:] = jnp.zeros((TILE, out.shape[1]), BF16)
-    out[FIELD_ROW : FIELD_ROW + fields.shape[0], : fields.shape[1]] = fields[...]
-    walk = lax.axis_index("walk")
-    mate = partner[walk]
-    row_id = lax.broadcasted_iota(jnp.int32, (TILE, kept.shape[1]), 0)
-    plan = (jnp.bitwise_xor(mate, walk), counts[walk], jnp.maximum(counts[mate] - LIVE, 0))
-    tile = jnp.zeros(row_id.shape, jnp.int32)
-    for row, value in zip((DISTANCE, OWN, ARRIVING), plan):
-        tile = jnp.where(row_id == row, value, tile)
-    kept[FIELD_ROW:] = tile.astype(F32).astype(BF16)
-    kept[FIELD_ROW : FIELD_ROW + fields.shape[0], : fields.shape[1]] = fields[...]
-    for copy in copies:
-        copy.wait()
-
-
-def pack_call(counts, partner, walkers, inv, fields):
+
+    def rest():
+        walk = lax.axis_index("walk")
+        mate = partner[walk]
+        row_id = lax.broadcasted_iota(jnp.int32, (TILE, kept.shape[1]), 0)
+        plan = (jnp.bitwise_xor(mate, walk), counts[walk], jnp.maximum(counts[mate] - LIVE, 0))
+        tile = jnp.zeros(row_id.shape, jnp.int32)
+        for row, value in zip((DISTANCE, OWN, ARRIVING), plan):
+            tile = jnp.where(row_id == row, value, tile)
+        kept[FIELD_ROW:] = tile.astype(F32).astype(BF16)
+        kept[FIELD_ROW : FIELD_ROW + fields.shape[0], : fields.shape[1]] = fields[...]
+
+    run_copies(copies, rest)
+
+
+def keep_call(counts, partner, walkers, inv, fields):
     lanes = walkers.shape[2]
     return pl.pallas_call(
-        pack_kernel,
+        keep_kernel,
         in_specs=[SCALARS, SCALARS, HBM, HBM, WHOLE],
-        out_specs=(WHOLE,) * 3,
+        out_specs=(WHOLE, WHOLE),
         out_shape=(
-            jax.ShapeDtypeStruct((FIELD_ROW + TILE, lanes), BF16),
             jax.ShapeDtypeStruct((N_CHOL, 2 * ORBS, lanes), BF16),
             jax.ShapeDtypeStruct((FIELD_ROW + TILE, lanes), BF16),
         ),
-        scratch_shapes=[pltpu.SemaphoreType.DMA(((4 + N_CHOL) * MOVE,))],
-        name="pack",
+        scratch_shapes=[pltpu.SemaphoreType.DMA(((2 + N_CHOL) * MOVE,))],
+        name="keep",
     )(counts, partner, walkers, inv, fields)
 
 
@@ -129,7 +157,7 @@
     for q in range(2):
         mask = (own[:, q : q + 1] > 2 + q) | (row_id >= DISTANCE)
         column = jnp.where(mask, tile[:, 2 + q : 3 + q], theirs[:, LIVE + 1 - q : LIVE + 2 - q])
-        x[:, q : q + 1] = column
+        x[:, 2 + q : 3 + q] = column
 
 
 def merge_call(kept, received):
@@ -196,7 +224,7 @@
         for g, both in enumerate(products):
             product = both[:, q * lanes : (q + 1) * lanes]
             bias = -STEP_ROOT * jnp.sum(product * weighted, keepdims=True)
-            field = x[g : g + 1, q : q + 1].astype(F32)
+            field = x[g : g + 1, base + q : base + q + 1]
             total += STEP_ROOT * (field - bias) * product
             log += field * bias - 0.5 * bias * bias
         spread = total.astype(BF16).reshape(N_CHOL, ROWS_DEV, lanes)
@@ -277,9 +305,8 @@
 def shards(walkers, inv_intersection, fields, cholesky, trial_rows, counts, partner):
     walk_size = lax.axis_size("walk")
     fields = fields.T
-    outgoing, early, kept = pack_call(
-        counts, partner, walkers, inv_intersection, fields
-    )
+    outgoing = pack_call(walkers, inv_intersection, fields)
+    early, kept = keep_call(counts, partner, walkers, inv_intersection, fields)
     early_parts = gather(early)
     received = []
     for bit in range(walk_size.bit_length() - 1):
@@ -288,7 +315,7 @@
     late, x = merge_call(kept, received)
     late_parts = gather_in_two(late)
     first = product_call(
-        False, fields, cholesky, trial_rows, inv_intersection, [early_parts]
+        False, x, cholesky, trial_rows, inv_intersection, [early_parts]
     )
     sums = product_call(True, x, cholesky, trial_rows, first, late_parts)
     sums = lax.all_to_all(sums, "chol", 0, 0, tiled=True)

time: 121 us -> 123 us (1.017)
  the two profiles are of different devices: /device:TPU:4 before, /device:TPU:2 now
where the time goes in v7:
time: 123 us; the launch traced here: 122 us
  starting transfers between devices  79.3 us (64%)
  waiting for transfers between devices  26.5 us (22%)
  Pallas kernels  11.5 us (9%)
  local copies, waits for them, and re-layouts  4.02 us (3%)
    ppermute x7, starting transfers between devices, shards(): received.append(lax.ppermute(outgoing, 'walk', route))  42.4 us
    ppermute x7, starting transfers between devices, shift(): return lax.ppermute(value, 'chol', route)  24.8 us
    all_to_all x1, waiting for transfers between devices, shards(): sums = lax.all_to_all(sums, 'chol', 0, 0, tiled=True)  16.9 us
    all_to_all x1, starting transfers between devices, gather(): return lax.all_to_all(copies, 'chol', 0, 0, tiled=True)  7.11 us
    ppermute x7, waiting for transfers between devices, shards(): received.append(lax.ppermute(outgoing, 'walk', route))  6.24 us
    all_to_all x1, starting transfers between devices, shards(): sums = lax.all_to_all(sums, 'chol', 0, 0, tiled=True)  4.97 us
    pallas_call x2, Pallas kernels, product_call(): pl.pallas_call(body, in_specs=[WHOLE] * (4 + len(parts)), out_specs=WHOLE...  4.69 us
    pallas_call x1, Pallas kernels, keep_call(): pl.pallas_call(keep_kernel, in_specs=[SCALARS, SCALARS, HBM, HBM, WHOLE],...  3.59 us
  transfers between devices with their start and end apart: 16, of which 5 were waited for; matrix products, arithmetic and copies ran while one was open for 1% of the time, Pallas kernels for 4%

profile of v7, /device:TPU:2, one launch (start us, length us, event | category | flops | bytes accessed | tf_op | source)
XLA Modules:
  0.0 122.2 jit_solution(12482409325230892214)
XLA Ops:
  0.6 0.0 copy-start.2
  0.6 0.0 copy-start.3
  0.7 3.6 %keep.1 = (bf16[8,512,128]{2,1,0:T(8,128)(2,1)}, bf16[560,128]{1,0:T(8,128)(2,1)}) custom-call(s32[128]{0:T(128)} %counts.1, s32[128]{0:T(128)} %partner.1, bf16[6,256,128]{2,1,0:T(8,128)(2,1)} %walkers.3, bf16[6,128,128]{2,1,0:T(8,128)(2,1)} %refs_3_.1, bf16[2,6]{1,0:T(2,128)(2,1)} %bitcast.1), custom_call_target="tpu_custom_call" | custom-call | tf_op jit(solution)/shard_map/keep/pallas_call | solution.py:120
  4.3 7.1 %all-to-all-start = ((bf16[8,512,128]{2,1,0:T(8,128)(2,1)}), bf16[8,512,128]{2,1,0:T(8,128)(2,1)S(1)}, u32[]{:S(2)}, u32[]{:S(2)}) async-start(bf16[8,512,128]{2,1,0:T(8,128)(2,1)} %get-tuple-element.8), calls=%async_computation | async-start | bytes 2097152 | tf_op jit(solution)/shard_map/all_to_all | solution.py:35
  11.4 2.2 %pack.1 = bf16[560,128]{1,0:T(8,128)(2,1)} custom-call(bf16[6,256,128]{2,1,0:T(8,128)(2,1)} %walkers.3, bf16[6,128,128]{2,1,0:T(8,128)(2,1)} %refs_3_.1, bf16[2,6]{1,0:T(2,128)(2,1)} %bitcast.2), custom_call_target="tpu_custom_call" | custom-call | tf_op jit(solution)/shard_map/pack/pallas_call | solution.py:80
  13.6 19.4 %collective-permute-start.6 = (bf16[560,128]{1,0:T(8,128)(2,1)}, bf16[560,128]{1,0:T(8,128)(2,1)S(1)}, u32[]{:S(2)}, u32[]{:S(2)}) collective-permute-start(bf16[560,128]{1,0:T(8,128)(2,1)} %pack.1), channel_id=1, source_target_pairs={{0,512},{8,520},{16,528},{24,536},{32,544},{40,552},{48,560},{56,5... | collective-permute-start | bytes 430088 | tf_op jit(solution)/shard_map/ppermute | solution.py:314
  33.0 6.1 %collective-permute-start.5 = (bf16[560,128]{1,0:T(8,128)(2,1)}, bf16[560,128]{1,0:T(8,128)(2,1)S(1)}, u32[]{:S(2)}, u32[]{:S(2)}) collective-permute-start(bf16[560,128]{1,0:T(8,128)(2,1)} %pack.1), channel_id=1, source_target_pairs={{0,256},{8,264},{16,272},{24,280},{32,288},{40,296},{48,304},{56,3... | collective-permute-start | bytes 430088 | tf_op jit(solution)/shard_map/ppermute | solution.py:314
  39.1 4.3 %collective-permute-start.4 = (bf16[560,128]{1,0:T(8,128)(2,1)}, bf16[560,128]{1,0:T(8,128)(2,1)S(1)}, u32[]{:S(2)}, u32[]{:S(2)}) collective-permute-start(bf16[560,128]{1,0:T(8,128)(2,1)} %pack.1), channel_id=1, source_target_pairs={{0,128},{8,136},{16,144},{24,152},{32,160},{40,168},{48,176},{56,1... | collective-permute-start | bytes 430088 | tf_op jit(solution)/shard_map/ppermute | solution.py:314
  43.4 3.4 %collective-permute-start.3 = (bf16[560,128]{1,0:T(8,128)(2,1)}, bf16[560,128]{1,0:T(8,128)(2,1)S(1)}, u32[]{:S(2)}, u32[]{:S(2)}) collective-permute-start(bf16[560,128]{1,0:T(8,128)(2,1)} %pack.1), channel_id=1, source_target_pairs={{0,64},{8,72},{16,80},{24,88},{32,96},{40,104},{48,112},{56,120},{... | collective-permute-start | bytes 430088 | tf_op jit(solution)/shard_map/ppermute | solution.py:314
  46.8 4.0 %collective-permute-start.2 = (bf16[560,128]{1,0:T(8,128)(2,1)}, bf16[560,128]{1,0:T(8,128)(2,1)S(1)}, u32[]{:S(2)}, u32[]{:S(2)}) collective-permute-start(bf16[560,128]{1,0:T(8,128)(2,1)} %pack.1), channel_id=1, source_target_pairs={{0,32},{8,40},{16,48},{24,56},{32,0},{40,8},{48,16},{56,24},{64,96... | collective-permute-start | bytes 430088 | tf_op jit(solution)/shard_map/ppermute | solution.py:314
  50.8 0.0 collective-permute-done.6.refs_7_
  50.8 3.3 %collective-permute-start.1 = (bf16[560,128]{1,0:T(8,128)(2,1)}, bf16[560,128]{1,0:T(8,128)(2,1)S(1)}, u32[]{:S(2)}, u32[]{:S(2)}) collective-permute-start(bf16[560,128]{1,0:T(8,128)(2,1)} %pack.1), channel_id=1, source_target_pairs={{0,16},{8,24},{16,0},{24,8},{32,48},{40,56},{48,32},{56,40},{64,80... | collective-permute-start | bytes 430088 | tf_op jit(solution)/shard_map/ppermute | solution.py:314
  54.2 4.7 %collective-permute-done.5.refs_6_ = bf16[560,128]{1,0:T(8,128)(2,1)S(1)} collective-permute-done((bf16[560,128]{1,0:T(8,128)(2,1)}, bf16[560,128]{1,0:T(8,128)(2,1)S(1)}, u32[]{:S(2)}, u32[]{:S(2)}) %collective-permute-start.5) | collective-permute-done | bytes 143392 | tf_op jit(solution)/shard_map/ppermute | solution.py:314
  58.9 1.9 %collective-permute-start = (bf16[560,128]{1,0:T(8,128)(2,1)}, bf16[560,128]{1,0:T(8,128)(2,1)S(1)}, u32[]{:S(2)}, u32[]{:S(2)}) collective-permute-start(bf16[560,128]{1,0:T(8,128)(2,1)} %pack.1), channel_id=1, source_target_pairs={{0,8},{8,0},{16,24},{24,16},{32,40},{40,32},{48,56},{56,48},{64,72... | collective-permute-start | bytes 430088 | tf_op jit(solution)/shard_map/ppermute | solution.py:314
  60.8 0.0 collective-permute-done.4.refs_5_
  60.8 0.0 collective-permute-done.3.refs_4_
  60.8 0.0 collective-permute-done.2.refs_3_
  60.8 0.0 collective-permute-done.1.refs_2_
  60.9 1.5 %collective-permute-done.refs_1_ = bf16[560,128]{1,0:T(8,128)(2,1)S(1)} collective-permute-done((bf16[560,128]{1,0:T(8,128)(2,1)}, bf16[560,128]{1,0:T(8,128)(2,1)S(1)}, u32[]{:S(2)}, u32[]{:S(2)}) %collective-permute-start) | collective-permute-done | bytes 143392 | tf_op jit(solution)/shard_map/ppermute | solution.py:314
  62.4 0.0 copy-start.4
  62.4 0.9 copy-done.4
  63.3 0.2 merge.1
  63.5 5.7 %collective-permute-start.10 = (bf16[544,128]{1,0:T(8,128)(2,1)S(1)}, bf16[544,128]{1,0:T(8,128)(2,1)S(1)}, u32[]{:S(2)}, u32[]{:S(2)}) collective-permute-start(bf16[544,128]{1,0:T(8,128)(2,1)S(1)} %get-tuple-element.9.refs_4_.late), channel_id=1, source_target_pairs={{0,6},{1,7},{2,0},{3,1},{4,2},{5,3},{6,4},{7,5},{8,14},{9,15},{10,... | collective-permute-start | bytes 417800 | tf_op jit(solution)/shard_map/ppermute | solution.py:41
  69.2 1.9 %collective-permute-start.9 = (bf16[544,128]{1,0:T(8,128)(2,1)S(1)}, bf16[544,128]{1,0:T(8,128)(2,1)S(1)}, u32[]{:S(2)}, u32[]{:S(2)}) collective-permute-start(bf16[544,128]{1,0:T(8,128)(2,1)S(1)} %get-tuple-element.9.refs_4_.late), channel_id=1, source_target_pairs={{0,2},{1,3},{2,4},{3,5},{4,6},{5,7},{6,0},{7,1},{8,10},{9,11},{10,... | collective-permute-start | bytes 417800 | tf_op jit(solution)/shard_map/ppermute | solution.py:41
  71.1 5.1 %collective-permute-start.8 = (bf16[544,128]{1,0:T(8,128)(2,1)S(1)}, bf16[544,128]{1,0:T(8,128)(2,1)S(1)}, u32[]{:S(2)}, u32[]{:S(2)}) collective-permute-start(bf16[544,128]{1,0:T(8,128)(2,1)S(1)} %get-tuple-element.9.refs_4_.late), channel_id=1, source_target_pairs={{0,7},{1,0},{2,1},{3,2},{4,3},{5,4},{6,5},{7,6},{8,15},{9,8},{10,9... | collective-permute-start | bytes 417800 | tf_op jit(solution)/shard_map/ppermute | solution.py:41
  76.3 1.9 %collective-permute-start.7 = (bf16[544,128]{1,0:T(8,128)(2,1)S(1)}, bf16[544,128]{1,0:T(8,128)(2,1)S(1)}, u32[]{:S(2)}, u32[]{:S(2)}) collective-permute-start(bf16[544,128]{1,0:T(8,128)(2,1)S(1)} %get-tuple-element.9.refs_4_.late), channel_id=1, source_target_pairs={{0,1},{1,2},{2,3},{3,4},{4,5},{5,6},{6,7},{7,0},{8,9},{9,10},{10,1... | collective-permute-start | bytes 417800 | tf_op jit(solution)/shard_map/ppermute | solution.py:41
  78.2 0.0 collective-permute-done.10.refs_8_
  78.2 5.1 %collective-permute-start.12 = (bf16[544,128]{1,0:T(8,128)(2,1)S(1)}, bf16[544,128]{1,0:T(8,128)(2,1)S(1)}, u32[]{:S(2)}, u32[]{:S(2)}) collective-permute-start(bf16[544,128]{1,0:T(8,128)(2,1)S(1)} %collective-permute-done.10.refs_8_), channel_id=1, source_target_pairs={{0,7},{1,0},{2,1},{3,2},{4,3},{5,4},{6,5},{7,6},{8,15},{9,8},{10,9... | collective-permute-start | bytes 417800 | tf_op jit(solution)/shard_map/ppermute | solution.py:41
  83.4 0.0 collective-permute-done.9.refs_7_
  83.4 1.9 %collective-permute-start.13 = (bf16[544,128]{1,0:T(8,128)(2,1)S(1)}, bf16[544,128]{1,0:T(8,128)(2,1)S(1)}, u32[]{:S(2)}, u32[]{:S(2)}) collective-permute-start(bf16[544,128]{1,0:T(8,128)(2,1)S(1)} %collective-permute-done.9.refs_7_), channel_id=1, source_target_pairs={{0,2},{1,3},{2,4},{3,5},{4,6},{5,7},{6,0},{7,1},{8,10},{9,11},{10,... | collective-permute-start | bytes 417800 | tf_op jit(solution)/shard_map/ppermute | solution.py:41
  85.3 3.1 %collective-permute-start.11 = (bf16[544,128]{1,0:T(8,128)(2,1)S(1)}, bf16[544,128]{1,0:T(8,128)(2,1)S(1)}, u32[]{:S(2)}, u32[]{:S(2)}) collective-permute-start(bf16[544,128]{1,0:T(8,128)(2,1)S(1)} %collective-permute-done.9.refs_7_), channel_id=1, source_target_pairs={{0,1},{1,2},{2,3},{3,4},{4,5},{5,6},{6,7},{7,0},{8,9},{9,10},{10,1... | collective-permute-start | bytes 417800 | tf_op jit(solution)/shard_map/ppermute | solution.py:41
  88.4 0.0 all-to-all-done.refs_4_
  88.4 0.0 copy-done.2
  88.4 0.0 copy-done.3
  88.4 0.0 copy-start
  88.4 2.2 %copy-done = bf16[2,512,2048]{2,1,0:T(8,128)(2,1)S(1)} copy-done((bf16[2,512,2048]{2,1,0:T(8,128)(2,1)S(1)}, bf16[2,512,2048]{2,1,0:T(8,128)(2,1)}, u32[]{:S(2)}) %copy-start) | copy-done | bytes 4194328
  90.6 1.9 %early_products.1.refs_3_ = bf16[8,144,128]{2,1,0:T(8,128)(2,1)S(1)} custom-call(f32[16,128]{1,0:T(8,128)S(1)} %get-tuple-element.7.refs_0_.x, bf16[2,512,2048]{2,1,0:T(8,128)(2,1)S(1)} %copy-done, bf16[512,128]{1,0:T(8,128)(2,1)S(1)} %copy-done.3, bf16[6,128,128]{2,1,0:T(8,128)(2,1)S(1)} %copy-done.2, bf16[8,512,128]{2,1,0:T(8,128)(2,1)S(1)} %all-to-all-done.refs_4_), custom_call_target="tpu_custom_call" | custom-call | flops 1073741824 | bytes 6291456 | tf_op jit(solution)/shard_map/early_products/pallas_call | solution.py:250
  92.5 0.0 collective-permute-done.8.refs_6_
  92.5 0.0 collective-permute-done.7.refs_5_
  92.5 0.0 collective-permute-done.12.refs_10_
  92.5 2.3 %collective-permute-done.13.refs_11_ = bf16[544,128]{1,0:T(8,128)(2,1)S(1)} collective-permute-done((bf16[544,128]{1,0:T(8,128)(2,1)S(1)}, bf16[544,128]{1,0:T(8,128)(2,1)S(1)}, u32[]{:S(2)}, u32[]{:S(2)}) %collective-permute-start.13) | collective-permute-done | bytes 139296 | tf_op jit(solution)/shard_map/ppermute | solution.py:41
  94.8 1.1 collective-permute-done.11.refs_9_
  95.9 0.0 copy-done.1
  95.9 2.8 %late_products.1 = bf16[8,272,128]{2,1,0:T(8,128)(2,1)} custom-call(f32[16,128]{1,0:T(8,128)S(1)} %get-tuple-element.7.refs_0_.x, bf16[2,512,2048]{2,1,0:T(8,128)(2,1)S(1)} %copy-done.1, bf16[512,128]{1,0:T(8,128)(2,1)S(1)} %copy-done.3, bf16[8,144,128]{2,1,0:T(8,128)(2,1)S(1)} %early_products.1.refs_3_, bf16[544,128]{1,0:T(8,128)(2,1)S(1)} %get-tuple-element.9.refs_4_.late, ...), custom_call_target="tpu_custom_call" | custom-call | flops 1073741824 | bytes 6291456 | tf_op jit(solution)/shard_map/late_products/pallas_call | solution.py:250
  98.7 5.0 %all-to-all-start.1 = ((bf16[8,272,128]{2,1,0:T(8,128)(2,1)}), bf16[8,272,128]{2,1,0:T(8,128)(2,1)S(1)}, u32[]{:S(2)}, u32[]{:S(2)}) async-start(bf16[8,272,128]{2,1,0:T(8,128)(2,1)} %late_products.1), calls=%async_computation.1 | async-start | bytes 1114112 | tf_op jit(solution)/shard_map/all_to_all | solution.py:321
  103.7 0.9 slice.3.early
  104.6 16.9 %all-to-all-done.1.got = bf16[8,272,128]{2,1,0:T(8,128)(2,1)S(1)} async-done(((bf16[8,272,128]{2,1,0:T(8,128)(2,1)}), bf16[8,272,128]{2,1,0:T(8,128)(2,1)S(1)}, u32[]{:S(2)}, u32[]{:S(2)}) %all-to-all-start.1) | async-done | bytes 557088 | tf_op jit(solution)/shard_map/all_to_all | solution.py:321
  121.5 0.7 finish.1
  (1 shorter events, 0.0 us)
Async XLA Ops:
  0.6 87.8 %copy-start.2 = (bf16[6,128,128]{2,1,0:T(8,128)(2,1)S(1)}, bf16[6,128,128]{2,1,0:T(8,128)(2,1)}, u32[]{:S(2)}) copy-start(bf16[6,128,128]{2,1,0:T(8,128)(2,1)} %refs_3_.1) | copy-start | bytes 589828
  0.6 87.8 %copy-start.3 = (bf16[512,128]{1,0:T(8,128)(2,1)S(1)}, bf16[512,128]{1,0:T(8,128)(2,1)}, u32[]{:S(2)}) copy-start(bf16[512,128]{1,0:T(8,128)(2,1)} %refs_2_.3) | copy-start | bytes 393220
  4.3 84.1 %all-to-all-start = ((bf16[8,512,128]{2,1,0:T(8,128)(2,1)}), bf16[8,512,128]{2,1,0:T(8,128)(2,1)S(1)}, u32[]{:S(2)}, u32[]{:S(2)}) async-start(bf16[8,512,128]{2,1,0:T(8,128)(2,1)} %get-tuple-element.8), calls=%async_computation | async-start | bytes 2097152 | tf_op jit(solution)/shard_map/all_to_all | solution.py:35
  13.6 37.2 %collective-permute-start.6 = (bf16[560,128]{1,0:T(8,128)(2,1)}, bf16[560,128]{1,0:T(8,128)(2,1)S(1)}, u32[]{:S(2)}, u32[]{:S(2)}) collective-permute-start(bf16[560,128]{1,0:T(8,128)(2,1)} %pack.1), channel_id=1, source_target_pairs={{0,512},{8,520},{16,528},{24,536},{32,544},{40,552},{48,560},{56,5... | collective-permute-start | bytes 430088 | tf_op jit(solution)/shard_map/ppermute | solution.py:314
  33.0 25.9 %collective-permute-start.5 = (bf16[560,128]{1,0:T(8,128)(2,1)}, bf16[560,128]{1,0:T(8,128)(2,1)S(1)}, u32[]{:S(2)}, u32[]{:S(2)}) collective-permute-start(bf16[560,128]{1,0:T(8,128)(2,1)} %pack.1), channel_id=1, source_target_pairs={{0,256},{8,264},{16,272},{24,280},{32,288},{40,296},{48,304},{56,3... | collective-permute-start | bytes 430088 | tf_op jit(solution)/shard_map/ppermute | solution.py:314
  39.1 21.7 %collective-permute-start.4 = (bf16[560,128]{1,0:T(8,128)(2,1)}, bf16[560,128]{1,0:T(8,128)(2,1)S(1)}, u32[]{:S(2)}, u32[]{:S(2)}) collective-permute-start(bf16[560,128]{1,0:T(8,128)(2,1)} %pack.1), channel_id=1, source_target_pairs={{0,128},{8,136},{16,144},{24,152},{32,160},{40,168},{48,176},{56,1... | collective-permute-start | bytes 430088 | tf_op jit(solution)/shard_map/ppermute | solution.py:314
  43.4 17.4 %collective-permute-start.3 = (bf16[560,128]{1,0:T(8,128)(2,1)}, bf16[560,128]{1,0:T(8,128)(2,1)S(1)}, u32[]{:S(2)}, u32[]{:S(2)}) collective-permute-start(bf16[560,128]{1,0:T(8,128)(2,1)} %pack.1), channel_id=1, source_target_pairs={{0,64},{8,72},{16,80},{24,88},{32,96},{40,104},{48,112},{56,120},{... | collective-permute-start | bytes 430088 | tf_op jit(solution)/shard_map/ppermute | solution.py:314
  46.8 14.1 %collective-permute-start.2 = (bf16[560,128]{1,0:T(8,128)(2,1)}, bf16[560,128]{1,0:T(8,128)(2,1)S(1)}, u32[]{:S(2)}, u32[]{:S(2)}) collective-permute-start(bf16[560,128]{1,0:T(8,128)(2,1)} %pack.1), channel_id=1, source_target_pairs={{0,32},{8,40},{16,48},{24,56},{32,0},{40,8},{48,16},{56,24},{64,96... | collective-permute-start | bytes 430088 | tf_op jit(solution)/shard_map/ppermute | solution.py:314
  50.8 10.0 %collective-permute-start.1 = (bf16[560,128]{1,0:T(8,128)(2,1)}, bf16[560,128]{1,0:T(8,128)(2,1)S(1)}, u32[]{:S(2)}, u32[]{:S(2)}) collective-permute-start(bf16[560,128]{1,0:T(8,128)(2,1)} %pack.1), channel_id=1, source_target_pairs={{0,16},{8,24},{16,0},{24,8},{32,48},{40,56},{48,32},{56,40},{64,80... | collective-permute-start | bytes 430088 | tf_op jit(solution)/shard_map/ppermute | solution.py:314
  58.9 3.5 %collective-permute-start = (bf16[560,128]{1,0:T(8,128)(2,1)}, bf16[560,128]{1,0:T(8,128)(2,1)S(1)}, u32[]{:S(2)}, u32[]{:S(2)}) collective-permute-start(bf16[560,128]{1,0:T(8,128)(2,1)} %pack.1), channel_id=1, source_target_pairs={{0,8},{8,0},{16,24},{24,16},{32,40},{40,32},{48,56},{56,48},{64,72... | collective-permute-start | bytes 430088 | tf_op jit(solution)/shard_map/ppermute | solution.py:314
  62.4 0.9 copy-start.4
  63.5 14.7 %collective-permute-start.10 = (bf16[544,128]{1,0:T(8,128)(2,1)S(1)}, bf16[544,128]{1,0:T(8,128)(2,1)S(1)}, u32[]{:S(2)}, u32[]{:S(2)}) collective-permute-start(bf16[544,128]{1,0:T(8,128)(2,1)S(1)} %get-tuple-element.9.refs_4_.late), channel_id=1, source_target_pairs={{0,6},{1,7},{2,0},{3,1},{4,2},{5,3},{6,4},{7,5},{8,14},{9,15},{10,... | collective-permute-start | bytes 417800 | tf_op jit(solution)/shard_map/ppermute | solution.py:41
  69.2 14.2 %collective-permute-start.9 = (bf16[544,128]{1,0:T(8,128)(2,1)S(1)}, bf16[544,128]{1,0:T(8,128)(2,1)S(1)}, u32[]{:S(2)}, u32[]{:S(2)}) collective-permute-start(bf16[544,128]{1,0:T(8,128)(2,1)S(1)} %get-tuple-element.9.refs_4_.late), channel_id=1, source_target_pairs={{0,2},{1,3},{2,4},{3,5},{4,6},{5,7},{6,0},{7,1},{8,10},{9,11},{10,... | collective-permute-start | bytes 417800 | tf_op jit(solution)/shard_map/ppermute | solution.py:41
  71.1 21.3 %collective-permute-start.8 = (bf16[544,128]{1,0:T(8,128)(2,1)S(1)}, bf16[544,128]{1,0:T(8,128)(2,1)S(1)}, u32[]{:S(2)}, u32[]{:S(2)}) collective-permute-start(bf16[544,128]{1,0:T(8,128)(2,1)S(1)} %get-tuple-element.9.refs_4_.late), channel_id=1, source_target_pairs={{0,7},{1,0},{2,1},{3,2},{4,3},{5,4},{6,5},{7,6},{8,15},{9,8},{10,9... | collective-permute-start | bytes 417800 | tf_op jit(solution)/shard_map/ppermute | solution.py:41
  76.3 16.2 %collective-permute-start.7 = (bf16[544,128]{1,0:T(8,128)(2,1)S(1)}, bf16[544,128]{1,0:T(8,128)(2,1)S(1)}, u32[]{:S(2)}, u32[]{:S(2)}) collective-permute-start(bf16[544,128]{1,0:T(8,128)(2,1)S(1)} %get-tuple-element.9.refs_4_.late), channel_id=1, source_target_pairs={{0,1},{1,2},{2,3},{3,4},{4,5},{5,6},{6,7},{7,0},{8,9},{9,10},{10,1... | collective-permute-start | bytes 417800 | tf_op jit(solution)/shard_map/ppermute | solution.py:41
  78.2 14.3 %collective-permute-start.12 = (bf16[544,128]{1,0:T(8,128)(2,1)S(1)}, bf16[544,128]{1,0:T(8,128)(2,1)S(1)}, u32[]{:S(2)}, u32[]{:S(2)}) collective-permute-start(bf16[544,128]{1,0:T(8,128)(2,1)S(1)} %collective-permute-done.10.refs_8_), channel_id=1, source_target_pairs={{0,7},{1,0},{2,1},{3,2},{4,3},{5,4},{6,5},{7,6},{8,15},{9,8},{10,9... | collective-permute-start | bytes 417800 | tf_op jit(solution)/shard_map/ppermute | solution.py:41
  83.4 11.4 %collective-permute-start.13 = (bf16[544,128]{1,0:T(8,128)(2,1)S(1)}, bf16[544,128]{1,0:T(8,128)(2,1)S(1)}, u32[]{:S(2)}, u32[]{:S(2)}) collective-permute-start(bf16[544,128]{1,0:T(8,128)(2,1)S(1)} %collective-permute-done.9.refs_7_), channel_id=1, source_target_pairs={{0,2},{1,3},{2,4},{3,5},{4,6},{5,7},{6,0},{7,1},{8,10},{9,11},{10,... | collective-permute-start | bytes 417800 | tf_op jit(solution)/shard_map/ppermute | solution.py:41
  85.3 10.6 %collective-permute-start.11 = (bf16[544,128]{1,0:T(8,128)(2,1)S(1)}, bf16[544,128]{1,0:T(8,128)(2,1)S(1)}, u32[]{:S(2)}, u32[]{:S(2)}) collective-permute-start(bf16[544,128]{1,0:T(8,128)(2,1)S(1)} %collective-permute-done.9.refs_7_), channel_id=1, source_target_pairs={{0,1},{1,2},{2,3},{3,4},{4,5},{5,6},{6,7},{7,0},{8,9},{9,10},{10,1... | collective-permute-start | bytes 417800 | tf_op jit(solution)/shard_map/ppermute | solution.py:41
  88.4 2.2 %copy-start = (bf16[2,512,2048]{2,1,0:T(8,128)(2,1)S(1)}, bf16[2,512,2048]{2,1,0:T(8,128)(2,1)}, u32[]{:S(2)}) copy-start(bf16[2,512,2048]{2,1,0:T(8,128)(2,1)} %refs_1_.3) | copy-start | bytes 12582916
  90.6 5.3 %copy-start.1 = (bf16[2,512,2048]{2,1,0:T(8,128)(2,1)S(1)}, bf16[2,512,2048]{2,1,0:T(8,128)(2,1)}, u32[]{:S(2)}) copy-start(bf16[2,512,2048]{2,1,0:T(8,128)(2,1)} %refs_1_.3) | copy-start | bytes 12582916
  98.7 22.8 %all-to-all-start.1 = ((bf16[8,272,128]{2,1,0:T(8,128)(2,1)}), bf16[8,272,128]{2,1,0:T(8,128)(2,1)S(1)}, u32[]{:S(2)}, u32[]{:S(2)}) async-start(bf16[8,272,128]{2,1,0:T(8,128)(2,1)} %late_products.1), calls=%async_computation.1 | async-start | bytes 1114112 | tf_op jit(solution)/shard_map/all_to_all | solution.py:321

commit v8 on v7

--- a/solution.py
+++ b/solution.py
@@ -96,8 +96,7 @@
         )
 
     for j in range(MOVE):
-        for k in range(N_CHOL):
-            add(walkers.at[j], early.at[k], j * ORBS, ORBS)
+        add(walkers.at[j], early.at[0], j * ORBS, ORBS)
         add(walkers.at[2 + j], kept, j * STRIDE, ORBS)
         add(inv_rows(inv, 2 + j), kept, j * STRIDE + ORBS, TILE)
 
@@ -113,6 +112,9 @@
         kept[FIELD_ROW : FIELD_ROW + fields.shape[0], : fields.shape[1]] = fields[...]
 
     run_copies(copies, rest)
+    block = early[0]
+    for k in range(1, N_CHOL):
+        early[k] = block
 
 
 def keep_call(counts, partner, walkers, inv, fields):
@@ -125,7 +127,7 @@
             jax.ShapeDtypeStruct((N_CHOL, 2 * ORBS, lanes), BF16),
             jax.ShapeDtypeStruct((FIELD_ROW + TILE, lanes), BF16),
         ),
-        scratch_shapes=[pltpu.SemaphoreType.DMA(((2 + N_CHOL) * MOVE,))],
+        scratch_shapes=[pltpu.SemaphoreType.DMA((3 * MOVE,))],
         name="keep",
     )(counts, partner, walkers, inv, fields)
 

time: 123 us -> 122 us (level)
  the two profiles are of different devices: /device:TPU:2 before, /device:TPU:6 now
where the time goes in v8:
time: 122 us
  starting transfers between devices  77.2 us (63%)
  waiting for transfers between devices  28.6 us (23%)
  Pallas kernels  10.8 us (9%)
  local copies, waits for them, and re-layouts  4.02 us (3%)
    ppermute x7, starting transfers between devices, shards(): received.append(lax.ppermute(outgoing, 'walk', route))  40.3 us
    ppermute x7, starting transfers between devices, shift(): return lax.ppermute(value, 'chol', route)  24.8 us
    all_to_all x1, waiting for transfers between devices, shards(): sums = lax.all_to_all(sums, 'chol', 0, 0, tiled=True)  16.9 us
    ppermute x7, waiting for transfers between devices, shards(): received.append(lax.ppermute(outgoing, 'walk', route))  8.38 us
    all_to_all x1, starting transfers between devices, gather(): return lax.all_to_all(copies, 'chol', 0, 0, tiled=True)  7.11 us
    all_to_all x1, starting transfers between devices, shards(): sums = lax.all_to_all(sums, 'chol', 0, 0, tiled=True)  4.97 us
    pallas_call x2, Pallas kernels, product_call(): pl.pallas_call(body, in_specs=[WHOLE] * (4 + len(parts)), out_specs=WHOLE...  4.7 us
    ppermute x7, waiting for transfers between devices, shift(): return lax.ppermute(value, 'chol', route)  3.38 us
  transfers between devices with their start and end apart: 16, of which 5 were waited for; matrix products, arithmetic and copies ran while one was open for 1% of the time, Pallas kernels for 4%

profile of v8, /device:TPU:6, one launch (start us, length us, event | category | flops | bytes accessed | tf_op | source)
XLA Modules:
  0.0 121.5 jit_solution(10950266363114737343)
XLA Ops:
  0.6 0.0 copy-start.2
  0.6 0.0 copy-start.3
  0.7 2.9 %keep.1 = (bf16[8,512,128]{2,1,0:T(8,128)(2,1)}, bf16[560,128]{1,0:T(8,128)(2,1)}) custom-call(s32[128]{0:T(128)} %counts.1, s32[128]{0:T(128)} %partner.1, bf16[6,256,128]{2,1,0:T(8,128)(2,1)} %walkers.3, bf16[6,128,128]{2,1,0:T(8,128)(2,1)} %refs_3_.1, bf16[2,6]{1,0:T(2,128)(2,1)} %bitcast.1), custom_call_target="tpu_custom_call" | custom-call | tf_op jit(solution)/shard_map/keep/pallas_call | solution.py:122
  3.6 7.1 %all-to-all-start = ((bf16[8,512,128]{2,1,0:T(8,128)(2,1)}), bf16[8,512,128]{2,1,0:T(8,128)(2,1)S(1)}, u32[]{:S(2)}, u32[]{:S(2)}) async-start(bf16[8,512,128]{2,1,0:T(8,128)(2,1)} %get-tuple-element.8), calls=%async_computation | async-start | bytes 2097152 | tf_op jit(solution)/shard_map/all_to_all | solution.py:35
  10.7 2.2 %pack.1 = bf16[560,128]{1,0:T(8,128)(2,1)} custom-call(bf16[6,256,128]{2,1,0:T(8,128)(2,1)} %walkers.3, bf16[6,128,128]{2,1,0:T(8,128)(2,1)} %refs_3_.1, bf16[2,6]{1,0:T(2,128)(2,1)} %bitcast.2), custom_call_target="tpu_custom_call" | custom-call | tf_op jit(solution)/shard_map/pack/pallas_call | solution.py:80
  12.9 19.4 %collective-permute-start.6 = (bf16[560,128]{1,0:T(8,128)(2,1)}, bf16[560,128]{1,0:T(8,128)(2,1)S(1)}, u32[]{:S(2)}, u32[]{:S(2)}) collective-permute-start(bf16[560,128]{1,0:T(8,128)(2,1)} %pack.1), channel_id=1, source_target_pairs={{0,512},{8,520},{16,528},{24,536},{32,544},{40,552},{48,560},{56,5... | collective-permute-start | bytes 430088 | tf_op jit(solution)/shard_map/ppermute | solution.py:316
  32.3 6.1 %collective-permute-start.5 = (bf16[560,128]{1,0:T(8,128)(2,1)}, bf16[560,128]{1,0:T(8,128)(2,1)S(1)}, u32[]{:S(2)}, u32[]{:S(2)}) collective-permute-start(bf16[560,128]{1,0:T(8,128)(2,1)} %pack.1), channel_id=1, source_target_pairs={{0,256},{8,264},{16,272},{24,280},{32,288},{40,296},{48,304},{56,3... | collective-permute-start | bytes 430088 | tf_op jit(solution)/shard_map/ppermute | solution.py:316
  38.4 4.3 %collective-permute-start.4 = (bf16[560,128]{1,0:T(8,128)(2,1)}, bf16[560,128]{1,0:T(8,128)(2,1)S(1)}, u32[]{:S(2)}, u32[]{:S(2)}) collective-permute-start(bf16[560,128]{1,0:T(8,128)(2,1)} %pack.1), channel_id=1, source_target_pairs={{0,128},{8,136},{16,144},{24,152},{32,160},{40,168},{48,176},{56,1... | collective-permute-start | bytes 430088 | tf_op jit(solution)/shard_map/ppermute | solution.py:316
  42.7 3.4 %collective-permute-start.3 = (bf16[560,128]{1,0:T(8,128)(2,1)}, bf16[560,128]{1,0:T(8,128)(2,1)S(1)}, u32[]{:S(2)}, u32[]{:S(2)}) collective-permute-start(bf16[560,128]{1,0:T(8,128)(2,1)} %pack.1), channel_id=1, source_target_pairs={{0,64},{8,72},{16,80},{24,88},{32,96},{40,104},{48,112},{56,120},{... | collective-permute-start | bytes 430088 | tf_op jit(solution)/shard_map/ppermute | solution.py:316
  46.1 3.3 %collective-permute-start.2 = (bf16[560,128]{1,0:T(8,128)(2,1)}, bf16[560,128]{1,0:T(8,128)(2,1)S(1)}, u32[]{:S(2)}, u32[]{:S(2)}) collective-permute-start(bf16[560,128]{1,0:T(8,128)(2,1)} %pack.1), channel_id=1, source_target_pairs={{0,32},{8,40},{16,48},{24,56},{32,0},{40,8},{48,16},{56,24},{64,96... | collective-permute-start | bytes 430088 | tf_op jit(solution)/shard_map/ppermute | solution.py:316
  49.4 0.0 collective-permute-done.6.refs_7_
  49.4 1.9 %collective-permute-start.1 = (bf16[560,128]{1,0:T(8,128)(2,1)}, bf16[560,128]{1,0:T(8,128)(2,1)S(1)}, u32[]{:S(2)}, u32[]{:S(2)}) collective-permute-start(bf16[560,128]{1,0:T(8,128)(2,1)} %pack.1), channel_id=1, source_target_pairs={{0,16},{8,24},{16,0},{24,8},{32,48},{40,56},{48,32},{56,40},{64,80... | collective-permute-start | bytes 430088 | tf_op jit(solution)/shard_map/ppermute | solution.py:316
  51.4 6.9 %collective-permute-done.5.refs_6_ = bf16[560,128]{1,0:T(8,128)(2,1)S(1)} collective-permute-done((bf16[560,128]{1,0:T(8,128)(2,1)}, bf16[560,128]{1,0:T(8,128)(2,1)S(1)}, u32[]{:S(2)}, u32[]{:S(2)}) %collective-permute-start.5) | collective-permute-done | bytes 143392 | tf_op jit(solution)/shard_map/ppermute | solution.py:316
  58.2 1.9 %collective-permute-start = (bf16[560,128]{1,0:T(8,128)(2,1)}, bf16[560,128]{1,0:T(8,128)(2,1)S(1)}, u32[]{:S(2)}, u32[]{:S(2)}) collective-permute-start(bf16[560,128]{1,0:T(8,128)(2,1)} %pack.1), channel_id=1, source_target_pairs={{0,8},{8,0},{16,24},{24,16},{32,40},{40,32},{48,56},{56,48},{64,72... | collective-permute-start | bytes 430088 | tf_op jit(solution)/shard_map/ppermute | solution.py:316
  60.2 0.0 collective-permute-done.4.refs_5_
  60.2 0.0 collective-permute-done.3.refs_4_
  60.2 0.0 collective-permute-done.2.refs_3_
  60.2 0.0 collective-permute-done.1.refs_2_
  60.2 1.5 %collective-permute-done.refs_1_ = bf16[560,128]{1,0:T(8,128)(2,1)S(1)} collective-permute-done((bf16[560,128]{1,0:T(8,128)(2,1)}, bf16[560,128]{1,0:T(8,128)(2,1)S(1)}, u32[]{:S(2)}, u32[]{:S(2)}) %collective-permute-start) | collective-permute-done | bytes 143392 | tf_op jit(solution)/shard_map/ppermute | solution.py:316
  61.7 0.0 copy-start.4
  61.7 0.9 copy-done.4
  62.6 0.2 merge.1
  62.8 5.7 %collective-permute-start.10 = (bf16[544,128]{1,0:T(8,128)(2,1)S(1)}, bf16[544,128]{1,0:T(8,128)(2,1)S(1)}, u32[]{:S(2)}, u32[]{:S(2)}) collective-permute-start(bf16[544,128]{1,0:T(8,128)(2,1)S(1)} %get-tuple-element.9.refs_4_.late), channel_id=1, source_target_pairs={{0,6},{1,7},{2,0},{3,1},{4,2},{5,3},{6,4},{7,5},{8,14},{9,15},{10,... | collective-permute-start | bytes 417800 | tf_op jit(solution)/shard_map/ppermute | solution.py:41
  68.6 1.9 %collective-permute-start.9 = (bf16[544,128]{1,0:T(8,128)(2,1)S(1)}, bf16[544,128]{1,0:T(8,128)(2,1)S(1)}, u32[]{:S(2)}, u32[]{:S(2)}) collective-permute-start(bf16[544,128]{1,0:T(8,128)(2,1)S(1)} %get-tuple-element.9.refs_4_.late), channel_id=1, source_target_pairs={{0,2},{1,3},{2,4},{3,5},{4,6},{5,7},{6,0},{7,1},{8,10},{9,11},{10,... | collective-permute-start | bytes 417800 | tf_op jit(solution)/shard_map/ppermute | solution.py:41
  70.5 5.1 %collective-permute-start.8 = (bf16[544,128]{1,0:T(8,128)(2,1)S(1)}, bf16[544,128]{1,0:T(8,128)(2,1)S(1)}, u32[]{:S(2)}, u32[]{:S(2)}) collective-permute-start(bf16[544,128]{1,0:T(8,128)(2,1)S(1)} %get-tuple-element.9.refs_4_.late), channel_id=1, source_target_pairs={{0,7},{1,0},{2,1},{3,2},{4,3},{5,4},{6,5},{7,6},{8,15},{9,8},{10,9... | collective-permute-start | bytes 417800 | tf_op jit(solution)/shard_map/ppermute | solution.py:41
  75.6 1.9 %collective-permute-start.7 = (bf16[544,128]{1,0:T(8,128)(2,1)S(1)}, bf16[544,128]{1,0:T(8,128)(2,1)S(1)}, u32[]{:S(2)}, u32[]{:S(2)}) collective-permute-start(bf16[544,128]{1,0:T(8,128)(2,1)S(1)} %get-tuple-element.9.refs_4_.late), channel_id=1, source_target_pairs={{0,1},{1,2},{2,3},{3,4},{4,5},{5,6},{6,7},{7,0},{8,9},{9,10},{10,1... | collective-permute-start | bytes 417800 | tf_op jit(solution)/shard_map/ppermute | solution.py:41
  77.6 0.0 collective-permute-done.10.refs_8_
  77.6 5.1 %collective-permute-start.12 = (bf16[544,128]{1,0:T(8,128)(2,1)S(1)}, bf16[544,128]{1,0:T(8,128)(2,1)S(1)}, u32[]{:S(2)}, u32[]{:S(2)}) collective-permute-start(bf16[544,128]{1,0:T(8,128)(2,1)S(1)} %collective-permute-done.10.refs_8_), channel_id=1, source_target_pairs={{0,7},{1,0},{2,1},{3,2},{4,3},{5,4},{6,5},{7,6},{8,15},{9,8},{10,9... | collective-permute-start | bytes 417800 | tf_op jit(solution)/shard_map/ppermute | solution.py:41
  82.7 0.0 collective-permute-done.9.refs_7_
  82.7 1.9 %collective-permute-start.13 = (bf16[544,128]{1,0:T(8,128)(2,1)S(1)}, bf16[544,128]{1,0:T(8,128)(2,1)S(1)}, u32[]{:S(2)}, u32[]{:S(2)}) collective-permute-start(bf16[544,128]{1,0:T(8,128)(2,1)S(1)} %collective-permute-done.9.refs_7_), channel_id=1, source_target_pairs={{0,2},{1,3},{2,4},{3,5},{4,6},{5,7},{6,0},{7,1},{8,10},{9,11},{10,... | collective-permute-start | bytes 417800 | tf_op jit(solution)/shard_map/ppermute | solution.py:41
  84.6 3.1 %collective-permute-start.11 = (bf16[544,128]{1,0:T(8,128)(2,1)S(1)}, bf16[544,128]{1,0:T(8,128)(2,1)S(1)}, u32[]{:S(2)}, u32[]{:S(2)}) collective-permute-start(bf16[544,128]{1,0:T(8,128)(2,1)S(1)} %collective-permute-done.9.refs_7_), channel_id=1, source_target_pairs={{0,1},{1,2},{2,3},{3,4},{4,5},{5,6},{6,7},{7,0},{8,9},{9,10},{10,1... | collective-permute-start | bytes 417800 | tf_op jit(solution)/shard_map/ppermute | solution.py:41
  87.7 0.0 all-to-all-done.refs_4_
  87.7 0.0 copy-done.2
  87.7 0.0 copy-done.3
  87.7 0.0 copy-start
  87.8 2.2 %copy-done = bf16[2,512,2048]{2,1,0:T(8,128)(2,1)S(1)} copy-done((bf16[2,512,2048]{2,1,0:T(8,128)(2,1)S(1)}, bf16[2,512,2048]{2,1,0:T(8,128)(2,1)}, u32[]{:S(2)}) %copy-start) | copy-done | bytes 4194328
  89.9 1.9 %early_products.1.refs_3_ = bf16[8,144,128]{2,1,0:T(8,128)(2,1)S(1)} custom-call(f32[16,128]{1,0:T(8,128)S(1)} %get-tuple-element.7.refs_0_.x, bf16[2,512,2048]{2,1,0:T(8,128)(2,1)S(1)} %copy-done, bf16[512,128]{1,0:T(8,128)(2,1)S(1)} %copy-done.3, bf16[6,128,128]{2,1,0:T(8,128)(2,1)S(1)} %copy-done.2, bf16[8,512,128]{2,1,0:T(8,128)(2,1)S(1)} %all-to-all-done.refs_4_), custom_call_target="tpu_custom_call" | custom-call | flops 1073741824 | bytes 6291456 | tf_op jit(solution)/shard_map/early_products/pallas_call | solution.py:252
  91.8 0.0 collective-permute-done.8.refs_6_
  91.8 0.0 collective-permute-done.7.refs_5_
  91.8 0.0 collective-permute-done.12.refs_10_
  91.8 2.3 %collective-permute-done.13.refs_11_ = bf16[544,128]{1,0:T(8,128)(2,1)S(1)} collective-permute-done((bf16[544,128]{1,0:T(8,128)(2,1)S(1)}, bf16[544,128]{1,0:T(8,128)(2,1)S(1)}, u32[]{:S(2)}, u32[]{:S(2)}) %collective-permute-start.13) | collective-permute-done | bytes 139296 | tf_op jit(solution)/shard_map/ppermute | solution.py:41
  94.1 1.1 collective-permute-done.11.refs_9_
  95.2 0.0 copy-done.1
  95.2 2.8 %late_products.1 = bf16[8,272,128]{2,1,0:T(8,128)(2,1)} custom-call(f32[16,128]{1,0:T(8,128)S(1)} %get-tuple-element.7.refs_0_.x, bf16[2,512,2048]{2,1,0:T(8,128)(2,1)S(1)} %copy-done.1, bf16[512,128]{1,0:T(8,128)(2,1)S(1)} %copy-done.3, bf16[8,144,128]{2,1,0:T(8,128)(2,1)S(1)} %early_products.1.refs_3_, bf16[544,128]{1,0:T(8,128)(2,1)S(1)} %get-tuple-element.9.refs_4_.late, ...), custom_call_target="tpu_custom_call" | custom-call | flops 1073741824 | bytes 6291456 | tf_op jit(solution)/shard_map/late_products/pallas_call | solution.py:252
  98.0 5.0 %all-to-all-start.1 = ((bf16[8,272,128]{2,1,0:T(8,128)(2,1)}), bf16[8,272,128]{2,1,0:T(8,128)(2,1)S(1)}, u32[]{:S(2)}, u32[]{:S(2)}) async-start(bf16[8,272,128]{2,1,0:T(8,128)(2,1)} %late_products.1), calls=%async_computation.1 | async-start | bytes 1114112 | tf_op jit(solution)/shard_map/all_to_all | solution.py:323
  103.0 0.9 slice.3.early
  103.9 16.9 %all-to-all-done.1.got = bf16[8,272,128]{2,1,0:T(8,128)(2,1)S(1)} async-done(((bf16[8,272,128]{2,1,0:T(8,128)(2,1)}), bf16[8,272,128]{2,1,0:T(8,128)(2,1)S(1)}, u32[]{:S(2)}, u32[]{:S(2)}) %all-to-all-start.1) | async-done | bytes 557088 | tf_op jit(solution)/shard_map/all_to_all | solution.py:323
  120.8 0.7 finish.1
  (1 shorter events, 0.0 us)
Async XLA Ops:
  0.6 87.1 %copy-start.2 = (bf16[6,128,128]{2,1,0:T(8,128)(2,1)S(1)}, bf16[6,128,128]{2,1,0:T(8,128)(2,1)}, u32[]{:S(2)}) copy-start(bf16[6,128,128]{2,1,0:T(8,128)(2,1)} %refs_3_.1) | copy-start | bytes 589828
  0.6 87.1 %copy-start.3 = (bf16[512,128]{1,0:T(8,128)(2,1)S(1)}, bf16[512,128]{1,0:T(8,128)(2,1)}, u32[]{:S(2)}) copy-start(bf16[512,128]{1,0:T(8,128)(2,1)} %refs_2_.3) | copy-start | bytes 393220
  3.6 84.1 %all-to-all-start = ((bf16[8,512,128]{2,1,0:T(8,128)(2,1)}), bf16[8,512,128]{2,1,0:T(8,128)(2,1)S(1)}, u32[]{:S(2)}, u32[]{:S(2)}) async-start(bf16[8,512,128]{2,1,0:T(8,128)(2,1)} %get-tuple-element.8), calls=%async_computation | async-start | bytes 2097152 | tf_op jit(solution)/shard_map/all_to_all | solution.py:35
  12.9 36.5 %collective-permute-start.6 = (bf16[560,128]{1,0:T(8,128)(2,1)}, bf16[560,128]{1,0:T(8,128)(2,1)S(1)}, u32[]{:S(2)}, u32[]{:S(2)}) collective-permute-start(bf16[560,128]{1,0:T(8,128)(2,1)} %pack.1), channel_id=1, source_target_pairs={{0,512},{8,520},{16,528},{24,536},{32,544},{40,552},{48,560},{56,5... | collective-permute-start | bytes 430088 | tf_op jit(solution)/shard_map/ppermute | solution.py:316
  32.3 25.9 %collective-permute-start.5 = (bf16[560,128]{1,0:T(8,128)(2,1)}, bf16[560,128]{1,0:T(8,128)(2,1)S(1)}, u32[]{:S(2)}, u32[]{:S(2)}) collective-permute-start(bf16[560,128]{1,0:T(8,128)(2,1)} %pack.1), channel_id=1, source_target_pairs={{0,256},{8,264},{16,272},{24,280},{32,288},{40,296},{48,304},{56,3... | collective-permute-start | bytes 430088 | tf_op jit(solution)/shard_map/ppermute | solution.py:316
  38.4 21.7 %collective-permute-start.4 = (bf16[560,128]{1,0:T(8,128)(2,1)}, bf16[560,128]{1,0:T(8,128)(2,1)S(1)}, u32[]{:S(2)}, u32[]{:S(2)}) collective-permute-start(bf16[560,128]{1,0:T(8,128)(2,1)} %pack.1), channel_id=1, source_target_pairs={{0,128},{8,136},{16,144},{24,152},{32,160},{40,168},{48,176},{56,1... | collective-permute-start | bytes 430088 | tf_op jit(solution)/shard_map/ppermute | solution.py:316
  42.7 17.4 %collective-permute-start.3 = (bf16[560,128]{1,0:T(8,128)(2,1)}, bf16[560,128]{1,0:T(8,128)(2,1)S(1)}, u32[]{:S(2)}, u32[]{:S(2)}) collective-permute-start(bf16[560,128]{1,0:T(8,128)(2,1)} %pack.1), channel_id=1, source_target_pairs={{0,64},{8,72},{16,80},{24,88},{32,96},{40,104},{48,112},{56,120},{... | collective-permute-start | bytes 430088 | tf_op jit(solution)/shard_map/ppermute | solution.py:316
  46.1 14.1 %collective-permute-start.2 = (bf16[560,128]{1,0:T(8,128)(2,1)}, bf16[560,128]{1,0:T(8,128)(2,1)S(1)}, u32[]{:S(2)}, u32[]{:S(2)}) collective-permute-start(bf16[560,128]{1,0:T(8,128)(2,1)} %pack.1), channel_id=1, source_target_pairs={{0,32},{8,40},{16,48},{24,56},{32,0},{40,8},{48,16},{56,24},{64,96... | collective-permute-start | bytes 430088 | tf_op jit(solution)/shard_map/ppermute | solution.py:316
  49.4 10.7 %collective-permute-start.1 = (bf16[560,128]{1,0:T(8,128)(2,1)}, bf16[560,128]{1,0:T(8,128)(2,1)S(1)}, u32[]{:S(2)}, u32[]{:S(2)}) collective-permute-start(bf16[560,128]{1,0:T(8,128)(2,1)} %pack.1), channel_id=1, source_target_pairs={{0,16},{8,24},{16,0},{24,8},{32,48},{40,56},{48,32},{56,40},{64,80... | collective-permute-start | bytes 430088 | tf_op jit(solution)/shard_map/ppermute | solution.py:316
  58.2 3.5 %collective-permute-start = (bf16[560,128]{1,0:T(8,128)(2,1)}, bf16[560,128]{1,0:T(8,128)(2,1)S(1)}, u32[]{:S(2)}, u32[]{:S(2)}) collective-permute-start(bf16[560,128]{1,0:T(8,128)(2,1)} %pack.1), channel_id=1, source_target_pairs={{0,8},{8,0},{16,24},{24,16},{32,40},{40,32},{48,56},{56,48},{64,72... | collective-permute-start | bytes 430088 | tf_op jit(solution)/shard_map/ppermute | solution.py:316
  61.7 0.9 copy-start.4
  62.8 14.7 %collective-permute-start.10 = (bf16[544,128]{1,0:T(8,128)(2,1)S(1)}, bf16[544,128]{1,0:T(8,128)(2,1)S(1)}, u32[]{:S(2)}, u32[]{:S(2)}) collective-permute-start(bf16[544,128]{1,0:T(8,128)(2,1)S(1)} %get-tuple-element.9.refs_4_.late), channel_id=1, source_target_pairs={{0,6},{1,7},{2,0},{3,1},{4,2},{5,3},{6,4},{7,5},{8,14},{9,15},{10,... | collective-permute-start | bytes 417800 | tf_op jit(solution)/shard_map/ppermute | solution.py:41
  68.6 14.2 %collective-permute-start.9 = (bf16[544,128]{1,0:T(8,128)(2,1)S(1)}, bf16[544,128]{1,0:T(8,128)(2,1)S(1)}, u32[]{:S(2)}, u32[]{:S(2)}) collective-permute-start(bf16[544,128]{1,0:T(8,128)(2,1)S(1)} %get-tuple-element.9.refs_4_.late), channel_id=1, source_target_pairs={{0,2},{1,3},{2,4},{3,5},{4,6},{5,7},{6,0},{7,1},{8,10},{9,11},{10,... | collective-permute-start | bytes 417800 | tf_op jit(solution)/shard_map/ppermute | solution.py:41
  70.5 21.3 %collective-permute-start.8 = (bf16[544,128]{1,0:T(8,128)(2,1)S(1)}, bf16[544,128]{1,0:T(8,128)(2,1)S(1)}, u32[]{:S(2)}, u32[]{:S(2)}) collective-permute-start(bf16[544,128]{1,0:T(8,128)(2,1)S(1)} %get-tuple-element.9.refs_4_.late), channel_id=1, source_target_pairs={{0,7},{1,0},{2,1},{3,2},{4,3},{5,4},{6,5},{7,6},{8,15},{9,8},{10,9... | collective-permute-start | bytes 417800 | tf_op jit(solution)/shard_map/ppermute | solution.py:41
  75.6 16.2 %collective-permute-start.7 = (bf16[544,128]{1,0:T(8,128)(2,1)S(1)}, bf16[544,128]{1,0:T(8,128)(2,1)S(1)}, u32[]{:S(2)}, u32[]{:S(2)}) collective-permute-start(bf16[544,128]{1,0:T(8,128)(2,1)S(1)} %get-tuple-element.9.refs_4_.late), channel_id=1, source_target_pairs={{0,1},{1,2},{2,3},{3,4},{4,5},{5,6},{6,7},{7,0},{8,9},{9,10},{10,1... | collective-permute-start | bytes 417800 | tf_op jit(solution)/shard_map/ppermute | solution.py:41
  77.6 14.3 %collective-permute-start.12 = (bf16[544,128]{1,0:T(8,128)(2,1)S(1)}, bf16[544,128]{1,0:T(8,128)(2,1)S(1)}, u32[]{:S(2)}, u32[]{:S(2)}) collective-permute-start(bf16[544,128]{1,0:T(8,128)(2,1)S(1)} %collective-permute-done.10.refs_8_), channel_id=1, source_target_pairs={{0,7},{1,0},{2,1},{3,2},{4,3},{5,4},{6,5},{7,6},{8,15},{9,8},{10,9... | collective-permute-start | bytes 417800 | tf_op jit(solution)/shard_map/ppermute | solution.py:41
  82.7 11.4 %collective-permute-start.13 = (bf16[544,128]{1,0:T(8,128)(2,1)S(1)}, bf16[544,128]{1,0:T(8,128)(2,1)S(1)}, u32[]{:S(2)}, u32[]{:S(2)}) collective-permute-start(bf16[544,128]{1,0:T(8,128)(2,1)S(1)} %collective-permute-done.9.refs_7_), channel_id=1, source_target_pairs={{0,2},{1,3},{2,4},{3,5},{4,6},{5,7},{6,0},{7,1},{8,10},{9,11},{10,... | collective-permute-start | bytes 417800 | tf_op jit(solution)/shard_map/ppermute | solution.py:41
  84.6 10.6 %collective-permute-start.11 = (bf16[544,128]{1,0:T(8,128)(2,1)S(1)}, bf16[544,128]{1,0:T(8,128)(2,1)S(1)}, u32[]{:S(2)}, u32[]{:S(2)}) collective-permute-start(bf16[544,128]{1,0:T(8,128)(2,1)S(1)} %collective-permute-done.9.refs_7_), channel_id=1, source_target_pairs={{0,1},{1,2},{2,3},{3,4},{4,5},{5,6},{6,7},{7,0},{8,9},{9,10},{10,1... | collective-permute-start | bytes 417800 | tf_op jit(solution)/shard_map/ppermute | solution.py:41
  87.7 2.2 %copy-start = (bf16[2,512,2048]{2,1,0:T(8,128)(2,1)S(1)}, bf16[2,512,2048]{2,1,0:T(8,128)(2,1)}, u32[]{:S(2)}) copy-start(bf16[2,512,2048]{2,1,0:T(8,128)(2,1)} %refs_1_.3) | copy-start | bytes 12582916
  89.9 5.3 %copy-start.1 = (bf16[2,512,2048]{2,1,0:T(8,128)(2,1)S(1)}, bf16[2,512,2048]{2,1,0:T(8,128)(2,1)}, u32[]{:S(2)}) copy-start(bf16[2,512,2048]{2,1,0:T(8,128)(2,1)} %refs_1_.3) | copy-start | bytes 12582916
  98.0 22.8 %all-to-all-start.1 = ((bf16[8,272,128]{2,1,0:T(8,128)(2,1)}), bf16[8,272,128]{2,1,0:T(8,128)(2,1)S(1)}, u32[]{:S(2)}, u32[]{:S(2)}) async-start(bf16[8,272,128]{2,1,0:T(8,128)(2,1)} %late_products.1), calls=%async_computation.1 | async-start | bytes 1114112 | tf_op jit(solution)/shard_map/all_to_all | solution.py:323
